TPU v7x, 32 devices: a whole 2x2x4 slice. The times are simulated.
32 devices in a mesh: head: 4 (over z), seq: 8 (over y, x, core).
Axes of the slice: x: 2, y: 2, z: 4, core: 2. Of those that a mesh axis runs over, the one named last changes fastest.
Arguments:
- hidden_in: bfloat16 [8192, 1536], P(('seq', 'head')), may hold values from -6 to 6
- out_grad: bfloat16 [8192, 1536], P(('seq', 'head')), may hold values from -6 to 6
- doc_lengths: int32 [32], replicated, may hold values from 1 to 1024, 8192 in all
- expert_ids: int32 [8192, 8], P(('seq', 'head')), may hold values from 0 to 15, all different within a row
- attention_norm: bfloat16 [1536], P(('head', 'seq')), may hold values from 0.5 to 1.5
- query_weight: bfloat16 [1536, 1536], P(('head', 'seq')), may hold values from -0.625 to 0.625
- key_matrix: bfloat16 [1536, 512], P(('head', 'seq')), may hold values from -0.625 to 0.625
- value_matrix: bfloat16 [1536, 512], P(('head', 'seq')), may hold values from -0.15625 to 0.15625
- output_weight: bfloat16 [1536, 1536], P(('head', 'seq')), may hold values from -2.5 to 2.5
- expert_norm: bfloat16 [1536], P(('head', 'seq')), may hold values from 0.5 to 1.5
- router_weight: bfloat16 [1536, 16], P(('head', 'seq')), may hold values from -0.078125 to 0.078125
- expert_input: bfloat16 [1536, 16, 1024], P(('head', 'seq')), may hold values from -0.15625 to 0.15625
- expert_output: bfloat16 [1536, 16, 512], P(('head', 'seq')), may hold values from -6 to 6
Outputs:
- block_out: bfloat16 [8192, 1536], P(('seq', 'head'))
- input_grad: float32 [8192, 1536], P(('seq', 'head'))
- attention_norm_grad: float32 [1536], P(('head', 'seq'))
- query_grad: float32 [1536, 1536], P(('head', 'seq'))
- key_grad: float32 [1536, 512], P(('head', 'seq'))
- value_grad: float32 [1536, 512], P(('head', 'seq'))
- output_grad: float32 [1536, 1536], P(('head', 'seq'))
- expert_norm_grad: float32 [1536], P(('head', 'seq'))
- router_grad: float32 [1536, 16], P(('head', 'seq'))
- expert_input_grad: float32 [1536, 16, 1024], P(('head', 'seq'))
- expert_output_grad: float32 [1536, 16, 512], P(('head', 'seq'))
Inputs may be any that keep to these rules, and one draw needn't show every extreme that they name: `doc_lengths`: the lengths sum to 8192; one document has exactly 1024 tokens. `expert_ids`: the 8 experts of a token are different.
All inputs are finite; a program needn't handle non-finite values.
Results may differ from a plain program's by a relative error of at most 0.017.
The roundings to bfloat16 on the way count: a program that leaves them out, or rounds other values in their place, can miss the bound.
Values may be sent and summed in bfloat16 or wider, within the bound.
No kernel may reach another device: no remote copies, remote signals or barrier semaphores. Data moves between devices by JAX's collectives and lax.ppermute only.
A program may use at most 576 MiB of HBM per device.

v0:
```python
import jax
import jax.numpy as jnp
from jax import lax
from jax.sharding import PartitionSpec as P

MODEL_WIDTH = 1536
QUERY_HEADS = 24
KEY_VALUE_HEADS = 8
HEAD_WIDTH = 64
FF = 512
TOPK = 8
EXPERTS = 16
QUERY_BLOCK_ROWS = 512
CAP = 160


EPS = 1e-06
ATTN_SCALE = 1.0 / 64.0
RESIDUAL_SCALE = 0.22
MASKED = -1e30


def from_behind(block, axis, distance):
    devices = range(lax.axis_size(axis))
    route = [(i - distance, i) for i in devices if i - distance in devices]
    return lax.ppermute(block, axis, route)


def rms_forward(values, gain):
    inverse = lax.rsqrt(jnp.mean(values * values, axis=-1, keepdims=True) + EPS)
    return (values * inverse * gain, inverse)


def rms_backward(values, inverse, gain, incoming):
    scaled = incoming * gain
    mean_term = jnp.mean(scaled * values, axis=-1, keepdims=True)
    values_grad = inverse * scaled - values * inverse * inverse * inverse * mean_term
    gain_grad = jnp.sum(incoming * values * inverse, axis=0)
    return (values_grad, gain_grad)


def doc_start(doc_lengths, places):
    starts = jnp.cumsum(doc_lengths) - doc_lengths
    earlier = starts[None, :] <= places[:, None]
    return jnp.max(jnp.where(earlier, starts[None, :], 0), axis=1)


def rope_tables(places):
    frequency = jnp.exp(
        -jnp.log(10000.0) * 2.0 * jnp.arange(HEAD_WIDTH // 2).astype(jnp.float32) / HEAD_WIDTH
    )
    angles = places.astype(jnp.float32)[:, None] * frequency[None, :]
    return (jnp.cos(angles), jnp.sin(angles))


def apply_rotation(values, cosine_lookup, sine_lookup, head_count):
    shaped = values.reshape(values.shape[0], head_count, 2, HEAD_WIDTH // 2)
    first_half = shaped[:, :, 0, :]
    second_half = shaped[:, :, 1, :]
    cos_part = cosine_lookup[:, None, :]
    sin_part = sine_lookup[:, None, :]
    turned = jnp.stack(
        [
            first_half * cos_part - second_half * sin_part,
            second_half * cos_part + first_half * sin_part,
        ],
        axis=2,
    )
    return turned.reshape(values.shape)


def rotate_back(values, cosine_lookup, sine_lookup, head_count):
    shaped = values.reshape(values.shape[0], head_count, 2, HEAD_WIDTH // 2)
    first_half = shaped[:, :, 0, :]
    second_half = shaped[:, :, 1, :]
    cos_part = cosine_lookup[:, None, :]
    sin_part = sine_lookup[:, None, :]
    turned = jnp.stack(
        [
            first_half * cos_part + second_half * sin_part,
            second_half * cos_part - first_half * sin_part,
        ],
        axis=2,
    )
    return turned.reshape(values.shape)


def assign_slots(identities):
    flat_ids = identities.reshape(-1)
    claims = flat_ids.shape[0]
    chosen_hot = (flat_ids[:, None] == jnp.arange(EXPERTS)[None, :]).astype(jnp.int32)
    earlier = jnp.cumsum(chosen_hot, axis=0) - chosen_hot
    slot_of = jnp.sum(earlier * chosen_hot, axis=1)
    destination = jnp.where(slot_of < CAP, flat_ids * CAP + slot_of, EXPERTS * CAP)
    ordinal = jnp.arange(claims)
    token_of = (
        jnp.full((EXPERTS * CAP + 1,), claims // TOPK, jnp.int32)
        .at[destination]
        .set(ordinal // TOPK)
    )
    claim_of = jnp.full((EXPERTS * CAP + 1,), claims, jnp.int32).at[destination].set(ordinal)
    return (destination, token_of[:-1], claim_of[:-1])


def contract_last(left, right):
    return lax.dot_general(
        left, right, (((1,), (1,)), ((), ())), preferred_element_type=jnp.float32
    )


def contract_first(left, right):
    return lax.dot_general(
        left, right, (((0,), (0,)), ((), ())), preferred_element_type=jnp.float32
    )


def shards(
    hidden_in,
    out_grad,
    doc_lengths,
    expert_ids,
    attention_norm,
    query_weight,
    key_matrix,
    value_matrix,
    output_weight,
    expert_norm,
    router_weight,
    expert_input,
    expert_output,
):
    tokens_dev = hidden_in.shape[0]
    heads_per_device = lax.axis_size("head")
    span = tokens_dev * heads_per_device
    head_index = lax.axis_index("head")
    seq_index = lax.axis_index("seq")
    query_heads = QUERY_HEADS // heads_per_device
    paired_heads = KEY_VALUE_HEADS // heads_per_device
    group_width = QUERY_HEADS // KEY_VALUE_HEADS
    query_cols = query_heads * HEAD_WIDTH
    pair_cols = paired_heads * HEAD_WIDTH
    width_extent = span + QUERY_BLOCK_ROWS
    block_count = span // QUERY_BLOCK_ROWS
    base_row = seq_index * span
    group_places = base_row + jnp.arange(span)
    group_starts = doc_start(doc_lengths, group_places)
    cosine_group, sine_group = rope_tables(group_places - group_starts)
    own_first = head_index * tokens_dev
    cosine_slice = lax.dynamic_slice_in_dim(cosine_group, own_first, tokens_dev, 0)
    sine_slice = lax.dynamic_slice_in_dim(sine_group, own_first, tokens_dev, 0)
    w_query, w_key, w_value, w_output, w_router, gain_one, gain_two = (
        lax.all_gather(query_weight, ("head", "seq"), axis=0, tiled=True),
        lax.all_gather(key_matrix, ("head", "seq"), axis=0, tiled=True),
        lax.all_gather(value_matrix, ("head", "seq"), axis=0, tiled=True),
        lax.all_gather(output_weight, ("head", "seq"), axis=0, tiled=True),
        lax.all_gather(router_weight, ("head", "seq"), axis=0, tiled=True),
        lax.all_gather(attention_norm, ("head", "seq"), axis=0, tiled=True),
        lax.all_gather(expert_norm, ("head", "seq"), axis=0, tiled=True),
    )
    gain_first = gain_one.astype(jnp.float32)
    gain_second = gain_two.astype(jnp.float32)
    stream = hidden_in.astype(jnp.float32)
    normed_float, inverse_one = rms_forward(stream, gain_first)
    normed = normed_float.astype(jnp.bfloat16)
    query_lin = jnp.dot(normed, w_query, preferred_element_type=jnp.float32)
    key_linear = jnp.dot(normed, w_key, preferred_element_type=jnp.float32)
    value_local = jnp.dot(normed, w_value, preferred_element_type=jnp.float32).astype(jnp.bfloat16)
    query_local = apply_rotation(query_lin, cosine_slice, sine_slice, QUERY_HEADS).astype(
        jnp.bfloat16
    )
    key_slice = apply_rotation(key_linear, cosine_slice, sine_slice, KEY_VALUE_HEADS).astype(
        jnp.bfloat16
    )
    query_group, key_group, value_group = (
        lax.all_to_all(query_local, "head", split_axis=1, concat_axis=0, tiled=True),
        lax.all_to_all(key_slice, "head", split_axis=1, concat_axis=0, tiled=True),
        lax.all_to_all(value_local, "head", split_axis=1, concat_axis=0, tiled=True),
    )
    key_before, value_before = from_behind((key_group, value_group), "seq", 1)
    key_all = jnp.concatenate([key_before, key_group], axis=0)
    value_all = jnp.concatenate([value_before, value_group], axis=0)

    def block_probs(leading_row):
        query_tile_block = lax.dynamic_slice_in_dim(
            query_group, leading_row, QUERY_BLOCK_ROWS, 0
        ).reshape(QUERY_BLOCK_ROWS, paired_heads, group_width, HEAD_WIDTH)
        key_tile_block = lax.dynamic_slice_in_dim(key_all, leading_row, width_extent, 0).reshape(
            width_extent, paired_heads, HEAD_WIDTH
        )
        value_tile_block = lax.dynamic_slice_in_dim(
            value_all, leading_row, width_extent, 0
        ).reshape(width_extent, paired_heads, HEAD_WIDTH)
        start_block = lax.dynamic_slice_in_dim(group_starts, leading_row, QUERY_BLOCK_ROWS, 0)
        query_place = base_row + leading_row + jnp.arange(QUERY_BLOCK_ROWS)
        key_place = base_row - span + leading_row + jnp.arange(width_extent)
        visible = (key_place[None, :] >= start_block[:, None]) & (
            key_place[None, :] <= query_place[:, None]
        )
        raw_scores = jnp.einsum(
            "qhgd,khd->hgqk", query_tile_block, key_tile_block, preferred_element_type=jnp.float32
        )
        scaled = jnp.where(visible[None, None], raw_scores * ATTN_SCALE, MASKED)
        return (jax.nn.softmax(scaled, axis=-1), query_tile_block, key_tile_block, value_tile_block)

    def forward_block(block_id):
        soft_weights, query_tile_block, key_tile_block, value_tile_block = block_probs(
            block_id * QUERY_BLOCK_ROWS
        )
        mixture = jnp.einsum(
            "hgqk,khd->qhgd",
            soft_weights.astype(jnp.bfloat16),
            value_tile_block,
            preferred_element_type=jnp.float32,
        )
        return mixture.reshape(QUERY_BLOCK_ROWS, query_cols).astype(jnp.bfloat16)

    block_ids = jnp.arange(block_count)
    mixture_group = lax.map(forward_block, block_ids).reshape(span, query_cols)
    mixture_local = lax.all_to_all(mixture_group, "head", split_axis=0, concat_axis=1, tiled=True)
    branch = contract_last(mixture_local, w_output)
    middle = stream + RESIDUAL_SCALE * branch
    second_float, inverse_two = rms_forward(middle, gain_second)
    normed_two = second_float.astype(jnp.bfloat16)
    logits = jnp.dot(normed_two, w_router, preferred_element_type=jnp.float32)
    chosen_hot = (expert_ids[:, :, None] == jnp.arange(EXPERTS)[None, None, :]).astype(jnp.float32)
    chosen = jnp.sum(chosen_hot * logits[:, None, :], axis=-1)
    gates = jax.nn.softmax(chosen, axis=-1)
    destination, token_of, claim_of = assign_slots(expert_ids)
    normed_pad = jnp.concatenate([normed_two, jnp.zeros((1, MODEL_WIDTH), jnp.bfloat16)], axis=0)
    dispatched = normed_pad[token_of].reshape(EXPERTS, CAP, MODEL_WIDTH)
    columns = dispatched
    gate_up = jnp.einsum(
        "ecd,dej->ecj",
        columns,
        lax.all_gather(expert_input, ("head", "seq"), axis=0, tiled=True),
        preferred_element_type=jnp.float32,
    )
    gate_part = gate_up[..., :FF]
    up_part = gate_up[..., FF:]
    sigmoid_gate = jax.nn.sigmoid(gate_part)
    silu_gate = gate_part * sigmoid_gate
    activation = (silu_gate * up_part).astype(jnp.bfloat16)
    returned = jnp.einsum(
        "ecf,def->ecd",
        activation,
        lax.all_gather(expert_output, ("head", "seq"), axis=0, tiled=True),
        preferred_element_type=jnp.float32,
    ).astype(jnp.bfloat16)
    returned_pad = jnp.concatenate(
        [returned.reshape(EXPERTS * CAP, MODEL_WIDTH), jnp.zeros((1, MODEL_WIDTH), jnp.bfloat16)],
        axis=0,
    )
    picked = returned_pad[destination].astype(jnp.float32).reshape(tokens_dev, TOPK, MODEL_WIDTH)
    moe_out = jnp.sum(picked * gates[:, :, None], axis=1)
    block_out = (middle + RESIDUAL_SCALE * moe_out).astype(jnp.bfloat16)
    grad_stream = out_grad.astype(jnp.float32)
    moe_grad = RESIDUAL_SCALE * grad_stream
    gate_grad = jnp.sum(picked * moe_grad[:, None, :], axis=-1)
    chosen_grad = gates * (gate_grad - jnp.sum(gates * gate_grad, axis=-1, keepdims=True))
    logits_grad = jnp.sum(chosen_hot * chosen_grad[:, :, None], axis=1).astype(jnp.bfloat16)
    gate_pad = jnp.concatenate([gates.reshape(-1), jnp.zeros((1,), jnp.float32)], axis=0)
    moe_grad_pad = jnp.concatenate([moe_grad, jnp.zeros((1, MODEL_WIDTH), jnp.float32)], axis=0)
    returned_grad = (
        (gate_pad[claim_of][:, None] * moe_grad_pad[token_of])
        .astype(jnp.bfloat16)
        .reshape(EXPERTS, CAP, MODEL_WIDTH)
    )
    columns = returned_grad
    activation_grad = jnp.einsum(
        "ecd,def->ecf",
        columns,
        lax.all_gather(expert_output, ("head", "seq"), axis=0, tiled=True),
        preferred_element_type=jnp.float32,
    )
    gate_grad_part = (
        activation_grad * up_part * sigmoid_gate * (1.0 + gate_part * (1.0 - sigmoid_gate))
    )
    up_grad_part = activation_grad * silu_gate
    gate_up_grad = jnp.concatenate([gate_grad_part, up_grad_part], axis=-1).astype(jnp.bfloat16)
    dispatched_grad = jnp.einsum(
        "ecj,dej->ecd",
        gate_up_grad,
        lax.all_gather(expert_input, ("head", "seq"), axis=0, tiled=True),
        preferred_element_type=jnp.float32,
    )
    dispatched_pad = jnp.concatenate(
        [
            dispatched_grad.reshape(EXPERTS * CAP, MODEL_WIDTH),
            jnp.zeros((1, MODEL_WIDTH), jnp.float32),
        ],
        axis=0,
    )
    normed_two_grad = jnp.sum(
        dispatched_pad[destination].reshape(tokens_dev, TOPK, MODEL_WIDTH), axis=1
    ) + contract_last(logits_grad, w_router)
    middle_norm_grad, second_gain_term = rms_backward(
        middle, inverse_two, gain_second, normed_two_grad
    )
    middle_grad = grad_stream + middle_norm_grad
    branch_grad = (RESIDUAL_SCALE * middle_grad).astype(jnp.bfloat16)
    mixture_grad_local = jnp.dot(branch_grad, w_output, preferred_element_type=jnp.float32).astype(
        jnp.bfloat16
    )
    mixture_grad = lax.all_to_all(
        mixture_grad_local, "head", split_axis=1, concat_axis=0, tiled=True
    )

    def backward_block(carry, block_id):
        key_total, value_total = carry
        leading_row = block_id * QUERY_BLOCK_ROWS
        soft_weights, query_tile_block, key_tile_block, value_tile_block = block_probs(leading_row)
        incoming = lax.dynamic_slice_in_dim(mixture_grad, leading_row, QUERY_BLOCK_ROWS, 0).reshape(
            QUERY_BLOCK_ROWS, paired_heads, group_width, HEAD_WIDTH
        )
        prob_grad = jnp.einsum(
            "qhgd,khd->hgqk", incoming, value_tile_block, preferred_element_type=jnp.float32
        )
        delta = jnp.sum(soft_weights * prob_grad, axis=-1, keepdims=True)
        score_grad = (soft_weights * (prob_grad - delta) * ATTN_SCALE).astype(jnp.bfloat16)
        query_part = jnp.einsum(
            "hgqk,khd->qhgd", score_grad, key_tile_block, preferred_element_type=jnp.float32
        ).reshape(QUERY_BLOCK_ROWS, query_cols)
        key_part = jnp.einsum(
            "hgqk,qhgd->khd", score_grad, query_tile_block, preferred_element_type=jnp.float32
        ).reshape(width_extent, pair_cols)
        value_part = jnp.einsum(
            "hgqk,qhgd->khd",
            soft_weights.astype(jnp.bfloat16),
            incoming,
            preferred_element_type=jnp.float32,
        ).reshape(width_extent, pair_cols)
        key_total = lax.dynamic_update_slice_in_dim(
            key_total,
            lax.dynamic_slice_in_dim(key_total, leading_row, width_extent, 0) + key_part,
            leading_row,
            0,
        )
        value_total = lax.dynamic_update_slice_in_dim(
            value_total,
            lax.dynamic_slice_in_dim(value_total, leading_row, width_extent, 0) + value_part,
            leading_row,
            0,
        )
        return ((key_total, value_total), query_part)

    zero_pairs = jnp.zeros((2 * span, pair_cols), jnp.float32)
    (key_total, value_total), query_parts = lax.scan(
        backward_block, (zero_pairs, zero_pairs), block_ids
    )
    query_rot_grad = query_parts.reshape(span, query_cols)
    key_later, value_later = (
        from_behind(key_total[:span].astype(jnp.bfloat16), "seq", -1).astype(jnp.float32),
        from_behind(value_total[:span].astype(jnp.bfloat16), "seq", -1).astype(jnp.float32),
    )
    key_rot_grad = key_total[span:] + key_later
    values_grad = (value_total[span:] + value_later).astype(jnp.bfloat16)
    query_lin_grad = rotate_back(query_rot_grad, cosine_group, sine_group, query_heads).astype(
        jnp.bfloat16
    )
    key_lin_grad = rotate_back(key_rot_grad, cosine_group, sine_group, paired_heads).astype(
        jnp.bfloat16
    )
    query_tok, key_tok, value_tok = (
        lax.all_to_all(query_lin_grad, "head", split_axis=0, concat_axis=1, tiled=True),
        lax.all_to_all(key_lin_grad, "head", split_axis=0, concat_axis=1, tiled=True),
        lax.all_to_all(values_grad, "head", split_axis=0, concat_axis=1, tiled=True),
    )
    normed_grad = (
        contract_last(query_tok, w_query)
        + contract_last(key_tok, w_key)
        + contract_last(value_tok, w_value)
    )
    input_norm_grad, first_gain_term = rms_backward(stream, inverse_one, gain_first, normed_grad)
    input_grad = middle_grad + input_norm_grad
    projection_grad = jnp.concatenate([query_tok, key_tok, value_tok], axis=1)
    own_rows = query_weight.shape[0]
    attention_part = contract_first(normed, projection_grad)
    output_part = contract_first(branch_grad, mixture_local)
    inner_part = jnp.einsum(
        "ecd,ecj->dej", dispatched, gate_up_grad, preferred_element_type=jnp.float32
    ).reshape(own_rows * lax.axis_size(("head", "seq")), EXPERTS * 2 * FF)
    outer_part = jnp.einsum(
        "ecd,ecf->def", returned_grad, activation, preferred_element_type=jnp.float32
    ).reshape(own_rows * lax.axis_size(("head", "seq")), EXPERTS * FF)
    summed = lax.psum_scatter(
        jnp.concatenate([attention_part, output_part, inner_part, outer_part], axis=1),
        ("head", "seq"),
        scatter_dimension=0,
        tiled=True,
    )
    query_stop = QUERY_HEADS * HEAD_WIDTH
    key_stop = query_stop + KEY_VALUE_HEADS * HEAD_WIDTH
    value_stop = key_stop + KEY_VALUE_HEADS * HEAD_WIDTH
    output_end = value_stop + QUERY_HEADS * HEAD_WIDTH
    inner_end = output_end + EXPERTS * 2 * FF
    query_grad = summed[:, :query_stop]
    key_grad = summed[:, query_stop:key_stop]
    value_grad = summed[:, key_stop:value_stop]
    output_grad = summed[:, value_stop:output_end]
    expert_input_grad = summed[:, output_end:inner_end].reshape(own_rows, EXPERTS, 2 * FF)
    expert_output_grad = summed[:, inner_end:].reshape(own_rows, EXPERTS, FF)
    router_term = contract_first(normed_two, logits_grad)
    router_grad, attention_norm_grad, expert_norm_grad = (
        lax.psum_scatter(router_term, ("head", "seq"), scatter_dimension=0, tiled=True),
        lax.psum_scatter(first_gain_term, ("head", "seq"), scatter_dimension=0, tiled=True),
        lax.psum_scatter(second_gain_term, ("head", "seq"), scatter_dimension=0, tiled=True),
    )
    return (
        block_out,
        input_grad,
        attention_norm_grad,
        query_grad,
        key_grad,
        value_grad,
        output_grad,
        expert_norm_grad,
        router_grad,
        expert_input_grad,
        expert_output_grad,
    )


def solution(mesh):
    return jax.shard_map(
        shards,
        mesh=mesh,
        in_specs=(
            P(("seq", "head"), None),
            P(("seq", "head"), None),
            P(),
            P(("seq", "head"), None),
            P(("head", "seq")),
            P(("head", "seq"), None),
            P(("head", "seq"), None),
            P(("head", "seq"), None),
            P(("head", "seq"), None),
            P(("head", "seq")),
            P(("head", "seq"), None),
            P(("head", "seq"), None, None),
            P(("head", "seq"), None, None),
        ),
        out_specs=(
            P(("seq", "head"), None),
            P(("seq", "head"), None),
            P(("head", "seq")),
            P(("head", "seq"), None),
            P(("head", "seq"), None),
            P(("head", "seq"), None),
            P(("head", "seq"), None),
            P(("head", "seq")),
            P(("head", "seq"), None),
            P(("head", "seq"), None, None),
            P(("head", "seq"), None, None),
        ),
        check_vma=False,
    )
```

profile of v0, /device:TPU:0, one launch (start us, length us, event | category | flops | bytes accessed | tf_op | source)
XLA Modules:
  0.0 2940.9 jit_solution(6881780402803995154)
XLA Ops:
  15.8 42.2 %all-reduce.9 = (bf16[1536]{0:T(1024)(128)(2,1)S(1)}, bf16[1536]{0:T(1024)(128)(2,1)S(1)}) all-reduce(bf16[1536]{0:T(1024)(128)(2,1)S(1)} %dynamic-update-slice, bf16[1536]{0:T(1024)(128)(2,1)S(1)} %dynamic-update-slice.1), channel_id=1, replica_groups=mesh['head'=4,'seq'=8] {'head','seq'}, use_global_device_ids=true, to_apply=%add.4 | all-reduce | flops 3072 | bytes 12288
  74.9 50.6 %all-gather.10.cloned.1.call-done = bf16[1536,512]{1,0:T(8,128)(2,1)} async-done(((bf16[48,512]{1,0:T(8,128)(2,1)}), bf16[1536,512]{1,0:T(8,128)(2,1)}) %all-gather.10.cloned.1.call-update) | async-done | bytes 1572880 | tf_op jit(solution)/shard_map/all_gather | solution.py:153
  128.6 62.4 %all-gather.12.cloned.1.call-done = bf16[1536,1536]{1,0:T(8,128)(2,1)} async-done(((bf16[48,1536]{1,0:T(8,128)(2,1)}), bf16[1536,1536]{1,0:T(8,128)(2,1)}) %all-gather.12.cloned.1.call-update) | async-done | bytes 4718608 | tf_op jit(solution)/shard_map/all_gather | solution.py:152
  219.9 44.3 %all-gather = bf16[32,48,16]{1,2,0:T(8,128)(2,1)S(1)} all-gather(bf16[1,48,16]{1,2,0:T(8,128)(2,1)S(1)} %bitcast.324), channel_id=1, replica_groups=mesh['head'=4,'seq'=8] {'head','seq'}, dimensions={0}, use_global_device_ids=true | all-gather | bytes 50688 | tf_op jit(solution)/shard_map/all_gather | solution.py:156
  283.9 46.9 %while.28 = (s32[]{:T(128)}, bf16[2,512,384]{2,1,0:T(8,128)(2,1)}, s32[2]{0:T(128)S(1)}, bf16[2048,128]{0,1:T(8,128)(2,1)S(1)}, s32[]{:T(128)}, /*index=5*/s32[1...) while((s32[]{:T(128)}, bf16[2,512,384]{2,1,0:T(8,128)(2,1)}, ...), condition=%wide.region_6.7_spmd, body=%wide.region_3.6_spmd.sunk | while | flops 1238830592 | bytes 51165512 | solution.py:218
  348.2 29.9 %all-to-all-done.3 = bf16[4,256,384]{2,1,0:T(8,128)(2,1)S(1)} async-done(((bf16[4,256,384]{2,1,0:T(8,128)(2,1)}), bf16[4,256,384]{2,1,0:T(8,128)(2,1)S(1)}, u32[]{:S(2)}, u32[]{:S(2)}) %all-to-all-start.3) | async-done | bytes 786464 | tf_op jit(solution)/shard_map/all_to_all | solution.py:219
  384.7 13.6 gather_fusion.2
  408.0 147.8 %all-gather.16.cloned.1.call-done = bf16[1536,16,1024]{2,0,1:T(8,128)(2,1)} async-done(((bf16[48,16,1024]{2,0,1:T(8,128)(2,1)}), bf16[1536,16,1024]{2,0,1:T(8,128)(2,1)}) %all-gather.16.cloned.1.call-update) | async-done | bytes 50331664 | tf_op jit(solution)/shard_map/all_gather | solution.py:235
  555.8 24.7 fusion.91
  580.5 131.5 %all-gather.18.cloned.1.call-done = bf16[1536,16,512]{2,0,1:T(8,128)(2,1)} async-done(((bf16[48,16,512]{2,0,1:T(8,128)(2,1)}), bf16[1536,16,512]{2,0,1:T(8,128)(2,1)}) %all-gather.18.cloned.1.call-update) | async-done | bytes 25165840 | tf_op jit(solution)/shard_map/all_gather | solution.py:246
  711.9 26.2 multiply_convert_fusion.2
  738.2 17.1 convolution_convert_fusion
  762.1 17.6 gather_fusion.1
  779.7 16.5 fusion.34
  796.4 28.8 fusion.37
  825.2 11.2 concatenate.38
  836.4 19.7 gather_fusion.4
  876.1 20.9 all-to-all-done.4
  899.1 202.6 %while.29 = (s32[]{:T(128)}, f32[2048,128]{0,1:T(8,128)}, f32[2048,128]{1,0:T(8,128)}, f32[2,512,384]{1,0,2:T(2,128)}, s32[2]{0:T(128)S(1)}, /*index=5*/bf16[102...) while((s32[]{:T(128)}, f32[2048,128]{0,1:T(8,128)}, ...), condition=%wide.region_26.27_spmd, body=%wide.region_22.26_spmd.sunk | while | flops 3117036032 | bytes 171743760 | solution.py:347
  934.5 24.9 fusion.171
  959.5 25.1 fusion.169
  985.6 15.0 dynamic_update_slice.32
  1035.5 24.9 fusion.171
  1060.4 25.1 fusion.169
  1086.6 15.0 dynamic_update_slice.32
  1107.3 38.9 %fusion.36 = f32[16,1024,1536]{2,1,0:T(8,128)} fusion(bf16[16,160,1536]{2,1,0:T(8,128)(2,1)} %bitcast.281, bf16[16,160,512]{2,1,0:T(8,128)(2,1)} %get-tuple-element.393, bf16[16,160,512]{2,1,0:T(8,128)(2,1)} %get-tuple-element.392), kind=kOutput, calls=%fused_computation.79 | convolution fusion | flops 8063549440 | bytes 113770496 | tf_op jit(solution)/shard_map/ecd,ecj->dej/dot_general | solution.py:379
  1181.8 23.4 fusion.38
  1206.6 49.2 %copy.212 = f32[1536,8192]{1,0:T(8,128)} copy(f32[1536,8192]{0,1:T(8,128)} %bitcast.277) | data formatting | bytes 100663296 | tf_op jit(solution)/shard_map/reshape | solution.py:384
  1255.9 97.4 %copy.211 = f32[1536,16384]{1,0:T(8,128)} copy(f32[1536,16384]{0,1:T(8,128)} %bitcast.73) | data formatting | bytes 201326592 | tf_op jit(solution)/shard_map/reshape | solution.py:381
  1368.7 115.2 %pad_maximum_fusion = f32[1536,28672]{1,0:T(8,128)} fusion(f32[1536,8192]{1,0:T(8,128)} %copy.212, f32[1536,16384]{1,0:T(8,128)} %copy.211, f32[1536,1536]{1,0:T(8,128)} %fusion.58, f32[1536,2560]{1,0:T(8,128)} %fusion.51), kind=kLoop, calls=%fused_computation.65 | loop fusion | flops 132120576 | bytes 352321536 | tf_op jit(solution)/shard_map/concatenate | solution.py:386
  1494.1 40.4 %all-reduce.8 = (f32[1536]{0:T(1024)S(1)}, f32[1536]{0:T(1024)S(1)}) all-reduce(f32[1536]{0:T(1024)S(1)} %get-tuple-element.336, f32[1536]{0:T(1024)S(1)} %copy-done.57), channel_id=2, replica_groups=mesh['head'=4,'seq'=8] {'head','seq'}, use_global_device_ids=true, to_apply=%region_29.30.clone | all-reduce | flops 3072 | bytes 24576
  1538.9 1385.9 %reduce-scatter.5.cloned.1.call-done = f32[48,28672]{1,0:T(8,128)} async-done(((f32[1536,28672]{1,0:T(8,128)}), f32[48,28672]{1,0:T(8,128)}) %reduce-scatter.5.cloned.1.call-update) | async-done | bytes 5505040 | tf_op jit(solution)/shard_map/reduce_scatter | solution.py:385
  (394 shorter events, 336.1 us)
Async XLA Ops:
  7.2 50.8 %copy-start.63 = (s32[32]{0:T(128)S(1)}, s32[32]{0:T(128)}, u32[]{:S(2)}) copy-start(s32[32]{0:T(128)} %param.19) | copy-start | bytes 388
  7.2 57.9 %copy-start.8 = (bf16[256,1536]{1,0:T(8,128)(2,1)S(1)}, bf16[256,1536]{1,0:T(8,128)(2,1)}, u32[]{:S(2)}) copy-start(bf16[256,1536]{1,0:T(8,128)(2,1)} %param.17) | copy-start | bytes 2359300
  7.2 61.4 %all-gather.8.cloned.1.call-start = ((), (), s32[]{:S(2)}) async-start(), calls=%async_computation.10 | async-start | bytes 1622016 | tf_op jit(solution)/shard_map/all_gather | solution.py:154
  8.0 117.6 %all-gather.10.cloned.1.call-start = ((), (), s32[]{:S(2)}) async-start(), calls=%async_computation.11 | async-start | bytes 1622016 | tf_op jit(solution)/shard_map/all_gather | solution.py:153
  8.7 182.3 %all-gather.12.cloned.1.call-start = ((), (), s32[]{:S(2)}) async-start(), calls=%async_computation.12 | async-start | bytes 4866048 | tf_op jit(solution)/shard_map/all_gather | solution.py:152
  9.5 368.9 %all-gather.14.cloned.1.call-start = ((), (), s32[]{:S(2)}) async-start(), calls=%async_computation.13 | async-start | bytes 4866048 | tf_op jit(solution)/shard_map/all_gather | solution.py:155
  10.0 545.8 %all-gather.16.cloned.1.call-start = ((), (), s32[]{:S(2)}) async-start(), calls=%async_computation.14 | async-start | bytes 51904512 | tf_op jit(solution)/shard_map/all_gather | solution.py:235
  13.5 698.4 %all-gather.18.cloned.1.call-start = ((), (), s32[]{:S(2)}) async-start(), calls=%async_computation.15 | async-start | bytes 25952256 | tf_op jit(solution)/shard_map/all_gather | solution.py:246
  58.0 133.0 %copy-start.40 = (f32[1536]{0:T(1024)}, f32[1536]{0:T(1024)S(1)}, u32[]{:S(2)}) copy-start(f32[1536]{0:T(1024)S(1)} %convert_element_type.142) | copy-start | bytes 18436
  65.4 130.0 %copy-start.54 = (f32[256]{0:T(256)}, f32[256]{0:T(256)S(1)}, u32[]{:S(2)}) copy-start(f32[256]{0:T(256)S(1)} %add_rsqrt_fusion.1) | copy-start | bytes 3076
  71.4 124.0 %all-to-all-start = ((bf16[256,4,128]{2,0,1:T(8,128)(2,1)}), bf16[256,4,128]{2,0,1:T(8,128)(2,1)S(1)}, u32[]{:S(2)}, u32[]{:S(2)}) async-start(bf16[256,4,128]{2,0,1:T(8,128)(2,1)} %bitcast.217), calls=%async_computation | async-start | bytes 524288 | tf_op jit(solution)/shard_map/all_to_all | solution.py:177
  195.4 14.7 all-to-all-start.1
  210.1 72.2 %all-to-all-start.2 = ((bf16[256,4,384]{0,2,1:T(8,128)(2,1)}), bf16[256,4,384]{0,2,1:T(8,128)(2,1)S(1)}, u32[]{:S(2)}, u32[]{:S(2)}) async-start(bf16[256,4,384]{0,2,1:T(8,128)(2,1)} %bitcast.43), calls=%async_computation.2 | async-start | bytes 1572864 | tf_op jit(solution)/shard_map/all_to_all | solution.py:175
  213.8 68.2 %collective-permute-start.1 = (bf16[1024,128]{1,0:T(8,128)(2,1)S(1)}, bf16[1024,128]{1,0:T(8,128)(2,1)S(1)}, u32[]{:S(2)}, u32[]{:S(2)}) collective-permute-start(bf16[1024,128]{1,0:T(8,128)(2,1)S(1)} %bitcast.313), channel_id=1, source_target_pairs={{0,1},{1,2},{2,3},{3,4},{4,5},{5,6},{6,7},{8,9},{9,10},{10,11},{11... | collective-permute-start | bytes 786440 | tf_op jit(solution)/shard_map/ppermute | solution.py:26
  215.2 67.1 %copy-start.58 = (s32[2048,1]{0,1:T(1,128)}, s32[2048,1]{0,1:T(1,128)S(1)}, u32[]{:S(2)}) copy-start(s32[2048,1]{0,1:T(1,128)S(1)} %compare_select_fusion) | copy-start | bytes 24580
  215.3 66.9 %collective-permute-start = (bf16[1024,128]{0,1:T(8,128)(2,1)S(1)}, bf16[1024,128]{0,1:T(8,128)(2,1)S(1)}, u32[]{:S(2)}, u32[]{:S(2)}) collective-permute-start(bf16[1024,128]{0,1:T(8,128)(2,1)S(1)} %copy.179), channel_id=1, source_target_pairs={{0,1},{1,2},{2,3},{3,4},{4,5},{5,6},{6,7},{8,9},{9,10},{10,11},{11... | collective-permute-start | bytes 786440 | tf_op jit(solution)/shard_map/ppermute | solution.py:26
  330.7 47.4 %all-to-all-start.3 = ((bf16[4,256,384]{2,1,0:T(8,128)(2,1)}), bf16[4,256,384]{2,1,0:T(8,128)(2,1)S(1)}, u32[]{:S(2)}, u32[]{:S(2)}) async-start(bf16[4,256,384]{2,1,0:T(8,128)(2,1)} %bitcast.315), calls=%async_computation.3 | async-start | bytes 1572864 | tf_op jit(solution)/shard_map/all_to_all | solution.py:219
  337.7 40.7 %copy-start.9 = (bf16[256,1536]{1,0:T(8,128)(2,1)S(1)}, bf16[256,1536]{1,0:T(8,128)(2,1)}, u32[]{:S(2)}) copy-start(bf16[256,1536]{1,0:T(8,128)(2,1)} %param.17) | copy-start | bytes 2359300
  398.4 313.5 %copy-start.45 = (f32[16,160]{1,0:T(8,128)}, f32[16,160]{1,0:T(8,128)S(1)}, u32[]{:S(2)}) copy-start(f32[16,160]{1,0:T(8,128)S(1)} %mul.482) | copy-start | bytes 30724
  796.4 68.5 %copy-start.51 = (bf16[256,16]{0,1:T(8,128)(2,1)}, bf16[256,16]{0,1:T(8,128)(2,1)S(1)}, u32[]{:S(2)}) copy-start(bf16[256,16]{0,1:T(8,128)(2,1)S(1)} %select_reduce_fusion) | copy-start | bytes 24580
  871.9 25.1 all-to-all-start.4
  1104.6 41.7 %copy-start.29 = (f32[2,512,384]{1,0,2:T(2,128)S(1)}, f32[2,512,384]{1,0,2:T(2,128)}, u32[]{:S(2)}) copy-start(f32[2,512,384]{1,0,2:T(2,128)} %get-tuple-element.245) | copy-start | bytes 4718596
  1104.6 44.2 %collective-permute-start.3 = (bf16[1024,128]{1,0:T(8,128)(2,1)}, bf16[1024,128]{1,0:T(8,128)(2,1)}, u32[]{:S(2)}, u32[]{:S(2)}) collective-permute-start(bf16[1024,128]{1,0:T(8,128)(2,1)} %slice.161), channel_id=1, source_target_pairs={{1,0},{2,1},{3,2},{4,3},{5,4},{6,5},{7,6},{9,8},{10,9},{11,10},{12... | collective-permute-start | bytes 786440 | tf_op jit(solution)/shard_map/ppermute | solution.py:26
  1106.0 48.7 %collective-permute-start.2 = (bf16[1024,128]{0,1:T(8,128)(2,1)S(1)}, bf16[1024,128]{0,1:T(8,128)(2,1)S(1)}, u32[]{:S(2)}, u32[]{:S(2)}) collective-permute-start(bf16[1024,128]{0,1:T(8,128)(2,1)S(1)} %slice.162), channel_id=1, source_target_pairs={{1,0},{2,1},{3,2},{4,3},{5,4},{6,5},{7,6},{9,8},{10,9},{11,10},{12... | collective-permute-start | bytes 786440 | tf_op jit(solution)/shard_map/ppermute | solution.py:26
  1150.6 12.7 all-to-all-start.7
  1163.4 14.2 all-to-all-start.6
  1177.5 182.0 %all-to-all-start.5 = ((bf16[4,256,384]{1,2,0:T(8,128)(2,1)}), bf16[4,256,384]{1,2,0:T(8,128)(2,1)}, u32[]{:S(2)}, u32[]{:S(2)}) async-start(bf16[4,256,384]{1,2,0:T(8,128)(2,1)} %copy.205), calls=%async_computation.5 | async-start | bytes 1572864 | tf_op jit(solution)/shard_map/all_to_all | solution.py:364
  1181.7 302.2 %reduce-scatter.7.cloned.1.call-start = ((), (), s32[]{:S(2)}) async-start(), calls=%async_computation.17 | async-start | bytes 811008
  1206.6 1718.2 %reduce-scatter.5.cloned.1.call-start = ((), (), s32[]{:S(2)}) async-start(), calls=%async_computation.16 | async-start | bytes 181665792 | tf_op jit(solution)/shard_map/reduce_scatter | solution.py:385
  1255.9 97.4 %copy-start.6 = (f32[256,1536]{1,0:T(8,128)S(1)}, f32[256,1536]{1,0:T(8,128)}, u32[]{:S(2)}) copy-start(f32[256,1536]{1,0:T(8,128)} %copy-done.5) | copy-start | bytes 4718596
  1255.9 97.4 %copy-start.26 = (bf16[256,4,384]{0,2,1:T(8,128)(2,1)S(1)}, bf16[256,4,384]{0,2,1:T(8,128)(2,1)}, u32[]{:S(2)}) copy-start(bf16[256,4,384]{0,2,1:T(8,128)(2,1)} %copy-done.25) | copy-start | bytes 2359300
  1489.6 46.1 %copy-start.7 = (f32[256,1536]{1,0:T(8,128)S(1)}, f32[256,1536]{1,0:T(8,128)}, u32[]{:S(2)}) copy-start(f32[256,1536]{1,0:T(8,128)} %copy-done.5) | copy-start | bytes 4718596
  (72 other events, 712.6 us)
Sparse Core Ops, SparseCore 0:
  10.9 57.6 all-gather.7
  71.5 53.9 all-gather.9
  128.5 62.5 all-gather.11
  193.8 69.0 all-gather.13
  266.1 289.6 all-gather.15
  559.1 152.8 all-gather.17
  1206.7 95.8 reduce-scatter.6
  1484.1 1440.7 reduce-scatter.4
where the time goes:
time: 2960 us; the launch traced here: 2940 us
  waiting for transfers between devices  1860 us (63%)
  matrix products  392 us (13%)
  local copies, waits for them, and re-layouts  343 us (12%)
  other arithmetic  163 us (6%)
  blocking collectives  127 us (4%)
  starting transfers between devices  39.7 us (1%)
    reduce_scatter x1, waiting for transfers between devices, shards(): lax.psum_scatter(jnp.concatenate([attention_part, output_part, inner_part...  1390 us
    all_gather x1, waiting for transfers between devices, shards(): lax.all_gather(expert_input, ('head', 'seq'), axis=0, tiled=True)  148 us
    all_gather x1, waiting for transfers between devices, shards(): lax.all_gather(expert_output, ('head', 'seq'), axis=0, tiled=True)  131 us
    concatenate x1, other arithmetic, shards(): jnp.concatenate([attention_part, output_part, inner_part, outer_part], ax...  115 us
    reshape x1, local copies, waits for them, and re-layouts, shards(): inner_part = jnp.einsum('ecd,ecj->dej', dispatched, gate_up_grad, preferr...  97.4 us
    unnamed x2, blocking collectives  82.5 us
    all_gather x1, waiting for transfers between devices, shards(): lax.all_gather(query_weight, ('head', 'seq'), axis=0, tiled=True)  62.4 us
  transfers between devices with their start and end apart: 20, of which 11 were waited for; matrix products, arithmetic and copies ran while one was open for 18% of the time, Pallas kernels for 0%

commit v1 on v0

v1 whole, which is shorter than its diff:
```python
import functools

import jax
import jax.numpy as jnp
from jax import lax
from jax.experimental import pallas as pl
from jax.experimental.pallas import tpu as pltpu
from jax.sharding import PartitionSpec as P

MODEL_WIDTH = 1536
QUERY_HEADS = 24
KEY_VALUE_HEADS = 8
HEAD_WIDTH = 64
FF = 512
EXPERTS = 16
CAP = 160

EPS = 1e-06
ATTN_SCALE = 1.0 / 64.0
RESIDUAL_SCALE = 0.22
MASKED = -1e30

GROUP = QUERY_HEADS // KEY_VALUE_HEADS
QUERY_COLS = QUERY_HEADS * HEAD_WIDTH
PAIR_COLS = KEY_VALUE_HEADS * HEAD_WIDTH
LANES = 128
HALF = HEAD_WIDTH // 2
PAIRED = LANES // HEAD_WIDTH
EXPERT_COLS = 3 * FF

bf16 = jnp.bfloat16
f32 = jnp.float32

NT = (((1,), (1,)), ((), ()))
TN = (((0,), (0,)), ((), ()))
VMEM_BYTES = 56 * 1024 * 1024


def dot(left, right, dims=(((1,), (0,)), ((), ()))):
    return lax.dot_general(left, right, dims, preferred_element_type=f32)


def swap(block, mask):
    count = lax.axis_size("seq")
    return lax.ppermute(block, "seq", [(i, i ^ mask) for i in range(count)])


def around(block, distance):
    count = lax.axis_size("head")
    return lax.ppermute(block, "head", [(i, (i + distance) % count) for i in range(count)])


def along_stream(block, distance):
    heads, groups = lax.axis_size("head"), lax.axis_size("seq")
    route = []
    for group in range(groups):
        for head in range(heads):
            target = group * heads + head + distance
            if 0 <= target < heads * groups:
                route.append((head * groups + group, (target % heads) * groups + target // heads))
    return lax.ppermute(block, ("head", "seq"), route)


def side(mask):
    return (lax.axis_index("seq") // mask) % 2


def far_masks():
    masks, mask = [], 2
    while mask < lax.axis_size("seq"):
        masks.append(mask)
        mask = mask * 2
    return masks


def join(own, other, bit, axis):
    return jnp.where(
        bit == 0, jnp.stack([own, other], axis=axis), jnp.stack([other, own], axis=axis)
    )


def swap_head(block, mask):
    count = lax.axis_size("head")
    return lax.ppermute(block, "head", [(i, i ^ mask) for i in range(count)])


def head_side(mask):
    return (lax.axis_index("head") // mask) % 2


def after(value, *others):
    return lax.optimization_barrier((value,) + others)[0]


class Flow:
    def __init__(self, steps):
        self.steps = steps
        self.value = None
        self.moves = []
        self.done = False
        self.feed(None)

    def feed(self, results):
        try:
            self.moves = self.steps.send(results)
        except StopIteration as stop:
            self.value, self.moves, self.done = stop.value, [], True


class Clock:
    def __init__(self):
        self.last = ()

    def begin(self, *flows, ready=()):
        flows = [flow for flow in flows if not flow.done]
        blocks = tuple(block for flow in flows for block, _ in flow.moves)
        if not blocks:
            return [], []
        tied = lax.optimization_barrier(blocks + tuple(self.last) + tuple(ready))
        movers = [move for flow in flows for _, move in flow.moves]
        return flows, [move(block) for move, block in zip(movers, tied)]

    def end(self, pending, *held):
        flows, results = pending
        if not results:
            return
        if held:
            results = list(lax.optimization_barrier(tuple(results) + held)[: len(results)])
        self.last = tuple(results)
        for flow in flows:
            count = len(flow.moves)
            flow.feed(results[:count])
            results = results[count:]

    def tick(self, *flows, ready=()):
        self.end(self.begin(*flows, ready=ready))

    def finish(self, *flows):
        while not all(flow.done for flow in flows):
            self.tick(*flows)
        return flows[0].value if len(flows) == 1 else [flow.value for flow in flows]


def by_seq(mask):
    return lambda block: swap(block, mask)


def by_head(mask):
    return lambda block: swap_head(block, mask)


def one_move(block, move):
    (result,) = yield [(block, move)]
    return result


def line_gather(block):
    heads = lax.axis_size("head")
    here = lax.axis_index("head")
    whole = jnp.zeros((heads,) + block.shape, block.dtype)
    whole = lax.dynamic_update_index_in_dim(whole, block, here, 0)
    results = yield [
        (block, functools.partial(around, distance=distance)) for distance in range(1, heads)
    ]
    for distance, result in enumerate(results, 1):
        whole = lax.dynamic_update_index_in_dim(whole, result, (here - distance) % heads, 0)
    return whole


def rows_gather(block):
    lines = yield from line_gather(block)
    masks = far_masks()
    middle = lines.shape[0] // 2
    parts = [(lines[:middle], masks), (lines[middle:], masks[::-1])]
    for step in range(len(masks)):
        results = yield [(part, by_seq(order[step])) for part, order in parts]
        parts = [
            (
                join(
                    part,
                    result,
                    side(order[step]),
                    1 + sum(1 for other in order[:step] if other > order[step]),
                ),
                order,
            )
            for (part, order), result in zip(parts, results)
        ]
    whole = jnp.concatenate([part for part, _ in parts], axis=0)
    (result,) = yield [(whole, by_seq(1))]
    whole = join(whole, result, side(1), 1 + len(masks))
    return whole.reshape(MODEL_WIDTH, block.shape[1])


def rows_scatter(kept, sent):
    masks = far_masks()
    (result,) = yield [(sent, by_seq(1))]
    whole = (kept.astype(f32) + result.astype(f32)).astype(bf16)
    whole = whole.reshape(whole.shape[:1] + (2,) * len(masks) + whole.shape[2:])
    middle = whole.shape[0] // 2
    parts = [(whole[:middle], masks), (whole[middle:], masks[::-1])]
    for step in range(len(masks)):
        axes = [
            1 + sum(1 for other in order[step + 1 :] if other > order[step])
            for _, order in parts
        ]
        results = yield [
            (lax.index_in_dim(part, 1, axis, False), by_seq(order[step]))
            for (part, order), axis in zip(parts, axes)
        ]
        parts = [
            (
                (
                    lax.index_in_dim(part, 0, axis, False).astype(f32) + result.astype(f32)
                ).astype(bf16),
                order,
            )
            for (part, order), axis, result in zip(parts, axes, results)
        ]
    return jnp.concatenate([part for part, _ in parts], axis=0)


def line_scatter(terms):
    heads = lax.axis_size("head")
    here = lax.axis_index("head")
    results = yield [
        (
            lax.dynamic_index_in_dim(terms, (here + distance) % heads, 0, False),
            functools.partial(around, distance=distance),
        )
        for distance in range(1, heads)
    ]
    total = lax.dynamic_index_in_dim(terms, here, 0, False).astype(f32)
    for result in results:
        total = total + result.astype(f32)
    return total


def tokens_gather(block):
    masks = far_masks()
    middle = block.shape[0] // 2
    parts = [(block[:middle], masks), (block[middle:], masks[::-1])]
    for step in range(len(masks)):
        results = yield [(part, by_seq(order[step])) for part, order in parts]
        parts = [
            (
                jnp.stack(
                    [part, result],
                    axis=sum(1 for other in order[:step] if other > order[step]),
                ),
                order,
            )
            for (part, order), result in zip(parts, results)
        ]
    whole = jnp.concatenate([part for part, _ in parts], axis=len(masks))
    return whole.reshape((lax.axis_size("seq") // 2 * block.shape[0],) + block.shape[1:])


def tokens_scatter(own, other):
    masks = far_masks()
    blocks = lax.axis_size("seq") // 2
    (result,) = yield [(other, by_seq(1))]
    whole = (own.astype(f32) + result.astype(f32)).astype(bf16)
    whole = whole.reshape((2,) * len(masks) + (own.shape[0] // blocks, own.shape[1]))
    middle = whole.shape[-2] // 2
    parts = [(whole[..., :middle, :], masks), (whole[..., middle:, :], masks[::-1])]
    for step in range(len(masks)):
        axes = [sum(1 for other in order[step + 1 :] if other > order[step]) for _, order in parts]
        results = yield [
            (lax.index_in_dim(part, 1, axis, False), by_seq(order[step]))
            for (part, order), axis in zip(parts, axes)
        ]
        last = step == len(masks) - 1
        parts = [
            (
                (
                    lax.index_in_dim(part, 0, axis, False).astype(f32) + result.astype(f32)
                ).astype(f32 if last else bf16),
                order,
            )
            for (part, order), axis, result in zip(parts, axes, results)
        ]
    return jnp.concatenate([part for part, _ in parts], axis=0)


def doc_start(doc_lengths, places):
    starts = jnp.cumsum(doc_lengths) - doc_lengths
    earlier = starts[None, :] <= places[:, None]
    return jnp.max(jnp.where(earlier, starts[None, :], 0), axis=1)


def rope_tables(places):
    frequency = jnp.exp(
        -jnp.log(10000.0) * 2.0 * jnp.arange(HALF).astype(f32) / HEAD_WIDTH
    )
    angles = places.astype(f32)[:, None] * frequency[None, :]
    cosine, sine = jnp.cos(angles), jnp.sin(angles)
    return (
        jnp.concatenate([cosine] * (LANES // HALF), axis=1),
        jnp.concatenate([-sine, sine] * PAIRED, axis=1),
    )


def turn(values, cosine, sine, sign):
    lane = lax.broadcasted_iota(jnp.int32, (values.shape[0], LANES), 1) % HEAD_WIDTH
    pieces = []
    for first in range(0, values.shape[1], LANES):
        piece = values[:, first : first + LANES]
        swapped = jnp.where(
            lane < HALF, pltpu.roll(piece, LANES - HALF, 1), pltpu.roll(piece, HALF, 1)
        )
        pieces.append(piece * cosine + (sign * swapped) * sine)
    return jnp.concatenate(pieces, axis=1)


def whole_block(shape):
    return pl.BlockSpec(shape, lambda *_: (0,) * len(shape), pipeline_mode=pl.Buffered(1))


def params():
    return pltpu.CompilerParams(vmem_limit_bytes=VMEM_BYTES)


def cost(flops, moved, transcendentals=0, weight=1):
    return pl.CostEstimate(
        flops=weight * flops,
        bytes_accessed=weight * moved,
        transcendentals=weight * transcendentals,
    )


def rms_inverse(values):
    return lax.rsqrt(jnp.mean(values * values, axis=1, keepdims=True) + EPS)


def norm_backward(values, inverse, gain, incoming):
    scaled = incoming * gain
    mean_term = jnp.mean(scaled * values, axis=1, keepdims=True)
    values_grad = inverse * scaled - values * (inverse * inverse * inverse * mean_term)
    gain_grad = jnp.sum(incoming * values * inverse, axis=0, keepdims=True)
    return (values_grad, gain_grad)


def enter(hidden_in, w_small, cosine, sine):
    tokens = hidden_in.shape[0]
    small_cols = w_small.shape[1]

    def kernel(hidden_ref, weight_ref, cosine_ref, sine_ref, normed_ref, kv_ref, gain_ref):
        extras = jnp.transpose(weight_ref[:, 2 * PAIR_COLS :].astype(f32))
        gains = extras[EXPERTS : EXPERTS + 8]
        gain_ref[...] = gains
        values = hidden_ref[...].astype(f32)
        normed = (values * rms_inverse(values) * gains[:1]).astype(bf16)
        normed_ref[...] = normed
        keys = dot(normed, weight_ref[:, :PAIR_COLS])
        kv_ref[0] = turn(keys, cosine_ref[...], sine_ref[...], 1.0).astype(bf16)
        kv_ref[1] = dot(normed, weight_ref[:, PAIR_COLS : 2 * PAIR_COLS]).astype(bf16)

    return pl.pallas_call(
        kernel,
        out_shape=[
            jax.ShapeDtypeStruct((tokens, MODEL_WIDTH), bf16),
            jax.ShapeDtypeStruct((2, tokens, PAIR_COLS), bf16),
            jax.ShapeDtypeStruct((8, MODEL_WIDTH), f32),
        ],
        compiler_params=params(),
        cost_estimate=cost(
            4 * tokens * MODEL_WIDTH * PAIR_COLS, 2 * MODEL_WIDTH * (small_cols + 2 * tokens)
        ),
        name="enter",
    )(hidden_in, w_small, cosine, sine)


def project_queries(normed, w_square, cosine, sine):
    tokens = normed.shape[0]
    width = 512

    def kernel(normed_ref, weight_ref, cosine_ref, sine_ref, out_ref):
        product = dot(normed_ref[...], weight_ref[...])
        out_ref[...] = turn(product, cosine_ref[...], sine_ref[...], 1.0).astype(bf16)

    return pl.pallas_call(
        kernel,
        grid=(QUERY_COLS // width,),
        in_specs=[
            whole_block((tokens, MODEL_WIDTH)),
            pl.BlockSpec((MODEL_WIDTH, width), lambda i: (0, i)),
            whole_block((tokens, LANES)),
            whole_block((tokens, LANES)),
        ],
        out_specs=pl.BlockSpec((tokens, width), lambda i: (0, i)),
        out_shape=jax.ShapeDtypeStruct((tokens, QUERY_COLS), bf16),
        compiler_params=params(),
        cost_estimate=cost(
            2 * tokens * MODEL_WIDTH * QUERY_COLS, 2 * MODEL_WIDTH * (QUERY_COLS + 2 * tokens)
        ),
        name="project_queries",
    )(normed, w_square, cosine, sine)


def square_block(index):
    return pl.BlockSpec(
        (MODEL_WIDTH, MODEL_WIDTH), lambda *_: (0, index), pipeline_mode=pl.Buffered(1)
    )


def leave_attention(mixture, w_square, hidden_in, gains):
    tokens = mixture.shape[0]

    def kernel(mixture_ref, weight_ref, hidden_ref, gain_ref, middle_ref, normed_ref):
        branch = dot(mixture_ref[...], weight_ref[...], NT)
        middle = hidden_ref[...].astype(f32) + RESIDUAL_SCALE * branch
        middle_ref[...] = middle
        normed_ref[...] = (middle * rms_inverse(middle) * gain_ref[1:2]).astype(bf16)

    return pl.pallas_call(
        kernel,
        grid=(1,),
        in_specs=[
            whole_block((tokens, QUERY_COLS)),
            square_block(1),
            whole_block((tokens, MODEL_WIDTH)),
            whole_block((8, MODEL_WIDTH)),
        ],
        out_specs=[whole_block((tokens, MODEL_WIDTH))] * 2,
        out_shape=[
            jax.ShapeDtypeStruct((tokens, MODEL_WIDTH), f32),
            jax.ShapeDtypeStruct((tokens, MODEL_WIDTH), bf16),
        ],
        compiler_params=params(),
        cost_estimate=cost(
            2 * tokens * MODEL_WIDTH * QUERY_COLS, 2 * MODEL_WIDTH * (QUERY_COLS + 5 * tokens)
        ),
        name="leave_attention",
    )(mixture, w_square, hidden_in, gains)


def return_to_attention(back, back_parts, code, normed_two, middle, out_grad, w_small, w_square, gains):
    tokens = middle.shape[0]
    parts = len(back_parts)

    def kernel(
        back_ref,
        code_ref,
        normed_ref,
        middle_ref,
        grad_ref,
        router_ref,
        weight_ref,
        gain_ref,
        *refs,
    ):
        logits_grad_ref, middle_grad_ref, branch_grad_ref, mixture_grad_ref, gain_grad_ref = refs[
            parts:
        ]
        total = back_ref[...]
        for ref in refs[:parts]:
            total = total + ref[...].astype(f32)
        code = code_ref[...].astype(f32)
        lane = lax.broadcasted_iota(jnp.int32, (tokens, LANES), 1)
        router = jnp.where(
            lax.broadcasted_iota(jnp.int32, (MODEL_WIDTH, LANES), 1) < EXPERTS,
            router_ref[...],
            jnp.asarray(0.0, bf16),
        )
        logits = jnp.where(code > 0.5, dot(normed_ref[...], router), MASKED)
        raised = jnp.exp(logits - jnp.max(logits, axis=1, keepdims=True))
        raised = jnp.where(code > 0.5, raised, 0.0)
        gates = raised / jnp.sum(raised, axis=1, keepdims=True)
        extra = total[:, MODEL_WIDTH:]
        gate_grad = extra + pltpu.roll(extra, LANES - EXPERTS, 1)
        gate_grad = jnp.where((lane < EXPERTS) & (code > 0.5) & (code < 1.5), gate_grad, 0.0)
        inner = jnp.sum(gates * gate_grad, axis=1, keepdims=True)
        logits_grad = (gates * (gate_grad - inner)).astype(bf16)
        logits_grad_ref[...] = logits_grad
        incoming = total[:, :MODEL_WIDTH] + dot(logits_grad, router, NT)
        middle = middle_ref[...]
        norm_grad, gain_grad = norm_backward(
            middle, rms_inverse(middle), gain_ref[1:2], incoming
        )
        middle_grad = grad_ref[...].astype(f32) + norm_grad
        middle_grad_ref[...] = middle_grad
        branch_grad = (RESIDUAL_SCALE * middle_grad).astype(bf16)
        branch_grad_ref[...] = branch_grad
        mixture_grad_ref[...] = dot(branch_grad, weight_ref[...]).astype(bf16)
        gain_grad_ref[...] = jnp.broadcast_to(gain_grad, (8, MODEL_WIDTH))

    wide = MODEL_WIDTH + LANES
    return pl.pallas_call(
        kernel,
        grid=(1,),
        in_specs=[
            whole_block((tokens, wide)),
            whole_block((tokens, LANES)),
            whole_block((tokens, MODEL_WIDTH)),
            whole_block((tokens, MODEL_WIDTH)),
            whole_block((tokens, MODEL_WIDTH)),
            pl.BlockSpec(
                (MODEL_WIDTH, LANES),
                lambda *_: (0, 2 * PAIR_COLS // LANES),
                pipeline_mode=pl.Buffered(1),
            ),
            square_block(1),
            whole_block((8, MODEL_WIDTH)),
        ]
        + [whole_block((tokens, wide))] * parts,
        out_specs=[
            whole_block((tokens, LANES)),
            whole_block((tokens, MODEL_WIDTH)),
            whole_block((tokens, MODEL_WIDTH)),
            whole_block((tokens, QUERY_COLS)),
            whole_block((8, MODEL_WIDTH)),
        ],
        out_shape=[
            jax.ShapeDtypeStruct((tokens, LANES), bf16),
            jax.ShapeDtypeStruct((tokens, MODEL_WIDTH), f32),
            jax.ShapeDtypeStruct((tokens, MODEL_WIDTH), bf16),
            jax.ShapeDtypeStruct((tokens, QUERY_COLS), bf16),
            jax.ShapeDtypeStruct((8, MODEL_WIDTH), f32),
        ],
        compiler_params=params(),
        cost_estimate=cost(
            2 * tokens * MODEL_WIDTH * QUERY_COLS, 2 * MODEL_WIDTH * (QUERY_COLS + 12 * tokens)
        ),
        name="return_to_attention",
    )(back, code, normed_two, middle, out_grad, w_small, w_square, gains, *back_parts)


def store_rows(product, columns, place, core, kept_ref, sent_ref):
    heads, far, rows = kept_ref.shape[:3]
    for mine in range(2):

        @pl.when(core == mine)
        def _():
            for head in range(heads):
                for group in range(2 * far):
                    first = (head * 2 * far + group) * rows
                    piece = product[first : first + rows]
                    target = kept_ref if group % 2 == mine else sent_ref
                    target[head, (group // 2) ^ place, :, columns] = piece


def weight_terms(lefts, rights):
    tokens = lefts[0].shape[0]
    tile = 384
    operands, in_specs, runs = [], [], []
    first = 0
    for left, parts in zip(lefts, rights):
        left_at = len(operands)
        operands.append(left)
        in_specs.append(whole_block((tokens, MODEL_WIDTH)))
        for right in parts:
            steps = right.shape[1] // tile
            runs.append((first, steps, left_at, len(operands)))
            operands.append(right)
            in_specs.append(
                pl.BlockSpec(
                    (tokens, tile),
                    functools.partial(
                        lambda i, first, steps: (0, jnp.clip(i - first, 0, steps - 1)),
                        first=first,
                        steps=steps,
                    ),
                )
            )
            first = first + steps
    width = first * tile

    def kernel(*refs):
        step = pl.program_id(0)
        for start, steps, left_at, right_at in runs:

            @pl.when((step >= start) & (step < start + steps))
            def _():
                refs[-1][...] = dot(refs[left_at][...], refs[right_at][...], TN).astype(bf16)

    return pl.pallas_call(
        kernel,
        grid=(first,),
        in_specs=in_specs,
        out_specs=pl.BlockSpec((MODEL_WIDTH, tile), lambda i: (0, i)),
        out_shape=jax.ShapeDtypeStruct((MODEL_WIDTH, width), bf16),
        compiler_params=params(),
        cost_estimate=cost(
            2 * tokens * MODEL_WIDTH * width,
            2 * width * (MODEL_WIDTH + tokens),
        ),
        name="weight_terms",
    )(*operands)


def leave(
    place,
    heads,
    groups,
    terms,
    query_grads,
    cosine,
    sine,
    hidden_in,
    normed,
    middle_grad,
    normed_two,
    logits_grad,
    gain_grad_two,
    w_small,
    w_query,
    gains,
):
    tokens = hidden_in.shape[0]
    parts = len(terms)
    count = len(terms[0])
    part_cols = PAIR_COLS // parts
    query_cols = QUERY_COLS // parts
    small_cols = w_small.shape[1]
    part_shape = (heads, groups // 2, MODEL_WIDTH // (heads * groups), small_cols)

    def kernel(
        place_ref,
        cosine_ref,
        sine_ref,
        hidden_ref,
        normed_ref,
        middle_grad_ref,
        normed_two_ref,
        logits_grad_ref,
        gain_two_ref,
        small_ref,
        query_weight_ref,
        gain_ref,
        *refs,
    ):
        query_grad_refs, term_refs = refs[:parts], refs[parts:-3]
        input_grad_ref, kept_ref, sent_ref = refs[-3:]

        def store(product, columns):
            store_rows(
                product.astype(bf16), columns, place_ref[0], place_ref[1], kept_ref, sent_ref
            )

        keys, lists = [], []
        for part in range(parts):
            total = term_refs[part * count][...]
            for ref in term_refs[part * count + 1 : (part + 1) * count]:
                total = total + ref[...].astype(f32)
            keys.append(turn(total[0], cosine_ref[...], sine_ref[...], -1.0).astype(bf16))
            lists.append(total[1].astype(bf16))
        keys = jnp.concatenate(keys, axis=1)
        lists = jnp.concatenate(lists, axis=1)
        incoming = dot(keys, small_ref[:, :PAIR_COLS], NT) + dot(
            lists, small_ref[:, PAIR_COLS : 2 * PAIR_COLS], NT
        )
        for part in range(parts):
            columns = slice(part * query_cols, (part + 1) * query_cols)
            incoming = incoming + dot(
                query_grad_refs[part][...], query_weight_ref[:, columns], NT
            )
        values = hidden_ref[...].astype(f32)
        norm_grad, gain_grad = norm_backward(
            values, rms_inverse(values), gain_ref[:1], incoming
        )
        input_grad_ref[...] = middle_grad_ref[...] + norm_grad
        normed = normed_ref[...]
        store(dot(normed, keys, TN), slice(0, PAIR_COLS))
        store(dot(normed, lists, TN), slice(PAIR_COLS, 2 * PAIR_COLS))
        two = gain_two_ref[:1]
        first_high = gain_grad.astype(bf16).astype(f32)
        second_high = two.astype(bf16).astype(f32)
        rows = jnp.concatenate(
            [
                jnp.zeros((EXPERTS, MODEL_WIDTH), f32),
                first_high,
                second_high,
                gain_grad - first_high,
                two - second_high,
                jnp.zeros((LANES - EXPERTS - 4, MODEL_WIDTH), f32),
            ],
            axis=0,
        )
        extras = dot(normed_two_ref[...], logits_grad_ref[...], TN) + jnp.transpose(rows)
        store(extras, slice(2 * PAIR_COLS, small_cols))

    return pl.pallas_call(
        kernel,
        grid=(1,),
        in_specs=[
            pl.BlockSpec(memory_space=pltpu.SMEM),
            whole_block((tokens, LANES)),
            whole_block((tokens, LANES)),
            whole_block((tokens, MODEL_WIDTH)),
            whole_block((tokens, MODEL_WIDTH)),
            whole_block((tokens, MODEL_WIDTH)),
            whole_block((tokens, MODEL_WIDTH)),
            whole_block((tokens, LANES)),
            whole_block((8, MODEL_WIDTH)),
            whole_block((MODEL_WIDTH, small_cols)),
            square_block(0),
            whole_block((8, MODEL_WIDTH)),
        ]
        + [whole_block((tokens, query_cols))] * parts
        + [whole_block((2, tokens, part_cols))] * (parts * count),
        out_specs=[
            whole_block((tokens, MODEL_WIDTH)),
            whole_block(part_shape),
            whole_block(part_shape),
        ],
        out_shape=[
            jax.ShapeDtypeStruct((tokens, MODEL_WIDTH), f32),
            jax.ShapeDtypeStruct(part_shape, bf16),
            jax.ShapeDtypeStruct(part_shape, bf16),
        ],
        compiler_params=params(),
        cost_estimate=cost(
            2 * tokens * MODEL_WIDTH * (QUERY_COLS + 4 * PAIR_COLS),
            2 * MODEL_WIDTH * (QUERY_COLS + 2 * small_cols + 8 * tokens),
        ),
        name="leave",
    )(
        place,
        cosine,
        sine,
        hidden_in,
        normed,
        middle_grad,
        normed_two,
        logits_grad,
        gain_grad_two,
        w_small,
        w_query,
        gains,
        *query_grads,
        *[array for part in terms for array in part],
    )


def stacked_heads(block, pair):
    first = pair * GROUP * HEAD_WIDTH
    return jnp.concatenate(
        [
            block[:, first + j * HEAD_WIDTH : first + (j + 1) * HEAD_WIDTH]
            for j in range(GROUP)
        ],
        axis=0,
    )


def masked_scores(keys, queries, starts, offset, causal):
    tokens = keys.shape[0]
    scores = dot(keys, queries, NT)
    key_place = lax.broadcasted_iota(jnp.int32, (tokens, tokens), 0)
    visible = key_place + offset >= starts
    if causal:
        visible = visible & (key_place <= lax.broadcasted_iota(jnp.int32, (tokens, tokens), 1))
    parts = [
        jnp.where(visible, scores[:, j * tokens : (j + 1) * tokens], MASKED) for j in range(GROUP)
    ]
    return jnp.concatenate(parts, axis=1)


def kv_spec(tokens):
    return pl.BlockSpec((2, tokens, LANES), lambda i: (0, 0, i))


def attend(queries, key_values, starts, name):
    tokens = queries.shape[0]
    blocks = len(key_values)
    pairs = KEY_VALUE_HEADS // PAIRED
    width = PAIRED * GROUP * HEAD_WIDTH

    def kernel(starts_ref, query_ref, *refs):
        kv_refs, (out_ref, lse_ref) = refs[:blocks], refs[blocks:]
        starts_row = starts_ref[...]
        turned = []
        lse_rows = []
        for pair in range(PAIRED):
            lanes = slice(pair * HEAD_WIDTH, (pair + 1) * HEAD_WIDTH)
            stacked = stacked_heads(query_ref[...], pair) * jnp.asarray(ATTN_SCALE, bf16)
            scores = [
                masked_scores(
                    kv_refs[b][0, :, lanes],
                    stacked,
                    starts_row,
                    (b - blocks + 1) * tokens,
                    b == blocks - 1,
                )
                for b in range(blocks)
            ]
            top = functools.reduce(
                jnp.maximum, [jnp.max(s, axis=0, keepdims=True) for s in scores]
            )
            total = jnp.zeros_like(top)
            mixed = jnp.zeros((HEAD_WIDTH, GROUP * tokens), f32)
            for b in range(blocks):
                weights = jnp.exp(scores[b] - top)
                total = total + jnp.sum(weights, axis=0, keepdims=True)
                mixed = mixed + dot(kv_refs[b][1, :, lanes], weights.astype(bf16), TN)
            mixed = mixed / total
            lse = top + jnp.log(total)
            for j in range(GROUP):
                columns = slice(j * tokens, (j + 1) * tokens)
                turned.append(mixed[:, columns])
                lse_rows.append(lse[:, columns])
        out_ref[...] = jnp.transpose(jnp.concatenate(turned, axis=0)).astype(bf16)
        lse_rows = lse_rows + [jnp.zeros((1, tokens), f32)] * (8 - len(lse_rows))
        lse_ref[0] = jnp.concatenate(lse_rows, axis=0)

    scores_count = QUERY_HEADS * tokens * tokens * blocks
    return pl.pallas_call(
        kernel,
        grid=(pairs,),
        in_specs=[
            whole_block((1, tokens)),
            pl.BlockSpec((tokens, width), lambda i: (0, i)),
        ]
        + [kv_spec(tokens)] * blocks,
        out_specs=[
            pl.BlockSpec((tokens, width), lambda i: (0, i)),
            pl.BlockSpec((1, 8, tokens), lambda i: (i, 0, 0)),
        ],
        out_shape=[
            jax.ShapeDtypeStruct((tokens, QUERY_COLS), bf16),
            jax.ShapeDtypeStruct((pairs, 8, tokens), f32),
        ],
        compiler_params=pltpu.CompilerParams(vmem_limit_bytes=VMEM_BYTES),
        cost_estimate=pl.CostEstimate(
            flops=4 * scores_count * HEAD_WIDTH,
            bytes_accessed=4 * tokens * (QUERY_COLS + blocks * PAIR_COLS),
            transcendentals=scores_count,
        ),
        name=name,
    )(starts, queries, *key_values)


def attend_backward(
    queries, key_values, starts, mixture_grad, lse, cosine, sine, part, parts, name
):
    tokens = queries.shape[0]
    blocks = len(key_values)
    pairs = KEY_VALUE_HEADS // PAIRED // parts
    first = part * pairs
    width = PAIRED * GROUP * HEAD_WIDTH

    def kernel(starts_ref, query_ref, grad_ref, lse_ref, cosine_ref, sine_ref, *refs):
        kv_refs = refs[:blocks]
        dq_ref = refs[blocks]
        dkv_refs = refs[blocks + 1 : 2 * blocks + 1]
        probs_ref, prob_grad_ref = refs[2 * blocks + 1 :]
        starts_row = starts_ref[...]
        turned = []
        for pair in range(PAIRED):
            lanes = slice(pair * HEAD_WIDTH, (pair + 1) * HEAD_WIDTH)
            stacked = stacked_heads(query_ref[...], pair) * jnp.asarray(ATTN_SCALE, bf16)
            incoming = stacked_heads(grad_ref[...], pair)
            lse_row = jnp.concatenate(
                [lse_ref[0, pair * GROUP + j : pair * GROUP + j + 1, :] for j in range(GROUP)],
                axis=1,
            )
            delta = jnp.zeros((1, GROUP * tokens), f32)
            for b in range(blocks):
                scores = masked_scores(
                    kv_refs[b][0, :, lanes],
                    stacked,
                    starts_row,
                    (b - blocks + 1) * tokens,
                    b == blocks - 1,
                )
                probs = jnp.exp(scores - lse_row)
                prob_grad = dot(kv_refs[b][1, :, lanes], incoming, NT)
                delta = delta + jnp.sum(probs * prob_grad, axis=0, keepdims=True)
                probs_ref[b] = probs
                prob_grad_ref[b] = prob_grad
            query_grad = jnp.zeros((HEAD_WIDTH, GROUP * tokens), f32)
            for b in range(blocks):
                probs = probs_ref[b]
                score_grad = (probs * (prob_grad_ref[b] - delta)).astype(bf16)
                query_grad = query_grad + dot(kv_refs[b][0, :, lanes], score_grad, TN)
                key_part = dot(score_grad, stacked)
                value_part = dot(probs.astype(bf16), incoming)
                dkv_refs[b][0, :, lanes] = key_part.astype(dkv_refs[b].dtype)
                dkv_refs[b][1, :, lanes] = value_part.astype(dkv_refs[b].dtype)
            query_grad = query_grad * ATTN_SCALE
            for j in range(GROUP):
                turned.append(query_grad[:, j * tokens : (j + 1) * tokens])
        query_grad = jnp.transpose(jnp.concatenate(turned, axis=0))
        dq_ref[...] = turn(query_grad, cosine_ref[...], sine_ref[...], -1.0).astype(bf16)

    scores_count = QUERY_HEADS // parts * tokens * tokens * blocks
    return pl.pallas_call(
        kernel,
        grid=(pairs,),
        in_specs=[
            whole_block((1, tokens)),
            pl.BlockSpec((tokens, width), lambda i: (0, first + i)),
            pl.BlockSpec((tokens, width), lambda i: (0, first + i)),
            pl.BlockSpec((1, 8, tokens), lambda i: (first + i, 0, 0)),
            whole_block((tokens, LANES)),
            whole_block((tokens, LANES)),
        ]
        + [pl.BlockSpec((2, tokens, LANES), lambda i: (0, 0, first + i))] * blocks,
        out_specs=[pl.BlockSpec((tokens, width), lambda i: (0, i))] + [kv_spec(tokens)] * blocks,
        out_shape=[jax.ShapeDtypeStruct((tokens, QUERY_COLS // parts), bf16)]
        + [jax.ShapeDtypeStruct((2, tokens, PAIR_COLS // parts), bf16)] * (blocks - 1)
        + [jax.ShapeDtypeStruct((2, tokens, PAIR_COLS // parts), f32)],
        scratch_shapes=[pltpu.VMEM((blocks, tokens, GROUP * tokens), f32)] * 2,
        compiler_params=pltpu.CompilerParams(vmem_limit_bytes=VMEM_BYTES),
        cost_estimate=pl.CostEstimate(
            flops=10 * scores_count * HEAD_WIDTH,
            bytes_accessed=4 * tokens * (2 * QUERY_COLS + 2 * blocks * PAIR_COLS),
            transcendentals=scores_count,
        ),
        name=name,
    )(starts, queries, mixture_grad, lse, cosine, sine, *key_values)


def expert_block(index):
    return pl.BlockSpec((MODEL_WIDTH, FF), lambda *_: (0, index), pipeline_mode=pl.Buffered(1))


def experts(order, inputs, grads, scaled, w_small, w_expert, expert, tokens):
    rows = inputs.shape[0]
    wide = MODEL_WIDTH + LANES
    fresh = scaled is None

    def kernel(
        order_ref, expert_ref, input_ref, grad_ref, router_ref, gate_ref, up_ref, down_ref, *refs
    ):
        scaled_ref, hidden_grad_ref, input_grad_ref = refs if fresh else refs[1:]
        block = input_ref[...]
        code = grad_ref[:, MODEL_WIDTH:].astype(f32)
        lane = lax.broadcasted_iota(jnp.int32, (tokens, LANES), 1)
        logits = jnp.where(code > 0.5, dot(block, router_ref[...]), MASKED)
        raised = jnp.exp(logits - jnp.max(logits, axis=1, keepdims=True))
        raised = jnp.where(code > 0.5, raised, 0.0)
        gates = raised / jnp.sum(raised, axis=1, keepdims=True)
        kept = (lane == expert_ref[0]) & (code > 0.5) & (code < 1.5)
        gate = jnp.sum(jnp.where(kept, gates, 0.0), axis=1, keepdims=True)
        gate_part = dot(block, gate_ref[...])
        up_part = dot(block, up_ref[...])
        sigmoid = 1.0 / (1.0 + jnp.exp(-gate_part))
        silu = gate_part * sigmoid
        activation = silu * up_part
        scaled_ref[...] = (activation * gate).astype(bf16)
        pulled = dot(grad_ref[:, :MODEL_WIDTH], down_ref[...])
        gate_grad = RESIDUAL_SCALE * jnp.sum(activation * pulled, axis=1, keepdims=True)
        high = gate_grad.astype(bf16).astype(f32)
        columns = jnp.where(
            lane == expert_ref[0],
            high,
            jnp.where(lane == expert_ref[0] + EXPERTS, gate_grad - high, 0.0),
        )
        input_grad_ref[:, MODEL_WIDTH:] = columns.astype(bf16)
        activation_grad = pulled * (RESIDUAL_SCALE * gate)
        slope = sigmoid * (1.0 + gate_part * (1.0 - sigmoid))
        gate_part_grad = (activation_grad * up_part * slope).astype(bf16)
        up_part_grad = (activation_grad * silu).astype(bf16)
        hidden_grad_ref[:, :FF] = gate_part_grad
        hidden_grad_ref[:, FF:] = up_part_grad
        input_grad_ref[:, :MODEL_WIDTH] = (
            dot(gate_part_grad, gate_ref[...], NT) + dot(up_part_grad, up_ref[...], NT)
        ).astype(bf16)

    in_specs = [
        pl.BlockSpec(memory_space=pltpu.SMEM),
        pl.BlockSpec((tokens, MODEL_WIDTH), lambda i, order_ref: (i, 0)),
        pl.BlockSpec((tokens, wide), lambda i, order_ref: (order_ref[i], 0)),
        pl.BlockSpec(
            (MODEL_WIDTH, LANES),
            lambda *_: (0, 2 * PAIR_COLS // LANES),
            pipeline_mode=pl.Buffered(1),
        ),
        expert_block(0),
        expert_block(1),
        expert_block(2),
    ]
    operands = [order, expert, inputs, grads, w_small, w_expert, w_expert, w_expert]
    if not fresh:
        in_specs.append(pl.BlockSpec(memory_space=pl.ANY))
        operands.append(scaled)
    return pl.pallas_call(
        kernel,
        grid_spec=pltpu.PrefetchScalarGridSpec(
            num_scalar_prefetch=1,
            grid=(rows // tokens,),
            in_specs=in_specs,
            out_specs=[
                pl.BlockSpec((tokens, FF), lambda i, order_ref: (order_ref[i], 0)),
                pl.BlockSpec((tokens, 2 * FF), lambda i, order_ref: (i, 0)),
                pl.BlockSpec((tokens, wide), lambda i, order_ref: (i, 0)),
            ],
        ),
        out_shape=[
            jax.ShapeDtypeStruct((grads.shape[0], FF), bf16),
            jax.ShapeDtypeStruct((rows, 2 * FF), bf16),
            jax.ShapeDtypeStruct((rows, wide), bf16),
        ],
        input_output_aliases={} if fresh else {8: 0},
        compiler_params=params(),
        cost_estimate=cost(
            10 * rows * MODEL_WIDTH * FF,
            2 * MODEL_WIDTH * (3 * rows + EXPERT_COLS),
            rows * FF,
        ),
        name="experts",
    )(*operands)


def expert_shares(scaled, weights, tokens):
    rows = scaled.shape[0]

    def kernel(scaled_ref, weight_ref, out_ref):
        out_ref[...] = dot(scaled_ref[...], weight_ref[...], NT).astype(bf16)

    return pl.pallas_call(
        kernel,
        grid=(rows // (2 * tokens),),
        in_specs=[
            pl.BlockSpec((2 * tokens, FF), lambda i: (i, 0)),
            expert_block(2),
        ],
        out_specs=pl.BlockSpec((2 * tokens, MODEL_WIDTH), lambda i: (i, 0)),
        out_shape=jax.ShapeDtypeStruct((rows, MODEL_WIDTH), bf16),
        compiler_params=params(),
        cost_estimate=cost(
            2 * rows * MODEL_WIDTH * FF, 2 * MODEL_WIDTH * (rows + FF) + 2 * rows * FF,
        ),
        name="expert_shares",
    )(scaled, weights)


def expert_terms(pieces, scale, name):
    width = pieces[0][1].shape[1]
    tile = 384
    rows = sum(left.shape[0] for left, _ in pieces)

    def kernel(*refs):
        total = None
        for k in range(len(pieces)):
            term = dot(refs[2 * k][...], refs[2 * k + 1][...], TN)
            total = term if total is None else total + term
        refs[-1][...] = (scale * total).astype(bf16)

    in_specs = []
    for left, right in pieces:
        in_specs.append(pl.BlockSpec((left.shape[0], tile), lambda i: (0, i)))
        in_specs.append(whole_block(right.shape))
    return pl.pallas_call(
        kernel,
        grid=(MODEL_WIDTH // tile,),
        in_specs=in_specs,
        out_specs=pl.BlockSpec((tile, width), lambda i: (i, 0)),
        out_shape=jax.ShapeDtypeStruct((MODEL_WIDTH, width), bf16),
        compiler_params=params(),
        cost_estimate=cost(
            2 * rows * MODEL_WIDTH * width, 2 * (rows + width) * MODEL_WIDTH + 2 * rows * width
        ),
        name=name,
    )(*[array for piece in pieces for array in piece])


def shards(
    hidden_in,
    out_grad,
    doc_lengths,
    expert_ids,
    attention_norm,
    query_weight,
    key_matrix,
    value_matrix,
    output_weight,
    expert_norm,
    router_weight,
    expert_input,
    expert_output,
):
    tokens = hidden_in.shape[0]
    heads = lax.axis_size("head")
    groups = lax.axis_size("seq")
    own_rows = query_weight.shape[0]
    head_index = lax.axis_index("head")
    seq_index = lax.axis_index("seq")
    shared = EXPERTS // groups
    first_row = (seq_index * heads + head_index) * tokens
    expert = (seq_index * shared + head_index % shared).astype(jnp.int32)[None]

    places = first_row + jnp.arange(tokens)
    starts = doc_start(doc_lengths, places)
    cosine, sine = rope_tables(places - starts)
    starts_row = (starts - first_row).astype(jnp.int32)[None, :]

    hot = (expert_ids[:, :, None] == jnp.arange(EXPERTS)[None, None, :]).astype(f32)
    chosen = jnp.sum(hot, axis=1)
    before = (jnp.arange(tokens)[:, None] > jnp.arange(tokens)[None, :]).astype(bf16)
    earlier = dot(before, chosen.astype(bf16))
    code = jnp.where(chosen > 0.5, jnp.where(earlier < CAP - 0.5, 1.0, 2.0), 0.0)
    code = jnp.concatenate(
        [code.astype(bf16), jnp.zeros((tokens, LANES - EXPERTS), bf16)], axis=1
    )
    coded_grad = jnp.concatenate([out_grad, code], axis=1)

    def spread(block, axes):
        return lax.all_to_all(block, axes, split_axis=0, concat_axis=0, tiled=True)

    clock = Clock()
    small = jnp.concatenate(
        [
            key_matrix,
            value_matrix,
            router_weight,
            attention_norm[:, None],
            expert_norm[:, None],
            jnp.zeros((own_rows, LANES - EXPERTS - 2), bf16),
        ],
        axis=1,
    )
    w_small = lax.all_gather(small, ("head", "seq"), axis=0, tiled=True)

    mine = jnp.concatenate(
        [
            expert_input.reshape(own_rows, groups, shared, 2 * FF),
            expert_output.reshape(own_rows, groups, shared, FF),
        ],
        axis=3,
    )
    mine = jnp.tile(jnp.transpose(mine, (2, 1, 0, 3)), (heads // shared, 1, 1, 1))
    mine = mine.reshape(heads * groups, own_rows, EXPERT_COLS)
    mine_flow = Flow(one_move(mine, functools.partial(spread, axes=("head", "seq"))))
    pending = clock.begin(mine_flow)

    normed, own_kv, gains = enter(hidden_in, w_small, cosine, sine)
    clock.end(pending, own_kv)
    kv_flows = [
        Flow(one_move(own_kv, functools.partial(along_stream, distance=distance)))
        for distance in range(1, heads + 1)
    ]
    w_large = lax.all_gather(
        jnp.concatenate([query_weight, output_weight], axis=1),
        ("head", "seq"),
        axis=0,
        tiled=True,
    )
    far_grads = [Flow(one_move(coded_grad, by_head(step))) for step in range(1, shared)]
    clock.tick(*kv_flows)
    key_values = [flow.value for flow in kv_flows[::-1]] + [own_kv]
    w_expert = mine_flow.value.reshape(MODEL_WIDTH, EXPERT_COLS)
    queries = project_queries(normed, w_large, cosine, sine)
    mixture, lse = attend(queries, key_values, starts_row, "attend")
    middle, normed_two = leave_attention(mixture, w_large, hidden_in, gains)

    input_flows = [Flow(tokens_gather(normed_two))]
    far_tokens = [Flow(one_move(normed_two, by_head(step))) for step in range(1, shared)]
    clock.tick(input_flows[0], *far_tokens)

    input_flows = input_flows + [Flow(tokens_gather(flow.value)) for flow in far_tokens]
    clock.tick(input_flows[0], *far_grads)

    def seq_gather(block):
        return lax.all_gather(block, "seq", axis=0, tiled=True)

    grads = [seq_gather(after(coded_grad, *key_values))] + [
        seq_gather(flow.value) for flow in far_grads
    ]
    core_flows = [Flow(one_move(clock.finish(input_flows[0]), by_seq(1)))]
    clock.tick(core_flows[0], *input_flows[1:])

    back = []
    inputs = {}
    hidden_grads = {}
    scaled = [None] * shared
    turn_of = expert
    blocks = jnp.arange(groups // 2, dtype=jnp.int32) * 2
    for step in range(shared):
        terms = []
        for core in range(2):
            if core == 0:
                inputs[step, 0] = clock.finish(input_flows[step])
                pending = clock.begin(*input_flows[step + 1 :], *back)
            else:
                inputs[step, 1] = clock.finish(core_flows[step])
                if step + 1 < shared:
                    following = clock.finish(input_flows[step + 1])
                    core_flows.append(Flow(one_move(following, by_seq(1))))
                pending = clock.begin(*core_flows[step + 1 :], *back)
            order = (blocks + core) ^ seq_index
            scaled[step], hidden_grads[step, core], input_grad = experts(
                order.astype(jnp.int32),
                inputs[step, core],
                grads[step],
                scaled[step],
                w_small,
                w_expert,
                turn_of,
                tokens,
            )
            turn_of = after(expert, input_grad)
            terms.append(input_grad)
            clock.end(pending, turn_of)
        back.append(Flow(tokens_scatter(*terms)))

    work = [
        lambda first: expert_shares(after(scaled[0], first), w_expert, tokens),
        lambda first: expert_terms(
            [(inputs[key], after(hidden_grads[key], first)) for key in inputs], 1.0, "up_terms"
        ),
        lambda first: expert_terms(
            [(grad, after(part, first)) for grad, part in zip(grads, scaled)],
            RESIDUAL_SCALE,
            "down_terms",
        ),
    ] + [
        functools.partial(
            lambda first, part: expert_shares(after(part, first), w_expert, tokens), part=part
        )
        for part in scaled[1:]
    ]
    made = []
    while not all(flow.done for flow in back):
        pending = clock.begin(*back)
        held = ()
        if len(made) < len(work):
            made.append(work[len(made)](after(turn_of, *clock.last)))
            turn_of = after(expert, made[-1])
            held = (turn_of,)
        clock.end(pending, *held)
    back_parts = [
        Flow(one_move(back[step].value.astype(bf16), by_head(step))) for step in range(1, shared)
    ]
    pending = clock.begin(*back_parts)
    while len(made) < len(work):
        made.append(work[len(made)](after(turn_of, *clock.last)))
        turn_of = after(expert, made[-1])
    clock.end(pending, turn_of)
    up_part, down_part = made[1:3]
    shares = made[:1] + made[3:]
    shares = [lax.psum_scatter(part, "seq", scatter_dimension=0, tiled=True) for part in shares]
    expert_part = jnp.concatenate([up_part, down_part], axis=1)
    expert_part = expert_part.reshape(heads * groups, own_rows, EXPERT_COLS)
    expert_flow = Flow(
        one_move(expert_part, functools.partial(spread, axes=("head", "seq")))
    )
    pending = clock.begin(expert_flow)
    logits_grad, middle_grad, branch_grad, mixture_grad, gain_grad_two = return_to_attention(
        back[0].value,
        [flow.value for flow in back_parts],
        code,
        normed_two,
        middle,
        out_grad,
        w_small,
        w_large,
        gains,
    )

    place = jnp.stack([seq_index // 2, seq_index % 2]).astype(jnp.int32)
    query_grad, *kv_terms = attend_backward(
        queries,
        key_values,
        starts_row,
        mixture_grad,
        lse,
        cosine,
        sine,
        0,
        1,
        "attend_backward",
    )
    query_grads = [query_grad]
    large_part = weight_terms(
        [normed, after(branch_grad, query_grad)], [query_grads, [mixture]]
    )
    clock.end(pending, large_part)
    large_part = lax.psum_scatter(large_part, ("head", "seq"), scatter_dimension=0, tiled=True)
    kv_flows = [
        Flow(one_move(term, functools.partial(along_stream, distance=-distance)))
        for term, distance in zip(kv_terms[:-1], range(heads, 0, -1))
    ]
    clock.tick(*kv_flows)
    terms = [(kv_terms[-1], kv_flows)]
    input_grad, *small_parts = leave(
        place,
        heads,
        groups,
        [[own] + [flow.value for flow in flows] for own, flows in terms],
        query_grads,
        cosine,
        sine,
        after(hidden_in, *shares),
        normed,
        middle_grad,
        normed_two,
        logits_grad,
        gain_grad_two,
        w_small,
        w_large,
        gains,
    )

    small_flow = Flow(rows_scatter(*small_parts))
    share_flows = [
        Flow(one_move(shares[step], by_head(step))) for step in range(1, shared)
    ]
    clock.tick(small_flow)
    clock.tick(small_flow, *share_flows)
    small_flow = Flow(line_scatter(clock.finish(small_flow)))
    clock.finish(small_flow)
    moe_out = shares[0].astype(f32)
    for flow in share_flows:
        moe_out = moe_out + flow.value.astype(f32)
    block_out = (middle + RESIDUAL_SCALE * moe_out).astype(bf16)

    expert_sum = expert_flow.value.reshape(
        heads // shared, shared, groups, own_rows, EXPERT_COLS
    )
    expert_sum = jnp.sum(expert_sum.astype(f32), axis=0)

    def expert_output_of(first, last):
        columns = jnp.transpose(expert_sum[..., first:last], (2, 1, 0, 3))
        return columns.reshape(own_rows, EXPERTS, last - first)

    expert_input_grad = expert_output_of(0, 2 * FF)
    expert_output_grad = expert_output_of(2 * FF, EXPERT_COLS)
    large_sum = large_part.astype(f32)
    query_weight_grad = large_sum[:, :QUERY_COLS]
    output_grad = large_sum[:, QUERY_COLS:]
    small_sum = small_flow.value
    key_grad = small_sum[:, :PAIR_COLS]
    value_grad = small_sum[:, PAIR_COLS : 2 * PAIR_COLS]
    rest = small_sum[:, 2 * PAIR_COLS :]
    router_grad = rest[:, :EXPERTS]
    attention_norm_grad = rest[:, EXPERTS] + rest[:, EXPERTS + 2]
    expert_norm_grad = rest[:, EXPERTS + 1] + rest[:, EXPERTS + 3]
    return (
        block_out,
        input_grad,
        attention_norm_grad,
        query_weight_grad,
        key_grad,
        value_grad,
        output_grad,
        expert_norm_grad,
        router_grad,
        expert_input_grad,
        expert_output_grad,
    )


def solution(mesh):
    return jax.shard_map(
        shards,
        mesh=mesh,
        in_specs=(
            P(("seq", "head"), None),
            P(("seq", "head"), None),
            P(),
            P(("seq", "head"), None),
            P(("head", "seq")),
            P(("head", "seq"), None),
            P(("head", "seq"), None),
            P(("head", "seq"), None),
            P(("head", "seq"), None),
            P(("head", "seq")),
            P(("head", "seq"), None),
            P(("head", "seq"), None, None),
            P(("head", "seq"), None, None),
        ),
        out_specs=(
            P(("seq", "head"), None),
            P(("seq", "head"), None),
            P(("head", "seq")),
            P(("head", "seq"), None),
            P(("head", "seq"), None),
            P(("head", "seq"), None),
            P(("head", "seq"), None),
            P(("head", "seq")),
            P(("head", "seq"), None),
            P(("head", "seq"), None, None),
            P(("head", "seq"), None, None),
        ),
        check_vma=False,
    )
```

time: 2960 us -> 827 us (0.28)
  waiting for transfers between devices: 1860 us -> 446 us
  matrix products: 392 us -> 0.16 us
  local copies, waits for them, and re-layouts: 343 us -> 36.3 us
  Pallas kernels: 0 us -> 198 us
  other arithmetic: 163 us -> 35 us
  blocking collectives: 127 us -> 0 us
  starting transfers between devices: 39.7 us -> 88.8 us
    reduce_scatter x1 -> x3, waiting for transfers between devices: 1390 us -> 0.01 us  [the longest x2 0.01 us: shards(): lax.psum_scatter(part, 'seq', scatter_dimension=0, tiled=True)]
    dot_general x28 -> x1, matrix products: 348 us -> 0.16 us  [dot(): return lax.dot_general(left, right, dims, preferred_element_type=f32)]
    all_gather x6 -> x4, waiting for transfers between devices: 395 us -> 76.2 us  [the longest x1 66 us: shards(): w_small = lax.all_gather(small, ('head', 'seq'), axis=0, tiled=True)]
    ppermute x4 -> x40, waiting for transfers between devices: 0.01 us -> 246 us  [the longest x25 104 us: swap(): return lax.ppermute(block, 'seq', [(i, i ^ mask) for i in range(count)])]
    pallas_call x0 -> x16, Pallas kernels: none -> 198 us  [the longest x4 61.6 us: experts(): pl.pallas_call(kernel, grid_spec=pltpu.PrefetchScalarGridSpec(num_scalar_...]
    reshape x2, local copies, waits for them, and re-layouts: 147 us -> 4.66 us  [the longest x1 2.5 us: shards(): expert_input.reshape(own_rows, groups, shared, 2 * FF)]
    concatenate x4 -> x7, other arithmetic: 115 us -> 9.77 us  [the longest x1 3.92 us: shards(): expert_part = jnp.concatenate([up_part, down_part], axis=1)]
    unnamed x2 -> x0, blocking collectives: 82.5 us -> none
  transfers between devices with their start and end apart: 20 -> 49, of which waited for: 11 -> 29; matrix products, arithmetic and copies ran while one was open for 18% -> 7% of each run, Pallas kernels for 0% -> 24%
where the time goes in v1:
time: 827 us; the launch traced here: 819 us
  waiting for transfers between devices  446 us (54%)
  Pallas kernels  198 us (24%)
  starting transfers between devices  88.8 us (11%)
  local copies, waits for them, and re-layouts  36.3 us (4%)
  other arithmetic  35 us (4%)
  between operations  15.2 us (2%)
    all_to_all x2, waiting for transfers between devices, spread(): return lax.all_to_all(block, axes, split_axis=0, concat_axis=0, tiled=True)  123 us
    ppermute x25, waiting for transfers between devices, swap(): return lax.ppermute(block, 'seq', [(i, i ^ mask) for i in range(count)])  104 us
    ppermute x8, waiting for transfers between devices, along_stream(): return lax.ppermute(block, ('head', 'seq'), route)  95.3 us
    all_gather x1, waiting for transfers between devices, shards(): w_small = lax.all_gather(small, ('head', 'seq'), axis=0, tiled=True)  66 us
    pallas_call x4, Pallas kernels, experts(): pl.pallas_call(kernel, grid_spec=pltpu.PrefetchScalarGridSpec(num_scalar_...  61.6 us
    ppermute x4, waiting for transfers between devices, swap_head(): return lax.ppermute(block, 'head', [(i, i ^ mask) for i in range(count)])  41.9 us
    pallas_call x2, Pallas kernels, expert_terms(): pl.pallas_call(kernel, grid=(MODEL_WIDTH // tile,), in_specs=in_specs, ou...  32.1 us
    ppermute x4, starting transfers between devices, swap_head(): return lax.ppermute(block, 'head', [(i, i ^ mask) for i in range(count)])  28.6 us
  transfers between devices with their start and end apart: 49, of which 29 were waited for; matrix products, arithmetic and copies ran while one was open for 7% of the time, Pallas kernels for 24%

profile of v1, /device:TPU:0, one launch (start us, length us, event | category | flops | bytes accessed | tf_op | source)
XLA Modules:
  0.0 819.4 jit_solution(14032290206910868695)
XLA Ops:
  24.5 7.4 all-to-all-start
  34.5 66.0 %all-gather.5.cloned.1.call-done.weight_ref.router_ref.small_ref = bf16[1536,1152]{1,0:T(8,128)(2,1)} async-done(((bf16[48,1152]{1,0:T(8,128)(2,1)}), bf16[1536,1152]{1,0:T(8,128)(2,1)}) %all-gather.5.cloned.1.call-update) | async-done | bytes 3538960 | tf_op jit(solution)/shard_map/all_gather | solution.py:1115
  104.8 65.8 %all-to-all-done = bf16[32,48,1536]{2,1,0:T(8,128)(2,1)} async-done(((bf16[32,48,1536]{2,1,0:T(8,128)(2,1)}), bf16[32,48,1536]{2,1,0:T(8,128)(2,1)}, u32[]{:S(2)}, u32[]{:S(2)}) %all-to-all-start) | async-done | bytes 4718624 | tf_op jit(solution)/shard_map/all_to_all | solution.py:1101
  182.1 15.1 %collective-permute-done.1.refs_1_ = bf16[2,256,512]{2,1,0:T(8,128)(2,1)S(1)} collective-permute-done((bf16[2,256,512]{2,1,0:T(8,128)(2,1)}, bf16[2,256,512]{2,1,0:T(8,128)(2,1)S(1)}, u32[]{:S(2)}, u32[]{:S(2)}) %collective-permute-start.1) | collective-permute-done | bytes 524320 | tf_op jit(solution)/shard_map/ppermute | solution.py:61
  197.2 19.7 %collective-permute-done.2.refs_2_ = bf16[2,256,512]{2,1,0:T(8,128)(2,1)S(1)} collective-permute-done((bf16[2,256,512]{2,1,0:T(8,128)(2,1)}, bf16[2,256,512]{2,1,0:T(8,128)(2,1)S(1)}, u32[]{:S(2)}, u32[]{:S(2)}) %collective-permute-start.2) | collective-permute-done | bytes 524320 | tf_op jit(solution)/shard_map/ppermute | solution.py:61
  216.9 11.2 %collective-permute-done.3.refs_3_ = bf16[2,256,512]{2,1,0:T(8,128)(2,1)S(1)} collective-permute-done((bf16[2,256,512]{2,1,0:T(8,128)(2,1)}, bf16[2,256,512]{2,1,0:T(8,128)(2,1)S(1)}, u32[]{:S(2)}, u32[]{:S(2)}) %collective-permute-start.3) | collective-permute-done | bytes 524320 | tf_op jit(solution)/shard_map/ppermute | solution.py:61
  228.3 10.1 %all-gather.7.cloned.1.call-done.weight_ref.query_weight_ref = bf16[1536,3072]{1,0:T(8,128)(2,1)} async-done(((bf16[48,3072]{1,0:T(8,128)(2,1)}), bf16[1536,3072]{1,0:T(8,128)(2,1)}) %all-gather.7.cloned.1.call-update) | async-done | bytes 9437200 | tf_op jit(solution)/shard_map/all_gather | solution.py:1135
  244.1 16.2 %attend.1 = (bf16[256,1536]{1,0:T(8,128)(2,1)}, f32[4,8,256]{2,1,0:T(8,128)}) custom-call(s32[1,256]{1,0:T(1,128)} %bitcast.187, bf16[256,1536]{1,0:T(8,128)(2,1)} %project_queries.1.query_ref, bf16[2,256,512]{2,1,0:T(8,128)(2,1)} %copy-done.31, bf16[2,256,512]{2,1,0:T(8,128)(2,1)} %copy-done.32, bf16[2,256,512]{2,1,0:T(8,128)(2,1)} %copy-done.33, ...), custom_call_target="tpu_custom_call" | custom-call | flops 2013265920 | bytes 4194304 | tf_op jit(solution)/shard_map/attend/pallas_call | solution.py:808
  267.5 7.4 collective-permute-start.5
  274.9 17.8 %collective-permute-done.5 = bf16[128,1536]{1,0:T(8,128)(2,1)S(1)} collective-permute-done((bf16[128,1536]{1,0:T(8,128)(2,1)S(1)}, bf16[128,1536]{1,0:T(8,128)(2,1)S(1)}, u32[]{:S(2)}, u32[]{:S(2)}) %collective-permute-start.5) | collective-permute-done | bytes 393248 | tf_op jit(solution)/shard_map/ppermute | solution.py:45
  297.2 17.0 %collective-permute-done.9 = bf16[256,1664]{1,0:T(8,128)(2,1)S(1)} collective-permute-done((bf16[256,1664]{1,0:T(8,128)(2,1)S(1)}, bf16[256,1664]{1,0:T(8,128)(2,1)S(1)}, u32[]{:S(2)}, u32[]{:S(2)}) %collective-permute-start.9) | collective-permute-done | bytes 852000 | tf_op jit(solution)/shard_map/ppermute | solution.py:84
  317.7 23.6 %collective-permute-done.7 = bf16[2,128,1536]{2,1,0:T(8,128)(2,1)S(1)} collective-permute-done((bf16[2,128,1536]{2,1,0:T(8,128)(2,1)}, bf16[2,128,1536]{2,1,0:T(8,128)(2,1)S(1)}, u32[]{:S(2)}, u32[]{:S(2)}) %collective-permute-start.7) | collective-permute-done | bytes 786464 | tf_op jit(solution)/shard_map/ppermute | solution.py:45
  346.3 16.2 %collective-permute-done.12 = bf16[128,1536]{1,0:T(8,128)(2,1)S(1)} collective-permute-done((bf16[128,1536]{1,0:T(8,128)(2,1)S(1)}, bf16[128,1536]{1,0:T(8,128)(2,1)S(1)}, u32[]{:S(2)}, u32[]{:S(2)}) %collective-permute-start.12) | collective-permute-done | bytes 393248 | tf_op jit(solution)/shard_map/ppermute | solution.py:45
  370.9 15.4 %experts.4 = (bf16[2048,512]{1,0:T(8,128)(2,1)}, bf16[1024,1024]{1,0:T(8,128)(2,1)}, bf16[1024,1664]{1,0:T(8,128)(2,1)}) custom-call(s32[4]{0:T(128)} %fusion.27.order_ref, s32[1]{0:T(128)} %bitcast.6.expert_ref, bf16[1024,1536]{1,0:T(8,128)(2,1)} %bitcast.176, bf16[2048,1664]{1,0:T(8,128)(2,1)} %all-gather.9.cloned.1.call-done.grad_ref.refs_0_, ...), custom_call_target="tpu_custom_call" | custom-call | flops 8053063680 | bytes 14155776 | tf_op jit(solution)/shard_map/experts/pallas_call | solution.py:979
  393.4 15.1 %experts.5 = (bf16[2048,512]{1,0:T(8,128)(2,1)}, bf16[1024,1024]{1,0:T(8,128)(2,1)}, bf16[1024,1664]{1,0:T(8,128)(2,1)}) custom-call(s32[4]{0:T(128)} %add_xor_fusion.order_ref, s32[1]{0:T(128)} %bitcast.6.expert_ref, bf16[1024,1536]{1,0:T(8,128)(2,1)} %copy-done.28, ...), custom_call_target="tpu_custom_call", output_to_operand_aliasing={{0}: (8, {})} | custom-call | flops 8053063680 | bytes 14155776 | tf_op jit(solution)/shard_map/experts/pallas_call | solution.py:979
  410.6 15.5 %experts.6 = (bf16[2048,512]{1,0:T(8,128)(2,1)}, bf16[1024,1024]{1,0:T(8,128)(2,1)}, bf16[1024,1664]{1,0:T(8,128)(2,1)}) custom-call(s32[4]{0:T(128)} %fusion.27.order_ref, s32[1]{0:T(128)} %bitcast.6.expert_ref, bf16[1024,1536]{1,0:T(8,128)(2,1)} %bitcast.179, bf16[2048,1664]{1,0:T(8,128)(2,1)} %all-gather.11.cloned.1.call-done.grad_ref.refs_2_, ...), custom_call_target="tpu_custom_call" | custom-call | flops 8053063680 | bytes 14155776 | tf_op jit(solution)/shard_map/experts/pallas_call | solution.py:979
  433.0 7.4 expert_shares.2
  440.9 15.7 %experts.7 = (bf16[2048,512]{1,0:T(8,128)(2,1)}, bf16[1024,1024]{1,0:T(8,128)(2,1)}, bf16[1024,1664]{1,0:T(8,128)(2,1)}) custom-call(s32[4]{0:T(128)} %add_xor_fusion.order_ref, s32[1]{0:T(128)} %bitcast.6.expert_ref, bf16[1024,1536]{1,0:T(8,128)(2,1)} %copy-done.29, ...), custom_call_target="tpu_custom_call", output_to_operand_aliasing={{0}: (8, {})} | custom-call | flops 8053063680 | bytes 14155776 | tf_op jit(solution)/shard_map/experts/pallas_call | solution.py:979
  460.4 18.2 %collective-permute-done.19 = bf16[128,1664]{1,0:T(8,128)(2,1)S(1)} collective-permute-done((bf16[128,1664]{1,0:T(8,128)(2,1)S(1)}, bf16[128,1664]{1,0:T(8,128)(2,1)S(1)}, u32[]{:S(2)}, u32[]{:S(2)}) %collective-permute-start.19) | collective-permute-done | bytes 426016 | tf_op jit(solution)/shard_map/ppermute | solution.py:45
  483.0 19.5 %up_terms.1 = bf16[1536,1024]{1,0:T(8,128)(2,1)} custom-call(bf16[1024,1536]{1,0:T(8,128)(2,1)} %bitcast.177, bf16[1024,1024]{1,0:T(8,128)(2,1)} %get-tuple-element.172.refs_1_, bf16[1024,1536]{1,0:T(8,128)(2,1)} %copy-done.28, bf16[1024,1024]{1,0:T(8,128)(2,1)} %get-tuple-element.174.refs_3_, bf16[1024,1536]{1,0:T(8,128)(2,1)} %bitcast.180, ...), custom_call_target="tpu_custom_call" | custom-call | flops 12884901888 | bytes 24117248 | tf_op jit(solution)/shard_map/up_terms/pallas_call | solution.py:1046
  502.5 8.2 collective-permute-done.22
  513.5 7.5 expert_shares.3
  525.7 12.5 %down_terms.1 = bf16[1536,512]{1,0:T(8,128)(2,1)} custom-call(bf16[2048,1664]{1,0:T(8,128)(2,1)} %all-gather.9.cloned.1.call-done.grad_ref.refs_0_, bf16[2048,512]{1,0:T(8,128)(2,1)} %get-tuple-element.199.scaled_ref.refs_1_, bf16[2048,1664]{1,0:T(8,128)(2,1)} %all-gather.11.cloned.1.call-done.grad_ref.refs_2_, ...), custom_call_target="tpu_custom_call" | custom-call | flops 6442450944 | bytes 18350080 | tf_op jit(solution)/shard_map/down_terms/pallas_call | solution.py:1046
  551.2 7.9 return_to_attention.1
  559.1 27.7 %attend_backward.1 = (bf16[256,1536]{1,0:T(8,128)(2,1)}, bf16[2,256,512]{2,1,0:T(8,128)(2,1)}, bf16[2,256,512]{2,1,0:T(8,128)(2,1)}, bf16[2,256,512]{2,1,0:T(8,1...) custom-call(s32[1,256]{1,0:T(1,128)} %bitcast.188, bf16[256,1536]{1,0:T(8,128)(2,1)} %project_queries.1.query_ref, ...), custom_call_target="tpu_custom_call" | custom-call | flops 5033164800 | bytes 8388608 | tf_op jit(solution)/shard_map/attend_backward/pallas_call | solution.py:888
  586.8 9.7 %weight_terms.1 = bf16[1536,3072]{1,0:T(8,128)(2,1)} custom-call(bf16[256,1536]{1,0:T(8,128)(2,1)} %get-tuple-element.116.normed_ref.refs_0_, bf16[256,1536]{1,0:T(8,128)(2,1)} %get-tuple-element.192.refs_1_.refs_0_, bf16[256,1536]{1,0:T(8,128)(2,1)} %get-tuple-element.203.refs_2_, bf16[256,1536]{1,0:T(8,128)(2,1)} %get-tuple-element.123.mixture_ref.refs_3_), custom_call_target="tpu_custom_call" | custom-call | flops 2415919104 | bytes 11010048 | tf_op jit(solution)/shard_map/weight_terms/pallas_call | solution.py:577
  596.6 57.6 %all-to-all-done.1 = bf16[32,48,1536]{2,1,0:T(8,128)(2,1)} async-done(((bf16[32,48,1536]{2,1,0:T(8,128)(2,1)}), bf16[32,48,1536]{2,1,0:T(8,128)(2,1)}, u32[]{:S(2)}, u32[]{:S(2)}) %all-to-all-start.1) | async-done | bytes 4718624 | tf_op jit(solution)/shard_map/all_to_all | solution.py:1101
  660.2 14.0 %collective-permute-done.28.refs_3_ = bf16[2,256,512]{2,1,0:T(8,128)(2,1)S(1)} collective-permute-done((bf16[2,256,512]{2,1,0:T(8,128)(2,1)}, bf16[2,256,512]{2,1,0:T(8,128)(2,1)S(1)}, u32[]{:S(2)}, u32[]{:S(2)}) %collective-permute-start.28) | collective-permute-done | bytes 524320 | tf_op jit(solution)/shard_map/ppermute | solution.py:61
  674.2 35.4 %collective-permute-done.29.refs_4_ = bf16[2,256,512]{2,1,0:T(8,128)(2,1)S(1)} collective-permute-done((bf16[2,256,512]{2,1,0:T(8,128)(2,1)S(1)}, bf16[2,256,512]{2,1,0:T(8,128)(2,1)S(1)}, u32[]{:S(2)}, u32[]{:S(2)}) %collective-permute-start.29) | collective-permute-done | bytes 524320 | tf_op jit(solution)/shard_map/ppermute | solution.py:61
  710.6 12.7 %leave.1 = (f32[256,1536]{1,0:T(8,128)}, bf16[4,4,48,1152]{3,2,1,0:T(8,128)(2,1)}, bf16[4,4,48,1152]{3,2,1,0:T(8,128)(2,1)}) custom-call(s32[2]{0:T(128)} %pad_add_fusion.place_ref, f32[256,128]{1,0:T(8,128)} %get-tuple-element.323.cosine_ref, f32[256,128]{1,0:T(8,128)} %get-tuple-element.324.sine_ref, bf16[256,1536]{1,0:T(8,128)(2,1)} %hidden_ref.4, ...), custom_call_target="tpu_custom_call" | custom-call | flops 2818572288 | bytes 18087936 | tf_op jit(solution)/shard_map/leave/pallas_call | solution.py:683
  739.2 25.3 %collective-permute-start.32 = (bf16[256,1536]{1,0:T(8,128)(2,1)S(1)}, bf16[256,1536]{1,0:T(8,128)(2,1)S(1)}, u32[]{:S(2)}, u32[]{:S(2)}) collective-permute-start(bf16[256,1536]{1,0:T(8,128)(2,1)S(1)} %copy-done.30), channel_id=1, source_target_pairs={{0,8},{8,0},{16,24},{24,16},{1,9},{9,1},{17,25},{25,17},{2,10},{10... | collective-permute-start | bytes 2359304 | tf_op jit(solution)/shard_map/ppermute | solution.py:84
  764.9 22.8 %collective-permute-done.32 = bf16[256,1536]{1,0:T(8,128)(2,1)S(1)} collective-permute-done((bf16[256,1536]{1,0:T(8,128)(2,1)S(1)}, bf16[256,1536]{1,0:T(8,128)(2,1)S(1)}, u32[]{:S(2)}, u32[]{:S(2)}) %collective-permute-start.32) | collective-permute-done | bytes 786464 | tf_op jit(solution)/shard_map/ppermute | solution.py:84
  (248 shorter events, 162.8 us)
Async XLA Ops:
  7.2 93.4 %all-gather.5.cloned.1.call-start = ((), (), s32[]{:S(2)}) async-start(), calls=%async_computation.5 | async-start | bytes 3649536 | tf_op jit(solution)/shard_map/all_gather | solution.py:1115
  11.1 227.3 %all-gather.7.cloned.1.call-start = ((), (), s32[]{:S(2)}) async-start(), calls=%async_computation.6 | async-start | bytes 9732096 | tf_op jit(solution)/shard_map/all_gather | solution.py:1135
  24.5 146.1 %all-to-all-start = ((bf16[32,48,1536]{2,1,0:T(8,128)(2,1)}), bf16[32,48,1536]{2,1,0:T(8,128)(2,1)}, u32[]{:S(2)}, u32[]{:S(2)}) async-start(bf16[32,48,1536]{2,1,0:T(8,128)(2,1)} %bitcast.161), calls=%async_computation | async-start | bytes 9437184 | tf_op jit(solution)/shard_map/all_to_all | solution.py:1101
  32.0 338.9 %all-gather.9.cloned.1.call-start = ((), (), s32[]{:S(2)}) async-start(), calls=%async_computation.7 | async-start | bytes 7667712 | tf_op jit(solution)/shard_map/all_gather | solution.py:1157
  172.2 25.0 %collective-permute-start.1 = (bf16[2,256,512]{2,1,0:T(8,128)(2,1)}, bf16[2,256,512]{2,1,0:T(8,128)(2,1)S(1)}, u32[]{:S(2)}, u32[]{:S(2)}) collective-permute-start(bf16[2,256,512]{2,1,0:T(8,128)(2,1)} %get-tuple-element.122.refs_4_), channel_id=1, source_target_pairs={{0,24},{8,1},{16,9},{24,17},{1,25},{9,2},{17,10},{25,18},{2,26},{1... | collective-permute-start | bytes 1572872 | tf_op jit(solution)/shard_map/ppermute | solution.py:61
  176.2 40.6 %collective-permute-start.2 = (bf16[2,256,512]{2,1,0:T(8,128)(2,1)}, bf16[2,256,512]{2,1,0:T(8,128)(2,1)S(1)}, u32[]{:S(2)}, u32[]{:S(2)}) collective-permute-start(bf16[2,256,512]{2,1,0:T(8,128)(2,1)} %get-tuple-element.122.refs_4_), channel_id=1, source_target_pairs={{0,16},{8,24},{16,1},{24,9},{1,17},{9,25},{17,2},{25,10},{2,18},{1... | collective-permute-start | bytes 1572872 | tf_op jit(solution)/shard_map/ppermute | solution.py:61
  177.5 50.5 %collective-permute-start.3 = (bf16[2,256,512]{2,1,0:T(8,128)(2,1)}, bf16[2,256,512]{2,1,0:T(8,128)(2,1)S(1)}, u32[]{:S(2)}, u32[]{:S(2)}) collective-permute-start(bf16[2,256,512]{2,1,0:T(8,128)(2,1)} %get-tuple-element.122.refs_4_), channel_id=1, source_target_pairs={{0,8},{8,16},{16,24},{24,1},{1,9},{9,17},{17,25},{25,2},{2,10},{10... | collective-permute-start | bytes 1572872 | tf_op jit(solution)/shard_map/ppermute | solution.py:61
  228.0 182.6 %all-gather.11.cloned.1.call-start = ((), (), s32[]{:S(2)}) async-start(), calls=%async_computation.9 | async-start | bytes 7667712 | tf_op jit(solution)/shard_map/all_gather | solution.py:1157
  267.5 25.2 %collective-permute-start.5 = (bf16[128,1536]{1,0:T(8,128)(2,1)S(1)}, bf16[128,1536]{1,0:T(8,128)(2,1)S(1)}, u32[]{:S(2)}, u32[]{:S(2)}) collective-permute-start(bf16[128,1536]{1,0:T(8,128)(2,1)S(1)} %get-tuple-element.128), channel_id=1, source_target_pairs={{0,4},{1,5},{2,6},{3,7},{4,0},{5,1},{6,2},{7,3},{8,12},{9,13},{10,... | collective-permute-start | bytes 1179656 | tf_op jit(solution)/shard_map/ppermute | solution.py:45
  274.9 20.6 %collective-permute-start.6 = (bf16[256,1536]{1,0:T(8,128)(2,1)}, bf16[256,1536]{1,0:T(8,128)(2,1)S(1)}, u32[]{:S(2)}, u32[]{:S(2)}) collective-permute-start(bf16[256,1536]{1,0:T(8,128)(2,1)} %get-tuple-element.129.normed_ref.normed_two_ref), channel_id=1, source_target_pairs={{0,8},{8,0},{16,24},{24,16},{1,9},{9,1},{17,25},{25,17},{2,10},{10... | collective-permute-start | bytes 2359304 | tf_op jit(solution)/shard_map/ppermute | solution.py:84
  274.9 19.6 %collective-permute-start.4 = (bf16[128,1536]{1,0:T(8,128)(2,1)S(1)}, bf16[128,1536]{1,0:T(8,128)(2,1)S(1)}, u32[]{:S(2)}, u32[]{:S(2)}) collective-permute-start(bf16[128,1536]{1,0:T(8,128)(2,1)S(1)} %get-tuple-element.127), channel_id=1, source_target_pairs={{0,2},{1,3},{2,0},{3,1},{4,6},{5,7},{6,4},{7,5},{8,10},{9,11},{10,... | collective-permute-start | bytes 1179656 | tf_op jit(solution)/shard_map/ppermute | solution.py:45
  315.2 345.0 %reduce-scatter.4.cloned.1.call-start = ((), (), s32[]{:S(2)}) async-start(), calls=%async_computation.8 | async-start | bytes 7077888 | tf_op jit(solution)/shard_map/reduce_scatter | solution.py:1234
  315.4 25.9 %collective-permute-start.7 = (bf16[2,128,1536]{2,1,0:T(8,128)(2,1)}, bf16[2,128,1536]{2,1,0:T(8,128)(2,1)S(1)}, u32[]{:S(2)}, u32[]{:S(2)}) collective-permute-start(bf16[2,128,1536]{2,1,0:T(8,128)(2,1)} %get-tuple-element.130), channel_id=1, source_target_pairs={{0,4},{1,5},{2,6},{3,7},{4,0},{5,1},{6,2},{7,3},{8,12},{9,13},{10,... | collective-permute-start | bytes 2359304 | tf_op jit(solution)/shard_map/ppermute | solution.py:45
  316.9 25.8 %collective-permute-start.8 = (bf16[2,128,1536]{2,1,0:T(8,128)(2,1)}, bf16[2,128,1536]{2,1,0:T(8,128)(2,1)S(1)}, u32[]{:S(2)}, u32[]{:S(2)}) collective-permute-start(bf16[2,128,1536]{2,1,0:T(8,128)(2,1)} %get-tuple-element.131), channel_id=1, source_target_pairs={{0,2},{1,3},{2,0},{3,1},{4,6},{5,7},{6,4},{7,5},{8,10},{9,11},{10,... | collective-permute-start | bytes 2359304 | tf_op jit(solution)/shard_map/ppermute | solution.py:45
  343.1 22.3 %collective-permute-start.10 = (bf16[1024,1536]{1,0:T(8,128)(2,1)S(1)}, bf16[1024,1536]{1,0:T(8,128)(2,1)S(1)}, u32[]{:S(2)}, u32[]{:S(2)}) collective-permute-start(bf16[1024,1536]{1,0:T(8,128)(2,1)S(1)} %bitcast.175), channel_id=1, source_target_pairs={{0,1},{1,0},{2,3},{3,2},{4,5},{5,4},{6,7},{7,6},{8,9},{9,8},{10,11... | collective-permute-start | bytes 9437192 | tf_op jit(solution)/shard_map/ppermute | solution.py:45
  344.6 19.6 %collective-permute-start.11 = (bf16[128,1536]{1,0:T(8,128)(2,1)S(1)}, bf16[128,1536]{1,0:T(8,128)(2,1)S(1)}, u32[]{:S(2)}, u32[]{:S(2)}) collective-permute-start(bf16[128,1536]{1,0:T(8,128)(2,1)S(1)} %get-tuple-element.141), channel_id=1, source_target_pairs={{0,2},{1,3},{2,0},{3,1},{4,6},{5,7},{6,4},{7,5},{8,10},{9,11},{10,... | collective-permute-start | bytes 1179656 | tf_op jit(solution)/shard_map/ppermute | solution.py:45
  367.1 22.8 %collective-permute-start.13 = (bf16[2,128,1536]{2,1,0:T(8,128)(2,1)}, bf16[2,128,1536]{2,1,0:T(8,128)(2,1)}, u32[]{:S(2)}, u32[]{:S(2)}) collective-permute-start(bf16[2,128,1536]{2,1,0:T(8,128)(2,1)} %get-tuple-element.143), channel_id=1, source_target_pairs={{0,4},{1,5},{2,6},{3,7},{4,0},{5,1},{6,2},{7,3},{8,12},{9,13},{10,... | collective-permute-start | bytes 2359304 | tf_op jit(solution)/shard_map/ppermute | solution.py:45
  368.6 22.3 %collective-permute-start.14 = (bf16[2,128,1536]{2,1,0:T(8,128)(2,1)}, bf16[2,128,1536]{2,1,0:T(8,128)(2,1)}, u32[]{:S(2)}, u32[]{:S(2)}) collective-permute-start(bf16[2,128,1536]{2,1,0:T(8,128)(2,1)} %get-tuple-element.144), channel_id=1, source_target_pairs={{0,2},{1,3},{2,0},{3,1},{4,6},{5,7},{6,4},{7,5},{8,10},{9,11},{10,... | collective-permute-start | bytes 2359304 | tf_op jit(solution)/shard_map/ppermute | solution.py:45
  430.9 25.7 %collective-permute-start.17 = (bf16[2,128,1664]{2,1,0:T(8,128)(2,1)}, bf16[2,128,1664]{2,1,0:T(8,128)(2,1)}, u32[]{:S(2)}, u32[]{:S(2)}) collective-permute-start(bf16[2,128,1664]{2,1,0:T(8,128)(2,1)} %slice_bitcast_fusion.8), channel_id=1, source_target_pairs={{0,2},{1,3},{2,0},{3,1},{4,6},{5,7},{6,4},{7,5},{8,10},{9,11},{10,... | collective-permute-start | bytes 2555912 | tf_op jit(solution)/shard_map/ppermute | solution.py:45
  431.4 25.1 %collective-permute-start.18 = (bf16[2,128,1664]{2,1,0:T(8,128)(2,1)}, bf16[2,128,1664]{2,1,0:T(8,128)(2,1)}, u32[]{:S(2)}, u32[]{:S(2)}) collective-permute-start(bf16[2,128,1664]{2,1,0:T(8,128)(2,1)} %slice_bitcast_fusion.7), channel_id=1, source_target_pairs={{0,4},{1,5},{2,6},{3,7},{4,0},{5,1},{6,2},{7,3},{8,12},{9,13},{10,... | collective-permute-start | bytes 2555912 | tf_op jit(solution)/shard_map/ppermute | solution.py:45
  440.4 219.8 %reduce-scatter.6.cloned.1.call-start = ((), (), s32[]{:S(2)}) async-start(), calls=%async_computation.10 | async-start | bytes 7077888 | tf_op jit(solution)/shard_map/reduce_scatter | solution.py:1234
  459.0 19.6 %collective-permute-start.21 = (bf16[1024,1664]{1,0:T(8,128)(2,1)S(1)}, bf16[1024,1664]{1,0:T(8,128)(2,1)S(1)}, u32[]{:S(2)}, u32[]{:S(2)}) collective-permute-start(bf16[1024,1664]{1,0:T(8,128)(2,1)S(1)} %copy-done.27), channel_id=1, source_target_pairs={{0,1},{1,0},{2,3},{3,2},{4,5},{5,4},{6,7},{7,6},{8,9},{9,8},{10,11... | collective-permute-start | bytes 10223624 | tf_op jit(solution)/shard_map/ppermute | solution.py:45
  480.5 30.2 %collective-permute-start.22 = (bf16[2,128,1664]{2,1,0:T(8,128)(2,1)S(1)}, bf16[2,128,1664]{2,1,0:T(8,128)(2,1)S(1)}, u32[]{:S(2)}, u32[]{:S(2)}) collective-permute-start(bf16[2,128,1664]{2,1,0:T(8,128)(2,1)S(1)} %slice_bitcast_fusion.4), channel_id=1, source_target_pairs={{0,2},{1,3},{2,0},{3,1},{4,6},{5,7},{6,4},{7,5},{8,10},{9,11},{10,... | collective-permute-start | bytes 2555912 | tf_op jit(solution)/shard_map/ppermute | solution.py:45
  482.8 28.3 %collective-permute-start.23 = (bf16[2,128,1664]{2,1,0:T(8,128)(2,1)S(1)}, bf16[2,128,1664]{2,1,0:T(8,128)(2,1)S(1)}, u32[]{:S(2)}, u32[]{:S(2)}) collective-permute-start(bf16[2,128,1664]{2,1,0:T(8,128)(2,1)S(1)} %slice_bitcast_fusion.3), channel_id=1, source_target_pairs={{0,4},{1,5},{2,6},{3,7},{4,0},{5,1},{6,2},{7,3},{8,12},{9,13},{10,... | collective-permute-start | bytes 2555912 | tf_op jit(solution)/shard_map/ppermute | solution.py:45
  524.2 20.0 %collective-permute-start.26 = (bf16[256,1664]{1,0:T(8,128)(2,1)S(1)}, bf16[256,1664]{1,0:T(8,128)(2,1)S(1)}, u32[]{:S(2)}, u32[]{:S(2)}) collective-permute-start(bf16[256,1664]{1,0:T(8,128)(2,1)S(1)} %pad_maximum_fusion.2), channel_id=1, source_target_pairs={{0,8},{8,0},{16,24},{24,16},{1,9},{9,1},{17,25},{25,17},{2,10},{10... | collective-permute-start | bytes 2555912 | tf_op jit(solution)/shard_map/ppermute | solution.py:84
  545.1 109.1 %all-to-all-start.1 = ((bf16[32,48,1536]{2,1,0:T(8,128)(2,1)}), bf16[32,48,1536]{2,1,0:T(8,128)(2,1)}, u32[]{:S(2)}, u32[]{:S(2)}) async-start(bf16[32,48,1536]{2,1,0:T(8,128)(2,1)} %bitcast.162), calls=%async_computation.3 | async-start | bytes 9437184 | tf_op jit(solution)/shard_map/all_to_all | solution.py:1101
  548.8 261.7 %reduce-scatter.8.cloned.1.call-start = ((), (), s32[]{:S(2)}) async-start(), calls=%async_computation.11 | async-start | bytes 9732096 | tf_op jit(solution)/shard_map/reduce_scatter | solution.py:1271
  656.8 52.8 %collective-permute-start.29 = (bf16[2,256,512]{2,1,0:T(8,128)(2,1)S(1)}, bf16[2,256,512]{2,1,0:T(8,128)(2,1)S(1)}, u32[]{:S(2)}, u32[]{:S(2)}) collective-permute-start(bf16[2,256,512]{2,1,0:T(8,128)(2,1)S(1)} %copy-done.36), channel_id=1, source_target_pairs={{16,0},{24,8},{1,16},{9,24},{17,1},{25,9},{2,17},{10,25},{18,2},{2... | collective-permute-start | bytes 1572872 | tf_op jit(solution)/shard_map/ppermute | solution.py:61
  658.1 51.5 %collective-permute-start.30 = (bf16[2,256,512]{2,1,0:T(8,128)(2,1)S(1)}, bf16[2,256,512]{2,1,0:T(8,128)(2,1)S(1)}, u32[]{:S(2)}, u32[]{:S(2)}) collective-permute-start(bf16[2,256,512]{2,1,0:T(8,128)(2,1)S(1)} %copy-done.35), channel_id=1, source_target_pairs={{8,0},{16,8},{24,16},{1,24},{9,1},{17,9},{25,17},{2,25},{10,2},{18... | collective-permute-start | bytes 1572872 | tf_op jit(solution)/shard_map/ppermute | solution.py:61
  730.4 34.2 %collective-permute-start.33 = (bf16[2,2,48,1152]{3,2,1,0:T(8,128)(2,1)S(1)}, bf16[2,2,48,1152]{3,2,1,0:T(8,128)(2,1)S(1)}, u32[]{:S(2)}, u32[]{:S(2)}) collective-permute-start(bf16[2,2,48,1152]{3,2,1,0:T(8,128)(2,1)S(1)} %slice_bitcast_fusion.13), channel_id=1, source_target_pairs={{0,2},{1,3},{2,0},{3,1},{4,6},{5,7},{6,4},{7,5},{8,10},{9,11},{10,... | collective-permute-start | bytes 1327112 | tf_op jit(solution)/shard_map/ppermute | solution.py:45
  738.6 26.1 %collective-permute-start.34 = (bf16[2,2,48,1152]{3,2,1,0:T(8,128)(2,1)S(1)}, bf16[2,2,48,1152]{3,2,1,0:T(8,128)(2,1)S(1)}, u32[]{:S(2)}, u32[]{:S(2)}) collective-permute-start(bf16[2,2,48,1152]{3,2,1,0:T(8,128)(2,1)S(1)} %slice_bitcast_fusion.12), channel_id=1, source_target_pairs={{0,4},{1,5},{2,6},{3,7},{4,0},{5,1},{6,2},{7,3},{8,12},{9,13},{10,... | collective-permute-start | bytes 1327112 | tf_op jit(solution)/shard_map/ppermute | solution.py:45
  739.2 48.5 %collective-permute-start.32 = (bf16[256,1536]{1,0:T(8,128)(2,1)S(1)}, bf16[256,1536]{1,0:T(8,128)(2,1)S(1)}, u32[]{:S(2)}, u32[]{:S(2)}) collective-permute-start(bf16[256,1536]{1,0:T(8,128)(2,1)S(1)} %copy-done.30), channel_id=1, source_target_pairs={{0,8},{8,0},{16,24},{24,16},{1,9},{9,1},{17,25},{25,17},{2,10},{10... | collective-permute-start | bytes 2359304 | tf_op jit(solution)/shard_map/ppermute | solution.py:84
  (54 other events, 1148.0 us)
Sparse Core Ops, SparseCore 0:
  11.5 89.0 all-gather.4
  104.0 134.3 all-gather.6
  240.9 55.7 all-gather.8
  315.3 63.0 all-gather.10
  440.5 77.2 reduce-scatter.3
  521.4 103.5 reduce-scatter.5
  630.9 164.5 reduce-scatter.7

commit v2 on v1

--- a/solution.py
+++ b/solution.py
@@ -916,7 +916,7 @@
     return pl.BlockSpec((MODEL_WIDTH, FF), lambda *_: (0, index), pipeline_mode=pl.Buffered(1))
 
 
-def experts(order, inputs, grads, scaled, w_small, w_expert, expert, tokens):
+def experts(order, inputs, grads, scaled, w_small, w_up, w_down, expert, tokens):
     rows = inputs.shape[0]
     wide = MODEL_WIDTH + LANES
     fresh = scaled is None
@@ -970,9 +970,9 @@
         ),
         expert_block(0),
         expert_block(1),
-        expert_block(2),
+        expert_block(0),
     ]
-    operands = [order, expert, inputs, grads, w_small, w_expert, w_expert, w_expert]
+    operands = [order, expert, inputs, grads, w_small, w_up, w_up, w_down]
     if not fresh:
         in_specs.append(pl.BlockSpec(memory_space=pl.ANY))
         operands.append(scaled)
@@ -1004,27 +1004,30 @@
     )(*operands)
 
 
-def expert_shares(scaled, weights, tokens):
-    rows = scaled.shape[0]
-
-    def kernel(scaled_ref, weight_ref, out_ref):
-        out_ref[...] = dot(scaled_ref[...], weight_ref[...], NT).astype(bf16)
-
+def expert_shares(scaled, weights, tokens, groups):
+    count = len(scaled)
+
+    def kernel(*refs):
+        weight_ref, out_ref = refs[count:]
+        for k in range(count):
+
+            @pl.when(pl.program_id(1) == k)
+            def _():
+                out_ref[...] = dot(refs[k][...], weight_ref[...], NT).astype(bf16)
+
+    rows = groups * count * tokens
     return pl.pallas_call(
         kernel,
-        grid=(rows // (2 * tokens),),
-        in_specs=[
-            pl.BlockSpec((2 * tokens, FF), lambda i: (i, 0)),
-            expert_block(2),
-        ],
-        out_specs=pl.BlockSpec((2 * tokens, MODEL_WIDTH), lambda i: (i, 0)),
+        grid=(groups, count),
+        in_specs=[pl.BlockSpec((tokens, FF), lambda i, k: (i, 0))] * count + [expert_block(0)],
+        out_specs=pl.BlockSpec((tokens, MODEL_WIDTH), lambda i, k: (i * count + k, 0)),
         out_shape=jax.ShapeDtypeStruct((rows, MODEL_WIDTH), bf16),
         compiler_params=params(),
         cost_estimate=cost(
-            2 * rows * MODEL_WIDTH * FF, 2 * MODEL_WIDTH * (rows + FF) + 2 * rows * FF,
+            2 * rows * MODEL_WIDTH * FF, 2 * MODEL_WIDTH * (rows + FF) + 2 * rows * FF
         ),
         name="expert_shares",
-    )(scaled, weights)
+    )(*scaled, weights)
 
 
 def expert_terms(pieces, scale, name):
@@ -1114,17 +1117,19 @@
     )
     w_small = lax.all_gather(small, ("head", "seq"), axis=0, tiled=True)
 
-    mine = jnp.concatenate(
-        [
-            expert_input.reshape(own_rows, groups, shared, 2 * FF),
-            expert_output.reshape(own_rows, groups, shared, FF),
-        ],
-        axis=3,
-    )
-    mine = jnp.tile(jnp.transpose(mine, (2, 1, 0, 3)), (heads // shared, 1, 1, 1))
-    mine = mine.reshape(heads * groups, own_rows, EXPERT_COLS)
-    mine_flow = Flow(one_move(mine, functools.partial(spread, axes=("head", "seq"))))
-    pending = clock.begin(mine_flow)
+    def expert_rows(weight):
+        weight = weight.reshape(own_rows, groups, shared, weight.shape[2])
+        weight = jnp.tile(jnp.transpose(weight, (2, 1, 0, 3)), (heads // shared, 1, 1, 1))
+        return Flow(
+            one_move(
+                weight.reshape(heads * groups, own_rows, weight.shape[3]),
+                functools.partial(spread, axes=("head", "seq")),
+            )
+        )
+
+    up_flow = expert_rows(expert_input)
+    far_grads = [Flow(one_move(coded_grad, by_head(step))) for step in range(1, shared)]
+    pending = clock.begin(up_flow, *far_grads)
 
     normed, own_kv, gains = enter(hidden_in, w_small, cosine, sine)
     clock.end(pending, own_kv)
@@ -1138,27 +1143,28 @@
         axis=0,
         tiled=True,
     )
-    far_grads = [Flow(one_move(coded_grad, by_head(step))) for step in range(1, shared)]
     clock.tick(*kv_flows)
     key_values = [flow.value for flow in kv_flows[::-1]] + [own_kv]
-    w_expert = mine_flow.value.reshape(MODEL_WIDTH, EXPERT_COLS)
+    down_flow = expert_rows(after(expert_output, kv_flows[-1].value))
+    Clock().tick(down_flow)
+    w_up = up_flow.value.reshape(MODEL_WIDTH, 2 * FF)
+    w_down = down_flow.value.reshape(MODEL_WIDTH, FF)
     queries = project_queries(normed, w_large, cosine, sine)
     mixture, lse = attend(queries, key_values, starts_row, "attend")
     middle, normed_two = leave_attention(mixture, w_large, hidden_in, gains)
 
     input_flows = [Flow(tokens_gather(normed_two))]
     far_tokens = [Flow(one_move(normed_two, by_head(step))) for step in range(1, shared)]
-    clock.tick(input_flows[0], *far_tokens)
-
-    input_flows = input_flows + [Flow(tokens_gather(flow.value)) for flow in far_tokens]
-    clock.tick(input_flows[0], *far_grads)
+    clock.tick(input_flows[0], *far_tokens, ready=(down_flow.value,))
 
     def seq_gather(block):
         return lax.all_gather(block, "seq", axis=0, tiled=True)
 
     grads = [seq_gather(after(coded_grad, *key_values))] + [
-        seq_gather(flow.value) for flow in far_grads
+        seq_gather(after(flow.value, *key_values)) for flow in far_grads
     ]
+    input_flows = input_flows + [Flow(tokens_gather(flow.value)) for flow in far_tokens]
+    clock.tick(input_flows[0])
     core_flows = [Flow(one_move(clock.finish(input_flows[0]), by_seq(1)))]
     clock.tick(core_flows[0], *input_flows[1:])
 
@@ -1170,16 +1176,16 @@
     blocks = jnp.arange(groups // 2, dtype=jnp.int32) * 2
     for step in range(shared):
         terms = []
+        inputs[step, 0] = clock.finish(input_flows[step])
+        if step > 0:
+            core_flows.append(Flow(one_move(inputs[step, 0], by_seq(1))))
+        pending = clock.begin(*core_flows[step:], *input_flows[step + 1 :], *back)
         for core in range(2):
-            if core == 0:
-                inputs[step, 0] = clock.finish(input_flows[step])
-                pending = clock.begin(*input_flows[step + 1 :], *back)
-            else:
+            if core == 1:
+                if step > 0:
+                    clock.end(pending, turn_of)
+                    pending = clock.begin(*back)
                 inputs[step, 1] = clock.finish(core_flows[step])
-                if step + 1 < shared:
-                    following = clock.finish(input_flows[step + 1])
-                    core_flows.append(Flow(one_move(following, by_seq(1))))
-                pending = clock.begin(*core_flows[step + 1 :], *back)
             order = (blocks + core) ^ seq_index
             scaled[step], hidden_grads[step, core], input_grad = experts(
                 order.astype(jnp.int32),
@@ -1187,17 +1193,20 @@
                 grads[step],
                 scaled[step],
                 w_small,
-                w_expert,
+                w_up,
+                w_down,
                 turn_of,
                 tokens,
             )
             turn_of = after(expert, input_grad)
             terms.append(input_grad)
-            clock.end(pending, turn_of)
+        clock.end(pending, turn_of)
         back.append(Flow(tokens_scatter(*terms)))
 
     work = [
-        lambda first: expert_shares(after(scaled[0], first), w_expert, tokens),
+        lambda first: expert_shares(
+            [after(part, first) for part in scaled], w_down, tokens, groups
+        ),
         lambda first: expert_terms(
             [(inputs[key], after(hidden_grads[key], first)) for key in inputs], 1.0, "up_terms"
         ),
@@ -1206,11 +1215,6 @@
             RESIDUAL_SCALE,
             "down_terms",
         ),
-    ] + [
-        functools.partial(
-            lambda first, part: expert_shares(after(part, first), w_expert, tokens), part=part
-        )
-        for part in scaled[1:]
     ]
     made = []
     while not all(flow.done for flow in back):
@@ -1229,9 +1233,8 @@
         made.append(work[len(made)](after(turn_of, *clock.last)))
         turn_of = after(expert, made[-1])
     clock.end(pending, turn_of)
-    up_part, down_part = made[1:3]
-    shares = made[:1] + made[3:]
-    shares = [lax.psum_scatter(part, "seq", scatter_dimension=0, tiled=True) for part in shares]
+    shares, up_part, down_part = made
+    shares = lax.psum_scatter(shares, "seq", scatter_dimension=0, tiled=True)
     expert_part = jnp.concatenate([up_part, down_part], axis=1)
     expert_part = expert_part.reshape(heads * groups, own_rows, EXPERT_COLS)
     expert_flow = Flow(
@@ -1273,7 +1276,11 @@
         Flow(one_move(term, functools.partial(along_stream, distance=-distance)))
         for term, distance in zip(kv_terms[:-1], range(heads, 0, -1))
     ]
-    clock.tick(*kv_flows)
+    share_flows = [
+        Flow(one_move(shares[step * tokens : (step + 1) * tokens], by_head(step)))
+        for step in range(1, shared)
+    ]
+    clock.tick(*kv_flows, *share_flows)
     terms = [(kv_terms[-1], kv_flows)]
     input_grad, *small_parts = leave(
         place,
@@ -1283,7 +1290,7 @@
         query_grads,
         cosine,
         sine,
-        after(hidden_in, *shares),
+        after(hidden_in, shares),
         normed,
         middle_grad,
         normed_two,
@@ -1295,14 +1302,9 @@
     )
 
     small_flow = Flow(rows_scatter(*small_parts))
-    share_flows = [
-        Flow(one_move(shares[step], by_head(step))) for step in range(1, shared)
-    ]
-    clock.tick(small_flow)
-    clock.tick(small_flow, *share_flows)
     small_flow = Flow(line_scatter(clock.finish(small_flow)))
     clock.finish(small_flow)
-    moe_out = shares[0].astype(f32)
+    moe_out = shares[:tokens].astype(f32)
     for flow in share_flows:
         moe_out = moe_out + flow.value.astype(f32)
     block_out = (middle + RESIDUAL_SCALE * moe_out).astype(bf16)
@@ -1318,7 +1320,7 @@
 
     expert_input_grad = expert_output_of(0, 2 * FF)
     expert_output_grad = expert_output_of(2 * FF, EXPERT_COLS)
-    large_sum = large_part.astype(f32)
+    large_sum = after(large_part, small_flow.value).astype(f32)
     query_weight_grad = large_sum[:, :QUERY_COLS]
     output_grad = large_sum[:, QUERY_COLS:]
     small_sum = small_flow.value

time: 827 us -> 778 us (0.941)
  waiting for transfers between devices: 446 us -> 393 us
  starting transfers between devices: 88.8 us -> 100 us
    all_to_all x2 -> x3, waiting for transfers between devices: 123 us -> 57.6 us  [spread(): return lax.all_to_all(block, axes, split_axis=0, concat_axis=0, tiled=True)]
    all_to_all x2 -> x3, starting transfers between devices: 11.1 us -> 38.1 us  [spread(): return lax.all_to_all(block, axes, split_axis=0, concat_axis=0, tiled=True)]
    ppermute x4, starting transfers between devices: 28.6 us -> 9.9 us  [swap_head(): return lax.ppermute(block, 'head', [(i, i ^ mask) for i in range(count)])]
    ppermute x4, waiting for transfers between devices: 41.9 us -> 25.6 us  [swap_head(): return lax.ppermute(block, 'head', [(i, i ^ mask) for i in range(count)])]
    ppermute x25, waiting for transfers between devices: 104 us -> 115 us  [swap(): return lax.ppermute(block, 'seq', [(i, i ^ mask) for i in range(count)])]
    pallas_call x2 -> x1, Pallas kernels: 14.8 us -> 17.4 us  [expert_shares(): pl.pallas_call(kernel, grid=(groups, count), in_specs=[pl.BlockSpec((toke...]
  transfers between devices with their start and end apart: 49 -> 49, of which waited for: 29 -> 33; matrix products, arithmetic and copies ran while one was open for 7% -> 7% of each run, Pallas kernels for 24% -> 24%
where the time goes in v2:
time: 778 us; the launch traced here: 772 us
  waiting for transfers between devices  393 us (51%)
  Pallas kernels  202 us (26%)
  starting transfers between devices  100 us (13%)
  other arithmetic  33.5 us (4%)
  local copies, waits for them, and re-layouts  29.2 us (4%)
  between operations  15.1 us (2%)
    ppermute x25, waiting for transfers between devices, swap(): return lax.ppermute(block, 'seq', [(i, i ^ mask) for i in range(count)])  115 us
    ppermute x8, waiting for transfers between devices, along_stream(): return lax.ppermute(block, ('head', 'seq'), route)  97.8 us
    all_gather x1, waiting for transfers between devices, shards(): w_small = lax.all_gather(small, ('head', 'seq'), axis=0, tiled=True)  68.6 us
    pallas_call x4, Pallas kernels, experts(): pl.pallas_call(kernel, grid_spec=pltpu.PrefetchScalarGridSpec(num_scalar_...  61.2 us
    all_to_all x3, waiting for transfers between devices, spread(): return lax.all_to_all(block, axes, split_axis=0, concat_axis=0, tiled=True)  57.6 us
    all_to_all x3, starting transfers between devices, spread(): return lax.all_to_all(block, axes, split_axis=0, concat_axis=0, tiled=True)  38.1 us
    pallas_call x2, Pallas kernels, expert_terms(): pl.pallas_call(kernel, grid=(MODEL_WIDTH // tile,), in_specs=in_specs, ou...  32.6 us
    pallas_call x1, Pallas kernels, attend_backward(): pl.pallas_call(kernel, grid=(pairs,), in_specs=[whole_block((1, tokens)),...  27.8 us
  transfers between devices with their start and end apart: 49, of which 33 were waited for; matrix products, arithmetic and copies ran while one was open for 7% of the time, Pallas kernels for 24%

profile of v2, /device:TPU:0, one launch (start us, length us, event | category | flops | bytes accessed | tf_op | source)
XLA Modules:
  0.0 772.3 jit_solution(12126591484084294791)
XLA Ops:
  20.0 7.4 all-to-all-start
  31.7 68.6 %all-gather.5.cloned.1.call-done.weight_ref.router_ref.small_ref = bf16[1536,1152]{1,0:T(8,128)(2,1)} async-done(((bf16[48,1152]{1,0:T(8,128)(2,1)}), bf16[1536,1152]{1,0:T(8,128)(2,1)}) %all-gather.5.cloned.1.call-update) | async-done | bytes 3538960 | tf_op jit(solution)/shard_map/all_gather | solution.py:1118
  104.6 11.5 %collective-permute-done = bf16[256,1664]{1,0:T(8,128)(2,1)S(1)} collective-permute-done((bf16[256,1664]{1,0:T(8,128)(2,1)S(1)}, bf16[256,1664]{1,0:T(8,128)(2,1)S(1)}, u32[]{:S(2)}, u32[]{:S(2)}) %collective-permute-start) | collective-permute-done | bytes 852000 | tf_op jit(solution)/shard_map/ppermute | solution.py:84
  117.4 6.8 collective-permute-start.2
  131.0 11.6 %collective-permute-done.2.refs_1_ = bf16[2,256,512]{2,1,0:T(8,128)(2,1)} collective-permute-done((bf16[2,256,512]{2,1,0:T(8,128)(2,1)}, bf16[2,256,512]{2,1,0:T(8,128)(2,1)}, u32[]{:S(2)}, u32[]{:S(2)}) %collective-permute-start.2) | collective-permute-done | bytes 524320 | tf_op jit(solution)/shard_map/ppermute | solution.py:61
  142.6 17.3 %collective-permute-done.3.refs_2_ = bf16[2,256,512]{2,1,0:T(8,128)(2,1)} collective-permute-done((bf16[2,256,512]{2,1,0:T(8,128)(2,1)}, bf16[2,256,512]{2,1,0:T(8,128)(2,1)}, u32[]{:S(2)}, u32[]{:S(2)}) %collective-permute-start.3) | collective-permute-done | bytes 524320 | tf_op jit(solution)/shard_map/ppermute | solution.py:61
  159.9 11.1 %collective-permute-done.4.refs_3_ = bf16[2,256,512]{2,1,0:T(8,128)(2,1)} collective-permute-done((bf16[2,256,512]{2,1,0:T(8,128)(2,1)}, bf16[2,256,512]{2,1,0:T(8,128)(2,1)}, u32[]{:S(2)}, u32[]{:S(2)}) %collective-permute-start.4) | collective-permute-done | bytes 524320 | tf_op jit(solution)/shard_map/ppermute | solution.py:61
  173.2 27.1 %all-to-all-start.1 = ((bf16[32,48,512]{2,1,0:T(8,128)(2,1)}), bf16[32,48,512]{2,1,0:T(8,128)(2,1)S(1)}, u32[]{:S(2)}, u32[]{:S(2)}) async-start(bf16[32,48,512]{2,1,0:T(8,128)(2,1)} %bitcast.9), calls=%async_computation.1 | async-start | bytes 3145728 | tf_op jit(solution)/shard_map/all_to_all | solution.py:1104
  201.1 14.0 %all-gather.7.cloned.1.call-done.weight_ref.query_weight_ref = bf16[1536,3072]{1,0:T(8,128)(2,1)} async-done(((bf16[48,3072]{1,0:T(8,128)(2,1)}), bf16[1536,3072]{1,0:T(8,128)(2,1)}) %all-gather.7.cloned.1.call-update) | async-done | bytes 9437200 | tf_op jit(solution)/shard_map/all_gather | solution.py:1140
  220.6 16.2 %attend.1 = (bf16[256,1536]{1,0:T(8,128)(2,1)}, f32[4,8,256]{2,1,0:T(8,128)}) custom-call(s32[1,256]{1,0:T(1,128)} %bitcast.193, bf16[256,1536]{1,0:T(8,128)(2,1)} %project_queries.1.query_ref, bf16[2,256,512]{2,1,0:T(8,128)(2,1)} %copy-done.24, bf16[2,256,512]{2,1,0:T(8,128)(2,1)} %collective-permute-done.2.refs_1_, ...), custom_call_target="tpu_custom_call" | custom-call | flops 2013265920 | bytes 4194304 | tf_op jit(solution)/shard_map/attend/pallas_call | solution.py:808
  236.8 5.7 leave_attention.1
  248.4 13.1 %collective-permute-done.5 = bf16[128,1536]{1,0:T(8,128)(2,1)S(1)} collective-permute-done((bf16[128,1536]{1,0:T(8,128)(2,1)S(1)}, bf16[128,1536]{1,0:T(8,128)(2,1)S(1)}, u32[]{:S(2)}, u32[]{:S(2)}) %collective-permute-start.5) | collective-permute-done | bytes 393248 | tf_op jit(solution)/shard_map/ppermute | solution.py:45
  270.6 20.8 %collective-permute-done.9 = bf16[2,128,1536]{2,1,0:T(8,128)(2,1)S(1)} collective-permute-done((bf16[2,128,1536]{2,1,0:T(8,128)(2,1)S(1)}, bf16[2,128,1536]{2,1,0:T(8,128)(2,1)S(1)}, u32[]{:S(2)}, u32[]{:S(2)}) %collective-permute-start.9) | collective-permute-done | bytes 786464 | tf_op jit(solution)/shard_map/ppermute | solution.py:45
  298.1 17.2 %collective-permute-done.11 = bf16[128,1536]{1,0:T(8,128)(2,1)} collective-permute-done((bf16[128,1536]{1,0:T(8,128)(2,1)}, bf16[128,1536]{1,0:T(8,128)(2,1)}, u32[]{:S(2)}, u32[]{:S(2)}) %collective-permute-start.11) | collective-permute-done | bytes 393248 | tf_op jit(solution)/shard_map/ppermute | solution.py:45
  321.9 15.2 %experts.4 = (bf16[2048,512]{1,0:T(8,128)(2,1)}, bf16[1024,1024]{1,0:T(8,128)(2,1)}, bf16[1024,1664]{1,0:T(8,128)(2,1)}) custom-call(s32[4]{0:T(128)} %fusion.27.order_ref, s32[1]{0:T(128)} %bitcast.6.expert_ref, bf16[1024,1536]{1,0:T(8,128)(2,1)} %bitcast.178, bf16[2048,1664]{1,0:T(8,128)(2,1)} %all-gather.9.cloned.1.call-done.grad_ref.refs_0_, ...), custom_call_target="tpu_custom_call" | custom-call | flops 8053063680 | bytes 14155776 | tf_op jit(solution)/shard_map/experts/pallas_call | solution.py:979
  337.1 15.3 %experts.5 = (bf16[2048,512]{1,0:T(8,128)(2,1)}, bf16[1024,1024]{1,0:T(8,128)(2,1)}, bf16[1024,1664]{1,0:T(8,128)(2,1)}) custom-call(s32[4]{0:T(128)} %add_xor_fusion.order_ref, s32[1]{0:T(128)} %bitcast.6.expert_ref, bf16[1024,1536]{1,0:T(8,128)(2,1)} %collective-permute-done.10.input_ref.refs_2_, ...), custom_call_target="tpu_custom_call", output_to_operand_aliasing={{0}: (8, {})} | custom-call | flops 8053063680 | bytes 14155776 | tf_op jit(solution)/shard_map/experts/pallas_call | solution.py:979
  362.1 15.6 %experts.6 = (bf16[2048,512]{1,0:T(8,128)(2,1)}, bf16[1024,1024]{1,0:T(8,128)(2,1)}, bf16[1024,1664]{1,0:T(8,128)(2,1)}) custom-call(s32[4]{0:T(128)} %fusion.27.order_ref, s32[1]{0:T(128)} %bitcast.6.expert_ref, bf16[1024,1536]{1,0:T(8,128)(2,1)} %bitcast.181, bf16[2048,1664]{1,0:T(8,128)(2,1)} %all-gather.11.cloned.1.call-done.grad_ref.refs_2_, ...), custom_call_target="tpu_custom_call" | custom-call | flops 8053063680 | bytes 14155776 | tf_op jit(solution)/shard_map/experts/pallas_call | solution.py:979
  382.9 15.1 %experts.7 = (bf16[2048,512]{1,0:T(8,128)(2,1)}, bf16[1024,1024]{1,0:T(8,128)(2,1)}, bf16[1024,1664]{1,0:T(8,128)(2,1)}) custom-call(s32[4]{0:T(128)} %add_xor_fusion.order_ref, s32[1]{0:T(128)} %bitcast.6.expert_ref, bf16[1024,1536]{1,0:T(8,128)(2,1)} %collective-permute-done.15.input_ref.refs_6_, ...), custom_call_target="tpu_custom_call", output_to_operand_aliasing={{0}: (8, {})} | custom-call | flops 8053063680 | bytes 14155776 | tf_op jit(solution)/shard_map/experts/pallas_call | solution.py:979
  403.0 17.4 %expert_shares.1 = bf16[4096,1536]{1,0:T(8,128)(2,1)} custom-call(bf16[2048,512]{1,0:T(8,128)(2,1)} %get-tuple-element.203.refs_0_.refs_1_, bf16[2048,512]{1,0:T(8,128)(2,1)} %get-tuple-element.204.refs_1_.refs_3_, bf16[1536,512]{1,0:T(8,128)(2,1)} %bitcast.188), custom_call_target="tpu_custom_call" | custom-call | flops 6442450944 | bytes 18350080 | tf_op jit(solution)/shard_map/expert_shares/pallas_call | solution.py:1019
  424.8 10.3 %collective-permute-done.19 = bf16[128,1664]{1,0:T(8,128)(2,1)S(1)} collective-permute-done((bf16[128,1664]{1,0:T(8,128)(2,1)S(1)}, bf16[128,1664]{1,0:T(8,128)(2,1)S(1)}, u32[]{:S(2)}, u32[]{:S(2)}) %collective-permute-start.19) | collective-permute-done | bytes 426016 | tf_op jit(solution)/shard_map/ppermute | solution.py:45
  439.7 20.3 %up_terms.1 = bf16[1536,1024]{1,0:T(8,128)(2,1)} custom-call(bf16[1024,1536]{1,0:T(8,128)(2,1)} %bitcast.179, bf16[1024,1024]{1,0:T(8,128)(2,1)} %get-tuple-element.190.refs_1_, bf16[1024,1536]{1,0:T(8,128)(2,1)} %collective-permute-done.10.input_ref.refs_2_, bf16[1024,1024]{1,0:T(8,128)(2,1)} %get-tuple-element.192.refs_3_, bf16[1024,1536]{1,0:T(8,128)(2,1)} %bitcast.182, ...), custom_call_target="tpu_custom_call" | custom-call | flops 12884901888 | bytes 24117248 | tf_op jit(solution)/shard_map/up_terms/pallas_call | solution.py:1049
  468.9 12.3 %down_terms.1 = bf16[1536,512]{1,0:T(8,128)(2,1)} custom-call(bf16[2048,1664]{1,0:T(8,128)(2,1)} %all-gather.9.cloned.1.call-done.grad_ref.refs_0_, bf16[2048,512]{1,0:T(8,128)(2,1)} %get-tuple-element.203.refs_0_.refs_1_, bf16[2048,1664]{1,0:T(8,128)(2,1)} %all-gather.11.cloned.1.call-done.grad_ref.refs_2_, bf16[2048,512]{1,0:T(8,128)(2,1)} %get-tuple-element.204.refs_1_.refs_3_), custom_call_target="tpu_custom_call" | custom-call | flops 6442450944 | bytes 18350080 | tf_op jit(solution)/shard_map/down_terms/pallas_call | solution.py:1049
  496.3 9.0 %collective-permute-done.26.refs_0_ = bf16[256,1664]{1,0:T(8,128)(2,1)S(1)} collective-permute-done((bf16[256,1664]{1,0:T(8,128)(2,1)S(1)}, bf16[256,1664]{1,0:T(8,128)(2,1)S(1)}, u32[]{:S(2)}, u32[]{:S(2)}) %collective-permute-start.26) | collective-permute-done | bytes 852000 | tf_op jit(solution)/shard_map/ppermute | solution.py:84
  512.1 7.8 %return_to_attention.1 = (bf16[256,128]{1,0:T(8,128)(2,1)}, f32[256,1536]{1,0:T(8,128)}, bf16[256,1536]{1,0:T(8,128)(2,1)}, bf16[256,1536]{1,0:T(8,128)(2,1)}, f32[8,1536]{1,0:T(8,128)}) custom-call(f32[256,1664]{1,0:T(8,128)} %pad_maximum_fusion.1.back_ref, bf16[256,128]{1,0:T(8,128)(2,1)} %concatenate.46.code_ref, ...), custom_call_target="tpu_custom_call" | custom-call | flops 1207959552 | bytes 14155776 | tf_op jit(solution)/shard_map/return_to_attention/pallas_call | solution.py:489
  520.0 27.8 %attend_backward.1 = (bf16[256,1536]{1,0:T(8,128)(2,1)}, bf16[2,256,512]{2,1,0:T(8,128)(2,1)}, bf16[2,256,512]{2,1,0:T(8,128)(2,1)}, bf16[2,256,512]{2,1,0:T(8,1...) custom-call(s32[1,256]{1,0:T(1,128)} %bitcast.194, bf16[256,1536]{1,0:T(8,128)(2,1)} %project_queries.1.query_ref, ...), custom_call_target="tpu_custom_call" | custom-call | flops 5033164800 | bytes 8388608 | tf_op jit(solution)/shard_map/attend_backward/pallas_call | solution.py:888
  547.8 9.8 %weight_terms.1 = bf16[1536,3072]{1,0:T(8,128)(2,1)} custom-call(bf16[256,1536]{1,0:T(8,128)(2,1)} %get-tuple-element.127.normed_ref.refs_0_, bf16[256,1536]{1,0:T(8,128)(2,1)} %get-tuple-element.217.refs_1_.refs_0_, bf16[256,1536]{1,0:T(8,128)(2,1)} %get-tuple-element.219.refs_2_, bf16[256,1536]{1,0:T(8,128)(2,1)} %get-tuple-element.137.mixture_ref.refs_3_), custom_call_target="tpu_custom_call" | custom-call | flops 2415919104 | bytes 11010048 | tf_op jit(solution)/shard_map/weight_terms/pallas_call | solution.py:577
  557.7 57.6 %all-to-all-done.2 = bf16[32,48,1536]{2,1,0:T(8,128)(2,1)} async-done(((bf16[32,48,1536]{2,1,0:T(8,128)(2,1)}), bf16[32,48,1536]{2,1,0:T(8,128)(2,1)}, u32[]{:S(2)}, u32[]{:S(2)}) %all-to-all-start.2) | async-done | bytes 4718624 | tf_op jit(solution)/shard_map/all_to_all | solution.py:1104
  625.0 16.3 %collective-permute-done.29.refs_3_ = bf16[2,256,512]{2,1,0:T(8,128)(2,1)S(1)} collective-permute-done((bf16[2,256,512]{2,1,0:T(8,128)(2,1)}, bf16[2,256,512]{2,1,0:T(8,128)(2,1)S(1)}, u32[]{:S(2)}, u32[]{:S(2)}) %collective-permute-start.29) | collective-permute-done | bytes 524320 | tf_op jit(solution)/shard_map/ppermute | solution.py:61
  641.3 41.5 %collective-permute-done.30.refs_4_ = bf16[2,256,512]{2,1,0:T(8,128)(2,1)} collective-permute-done((bf16[2,256,512]{2,1,0:T(8,128)(2,1)}, bf16[2,256,512]{2,1,0:T(8,128)(2,1)}, u32[]{:S(2)}, u32[]{:S(2)}) %collective-permute-start.30) | collective-permute-done | bytes 524320 | tf_op jit(solution)/shard_map/ppermute | solution.py:61
  682.8 13.1 %leave.1 = (f32[256,1536]{1,0:T(8,128)}, bf16[4,4,48,1152]{3,2,1,0:T(8,128)(2,1)}, bf16[4,4,48,1152]{3,2,1,0:T(8,128)(2,1)}) custom-call(s32[2]{0:T(128)} %pad_add_fusion.place_ref, f32[256,128]{1,0:T(8,128)} %get-tuple-element.345.cosine_ref, f32[256,128]{1,0:T(8,128)} %get-tuple-element.346.sine_ref, bf16[256,1536]{1,0:T(8,128)(2,1)} %hidden_ref.4, ...), custom_call_target="tpu_custom_call" | custom-call | flops 2818572288 | bytes 18087936 | tf_op jit(solution)/shard_map/leave/pallas_call | solution.py:683
  723.6 8.8 %collective-permute-done.34 = bf16[2,2,48,1152]{3,2,1,0:T(8,128)(2,1)S(1)} collective-permute-done((bf16[2,2,48,1152]{3,2,1,0:T(8,128)(2,1)S(1)}, bf16[2,2,48,1152]{3,2,1,0:T(8,128)(2,1)S(1)}, u32[]{:S(2)}, u32[]{:S(2)}) %collective-permute-start.34) | collective-permute-done | bytes 442400 | tf_op jit(solution)/shard_map/ppermute | solution.py:45
  754.0 7.2 collective-permute-done.38
  (224 shorter events, 188.3 us)
Async XLA Ops:
  7.2 93.2 %all-gather.5.cloned.1.call-start = ((), (), s32[]{:S(2)}) async-start(), calls=%async_computation.5 | async-start | bytes 3649536 | tf_op jit(solution)/shard_map/all_gather | solution.py:1118
  11.1 203.9 %all-gather.7.cloned.1.call-start = ((), (), s32[]{:S(2)}) async-start(), calls=%async_computation.6 | async-start | bytes 9732096 | tf_op jit(solution)/shard_map/all_gather | solution.py:1140
  20.0 96.1 %all-to-all-start = ((bf16[32,48,1024]{2,1,0:T(8,128)(2,1)}), bf16[32,48,1024]{2,1,0:T(8,128)(2,1)}, u32[]{:S(2)}, u32[]{:S(2)}) async-start(bf16[32,48,1024]{2,1,0:T(8,128)(2,1)} %bitcast.5), calls=%async_computation | async-start | bytes 6291456 | tf_op jit(solution)/shard_map/all_to_all | solution.py:1104
  27.4 294.5 %all-gather.9.cloned.1.call-start = ((), (), s32[]{:S(2)}) async-start(), calls=%async_computation.7 | async-start | bytes 7667712 | tf_op jit(solution)/shard_map/all_gather | solution.py:1161
  27.5 88.6 %collective-permute-start = (bf16[256,1664]{1,0:T(8,128)(2,1)S(1)}, bf16[256,1664]{1,0:T(8,128)(2,1)S(1)}, u32[]{:S(2)}, u32[]{:S(2)}) collective-permute-start(bf16[256,1664]{1,0:T(8,128)(2,1)S(1)} %concatenate.42), channel_id=1, source_target_pairs={{0,8},{8,0},{16,24},{24,16},{1,9},{9,1},{17,25},{25,17},{2,10},{10... | collective-permute-start | bytes 2555912 | tf_op jit(solution)/shard_map/ppermute | solution.py:84
  117.4 25.2 %collective-permute-start.2 = (bf16[2,256,512]{2,1,0:T(8,128)(2,1)}, bf16[2,256,512]{2,1,0:T(8,128)(2,1)}, u32[]{:S(2)}, u32[]{:S(2)}) collective-permute-start(bf16[2,256,512]{2,1,0:T(8,128)(2,1)} %get-tuple-element.136.refs_4_), channel_id=1, source_target_pairs={{0,24},{8,1},{16,9},{24,17},{1,25},{9,2},{17,10},{25,18},{2,26},{1... | collective-permute-start | bytes 1572872 | tf_op jit(solution)/shard_map/ppermute | solution.py:61
  124.2 35.7 %collective-permute-start.3 = (bf16[2,256,512]{2,1,0:T(8,128)(2,1)}, bf16[2,256,512]{2,1,0:T(8,128)(2,1)}, u32[]{:S(2)}, u32[]{:S(2)}) collective-permute-start(bf16[2,256,512]{2,1,0:T(8,128)(2,1)} %get-tuple-element.136.refs_4_), channel_id=1, source_target_pairs={{0,16},{8,24},{16,1},{24,9},{1,17},{9,25},{17,2},{25,10},{2,18},{1... | collective-permute-start | bytes 1572872 | tf_op jit(solution)/shard_map/ppermute | solution.py:61
  127.0 44.0 %collective-permute-start.4 = (bf16[2,256,512]{2,1,0:T(8,128)(2,1)}, bf16[2,256,512]{2,1,0:T(8,128)(2,1)}, u32[]{:S(2)}, u32[]{:S(2)}) collective-permute-start(bf16[2,256,512]{2,1,0:T(8,128)(2,1)} %get-tuple-element.136.refs_4_), channel_id=1, source_target_pairs={{0,8},{8,16},{16,24},{24,1},{1,9},{9,17},{17,25},{25,2},{2,10},{10... | collective-permute-start | bytes 1572872 | tf_op jit(solution)/shard_map/ppermute | solution.py:61
  173.2 70.5 %all-to-all-start.1 = ((bf16[32,48,512]{2,1,0:T(8,128)(2,1)}), bf16[32,48,512]{2,1,0:T(8,128)(2,1)S(1)}, u32[]{:S(2)}, u32[]{:S(2)}) async-start(bf16[32,48,512]{2,1,0:T(8,128)(2,1)} %bitcast.9), calls=%async_computation.1 | async-start | bytes 3145728 | tf_op jit(solution)/shard_map/all_to_all | solution.py:1104
  200.3 161.8 %all-gather.11.cloned.1.call-start = ((), (), s32[]{:S(2)}) async-start(), calls=%async_computation.8 | async-start | bytes 7667712 | tf_op jit(solution)/shard_map/all_gather | solution.py:1161
  200.8 414.4 %reduce-scatter.3.cloned.1.call-start = ((), (), s32[]{:S(2)}) async-start(), calls=%async_computation.9 | async-start | bytes 14155776 | tf_op jit(solution)/shard_map/reduce_scatter | solution.py:1237
  246.8 20.4 %collective-permute-start.7 = (bf16[256,1536]{1,0:T(8,128)(2,1)}, bf16[256,1536]{1,0:T(8,128)(2,1)S(1)}, u32[]{:S(2)}, u32[]{:S(2)}) collective-permute-start(bf16[256,1536]{1,0:T(8,128)(2,1)} %get-tuple-element.144.normed_ref.normed_two_ref), channel_id=1, source_target_pairs={{0,8},{8,0},{16,24},{24,16},{1,9},{9,1},{17,25},{25,17},{2,10},{10... | collective-permute-start | bytes 2359304 | tf_op jit(solution)/shard_map/ppermute | solution.py:84
  267.3 24.2 %collective-permute-start.9 = (bf16[2,128,1536]{2,1,0:T(8,128)(2,1)S(1)}, bf16[2,128,1536]{2,1,0:T(8,128)(2,1)S(1)}, u32[]{:S(2)}, u32[]{:S(2)}) collective-permute-start(bf16[2,128,1536]{2,1,0:T(8,128)(2,1)S(1)} %get-tuple-element.146), channel_id=1, source_target_pairs={{0,2},{1,3},{2,0},{3,1},{4,6},{5,7},{6,4},{7,5},{8,10},{9,11},{10,... | collective-permute-start | bytes 2359304 | tf_op jit(solution)/shard_map/ppermute | solution.py:45
  269.5 24.9 %collective-permute-start.8 = (bf16[2,128,1536]{2,1,0:T(8,128)(2,1)S(1)}, bf16[2,128,1536]{2,1,0:T(8,128)(2,1)S(1)}, u32[]{:S(2)}, u32[]{:S(2)}) collective-permute-start(bf16[2,128,1536]{2,1,0:T(8,128)(2,1)S(1)} %get-tuple-element.145), channel_id=1, source_target_pairs={{0,4},{1,5},{2,6},{3,7},{4,0},{5,1},{6,2},{7,3},{8,12},{9,13},{10,... | collective-permute-start | bytes 2359304 | tf_op jit(solution)/shard_map/ppermute | solution.py:45
  294.9 25.0 %collective-permute-start.10 = (bf16[1024,1536]{1,0:T(8,128)(2,1)S(1)}, bf16[1024,1536]{1,0:T(8,128)(2,1)}, u32[]{:S(2)}, u32[]{:S(2)}) collective-permute-start(bf16[1024,1536]{1,0:T(8,128)(2,1)S(1)} %bitcast.177), channel_id=1, source_target_pairs={{0,1},{1,0},{2,3},{3,2},{4,5},{5,4},{6,7},{7,6},{8,9},{9,8},{10,11... | collective-permute-start | bytes 9437192 | tf_op jit(solution)/shard_map/ppermute | solution.py:45
  295.0 20.3 %collective-permute-start.11 = (bf16[128,1536]{1,0:T(8,128)(2,1)}, bf16[128,1536]{1,0:T(8,128)(2,1)}, u32[]{:S(2)}, u32[]{:S(2)}) collective-permute-start(bf16[128,1536]{1,0:T(8,128)(2,1)} %get-tuple-element.155), channel_id=1, source_target_pairs={{0,2},{1,3},{2,0},{3,1},{4,6},{5,7},{6,4},{7,5},{8,10},{9,11},{10,... | collective-permute-start | bytes 1179656 | tf_op jit(solution)/shard_map/ppermute | solution.py:45
  296.8 21.0 %collective-permute-start.12 = (bf16[128,1536]{1,0:T(8,128)(2,1)}, bf16[128,1536]{1,0:T(8,128)(2,1)}, u32[]{:S(2)}, u32[]{:S(2)}) collective-permute-start(bf16[128,1536]{1,0:T(8,128)(2,1)} %get-tuple-element.156), channel_id=1, source_target_pairs={{0,4},{1,5},{2,6},{3,7},{4,0},{5,1},{6,2},{7,3},{8,12},{9,13},{10,... | collective-permute-start | bytes 1179656 | tf_op jit(solution)/shard_map/ppermute | solution.py:45
  320.0 34.8 %collective-permute-start.13 = (bf16[2,128,1536]{2,1,0:T(8,128)(2,1)}, bf16[2,128,1536]{2,1,0:T(8,128)(2,1)}, u32[]{:S(2)}, u32[]{:S(2)}) collective-permute-start(bf16[2,128,1536]{2,1,0:T(8,128)(2,1)} %get-tuple-element.157), channel_id=1, source_target_pairs={{0,4},{1,5},{2,6},{3,7},{4,0},{5,1},{6,2},{7,3},{8,12},{9,13},{10,... | collective-permute-start | bytes 2359304 | tf_op jit(solution)/shard_map/ppermute | solution.py:45
  320.0 35.7 %collective-permute-start.14 = (bf16[2,128,1536]{2,1,0:T(8,128)(2,1)}, bf16[2,128,1536]{2,1,0:T(8,128)(2,1)}, u32[]{:S(2)}, u32[]{:S(2)}) collective-permute-start(bf16[2,128,1536]{2,1,0:T(8,128)(2,1)} %get-tuple-element.158), channel_id=1, source_target_pairs={{0,2},{1,3},{2,0},{3,1},{4,6},{5,7},{6,4},{7,5},{8,10},{9,11},{10,... | collective-permute-start | bytes 2359304 | tf_op jit(solution)/shard_map/ppermute | solution.py:45
  357.5 20.2 %collective-permute-start.16 = (bf16[1024,1664]{1,0:T(8,128)(2,1)}, bf16[1024,1664]{1,0:T(8,128)(2,1)}, u32[]{:S(2)}, u32[]{:S(2)}) collective-permute-start(bf16[1024,1664]{1,0:T(8,128)(2,1)} %get-tuple-element.165), channel_id=1, source_target_pairs={{0,1},{1,0},{2,3},{3,2},{4,5},{5,4},{6,7},{7,6},{8,9},{9,8},{10,11... | collective-permute-start | bytes 10223624 | tf_op jit(solution)/shard_map/ppermute | solution.py:45
  357.6 20.1 %collective-permute-start.15 = (bf16[1024,1536]{1,0:T(8,128)(2,1)S(1)}, bf16[1024,1536]{1,0:T(8,128)(2,1)}, u32[]{:S(2)}, u32[]{:S(2)}) collective-permute-start(bf16[1024,1536]{1,0:T(8,128)(2,1)S(1)} %bitcast.180), channel_id=1, source_target_pairs={{0,1},{1,0},{2,3},{3,2},{4,5},{5,4},{6,7},{7,6},{8,9},{9,8},{10,11... | collective-permute-start | bytes 9437192 | tf_op jit(solution)/shard_map/ppermute | solution.py:45
  381.6 21.3 %collective-permute-start.17 = (bf16[2,128,1664]{2,1,0:T(8,128)(2,1)S(1)}, bf16[2,128,1664]{2,1,0:T(8,128)(2,1)}, u32[]{:S(2)}, u32[]{:S(2)}) collective-permute-start(bf16[2,128,1664]{2,1,0:T(8,128)(2,1)S(1)} %slice_bitcast_fusion.9), channel_id=1, source_target_pairs={{0,2},{1,3},{2,0},{3,1},{4,6},{5,7},{6,4},{7,5},{8,10},{9,11},{10,... | collective-permute-start | bytes 2555912 | tf_op jit(solution)/shard_map/ppermute | solution.py:45
  381.7 21.3 %collective-permute-start.18 = (bf16[2,128,1664]{2,1,0:T(8,128)(2,1)S(1)}, bf16[2,128,1664]{2,1,0:T(8,128)(2,1)}, u32[]{:S(2)}, u32[]{:S(2)}) collective-permute-start(bf16[2,128,1664]{2,1,0:T(8,128)(2,1)S(1)} %slice_bitcast_fusion.8), channel_id=1, source_target_pairs={{0,4},{1,5},{2,6},{3,7},{4,0},{5,1},{6,2},{7,3},{8,12},{9,13},{10,... | collective-permute-start | bytes 2555912 | tf_op jit(solution)/shard_map/ppermute | solution.py:45
  436.2 25.9 %collective-permute-start.22 = (bf16[2,128,1664]{2,1,0:T(8,128)(2,1)S(1)}, bf16[2,128,1664]{2,1,0:T(8,128)(2,1)S(1)}, u32[]{:S(2)}, u32[]{:S(2)}) collective-permute-start(bf16[2,128,1664]{2,1,0:T(8,128)(2,1)S(1)} %slice_bitcast_fusion.4), channel_id=1, source_target_pairs={{0,2},{1,3},{2,0},{3,1},{4,6},{5,7},{6,4},{7,5},{8,10},{9,11},{10,... | collective-permute-start | bytes 2555912 | tf_op jit(solution)/shard_map/ppermute | solution.py:45
  437.9 27.9 %collective-permute-start.23 = (bf16[2,128,1664]{2,1,0:T(8,128)(2,1)S(1)}, bf16[2,128,1664]{2,1,0:T(8,128)(2,1)S(1)}, u32[]{:S(2)}, u32[]{:S(2)}) collective-permute-start(bf16[2,128,1664]{2,1,0:T(8,128)(2,1)S(1)} %slice_bitcast_fusion.3), channel_id=1, source_target_pairs={{0,4},{1,5},{2,6},{3,7},{4,0},{5,1},{6,2},{7,3},{8,12},{9,13},{10,... | collective-permute-start | bytes 2555912 | tf_op jit(solution)/shard_map/ppermute | solution.py:45
  466.3 20.1 %collective-permute-start.24 = (bf16[128,1664]{1,0:T(8,128)(2,1)S(1)}, bf16[128,1664]{1,0:T(8,128)(2,1)S(1)}, u32[]{:S(2)}, u32[]{:S(2)}) collective-permute-start(bf16[128,1664]{1,0:T(8,128)(2,1)S(1)} %slice_bitcast_fusion.16), channel_id=1, source_target_pairs={{0,4},{1,5},{2,6},{3,7},{4,0},{5,1},{6,2},{7,3},{8,12},{9,13},{10,... | collective-permute-start | bytes 1277960 | tf_op jit(solution)/shard_map/ppermute | solution.py:45
  506.3 109.0 %all-to-all-start.2 = ((bf16[32,48,1536]{2,1,0:T(8,128)(2,1)}), bf16[32,48,1536]{2,1,0:T(8,128)(2,1)}, u32[]{:S(2)}, u32[]{:S(2)}) async-start(bf16[32,48,1536]{2,1,0:T(8,128)(2,1)} %bitcast.163), calls=%async_computation.3 | async-start | bytes 9437184 | tf_op jit(solution)/shard_map/all_to_all | solution.py:1104
  509.9 252.8 %reduce-scatter.5.cloned.1.call-start = ((), (), s32[]{:S(2)}) async-start(), calls=%async_computation.10 | async-start | bytes 9732096 | tf_op jit(solution)/shard_map/reduce_scatter | solution.py:1274
  617.8 23.5 %collective-permute-start.29 = (bf16[2,256,512]{2,1,0:T(8,128)(2,1)}, bf16[2,256,512]{2,1,0:T(8,128)(2,1)S(1)}, u32[]{:S(2)}, u32[]{:S(2)}) collective-permute-start(bf16[2,256,512]{2,1,0:T(8,128)(2,1)} %get-tuple-element.228), channel_id=1, source_target_pairs={{24,0},{1,8},{9,16},{17,24},{25,1},{2,9},{10,17},{18,25},{26,2},{3... | collective-permute-start | bytes 1572872 | tf_op jit(solution)/shard_map/ppermute | solution.py:61
  619.1 63.7 %collective-permute-start.30 = (bf16[2,256,512]{2,1,0:T(8,128)(2,1)}, bf16[2,256,512]{2,1,0:T(8,128)(2,1)}, u32[]{:S(2)}, u32[]{:S(2)}) collective-permute-start(bf16[2,256,512]{2,1,0:T(8,128)(2,1)} %get-tuple-element.229), channel_id=1, source_target_pairs={{16,0},{24,8},{1,16},{9,24},{17,1},{25,9},{2,17},{10,25},{18,2},{2... | collective-permute-start | bytes 1572872 | tf_op jit(solution)/shard_map/ppermute | solution.py:61
  620.4 62.4 %collective-permute-start.31 = (bf16[2,256,512]{2,1,0:T(8,128)(2,1)}, bf16[2,256,512]{2,1,0:T(8,128)(2,1)}, u32[]{:S(2)}, u32[]{:S(2)}) collective-permute-start(bf16[2,256,512]{2,1,0:T(8,128)(2,1)} %get-tuple-element.230), channel_id=1, source_target_pairs={{8,0},{16,8},{24,16},{1,24},{9,1},{17,9},{25,17},{2,25},{10,2},{18... | collective-permute-start | bytes 1572872 | tf_op jit(solution)/shard_map/ppermute | solution.py:61
  621.7 79.3 %collective-permute-start.27 = (bf16[256,1536]{1,0:T(8,128)(2,1)S(1)}, bf16[256,1536]{1,0:T(8,128)(2,1)S(1)}, u32[]{:S(2)}, u32[]{:S(2)}) collective-permute-start(bf16[256,1536]{1,0:T(8,128)(2,1)S(1)} %slice.217), channel_id=1, source_target_pairs={{0,8},{8,0},{16,24},{24,16},{1,9},{9,1},{17,25},{25,17},{2,10},{10... | collective-permute-start | bytes 2359304 | tf_op jit(solution)/shard_map/ppermute | solution.py:84
  (42 other events, 785.2 us)
Sparse Core Ops, SparseCore 0:
  11.5 88.8 all-gather.4
  103.8 111.1 all-gather.6
  217.5 68.4 all-gather.8
  287.8 74.2 all-gather.10
  420.5 149.7 reduce-scatter.2
  576.1 183.2 reduce-scatter.4

commit v3 on v2

--- a/solution.py
+++ b/solution.py
@@ -1004,10 +1004,10 @@
     )(*operands)
 
 
-def expert_shares(scaled, weights, tokens, groups):
+def expert_shares(orders, scaled, weights, tokens, groups):
     count = len(scaled)
 
-    def kernel(*refs):
+    def kernel(orders_ref, *refs):
         weight_ref, out_ref = refs[count:]
         for k in range(count):
 
@@ -1015,19 +1015,29 @@
             def _():
                 out_ref[...] = dot(refs[k][...], weight_ref[...], NT).astype(bf16)
 
+    def piece_spec(piece):
+        return pl.BlockSpec(
+            (tokens, FF), lambda i, k, orders_ref: (orders_ref[piece * groups + i], 0)
+        )
+
     rows = groups * count * tokens
     return pl.pallas_call(
         kernel,
-        grid=(groups, count),
-        in_specs=[pl.BlockSpec((tokens, FF), lambda i, k: (i, 0))] * count + [expert_block(0)],
-        out_specs=pl.BlockSpec((tokens, MODEL_WIDTH), lambda i, k: (i * count + k, 0)),
+        grid_spec=pltpu.PrefetchScalarGridSpec(
+            num_scalar_prefetch=1,
+            grid=(groups, count),
+            in_specs=[piece_spec(k) for k in range(count)] + [expert_block(0)],
+            out_specs=pl.BlockSpec(
+                (tokens, MODEL_WIDTH), lambda i, k, orders_ref: (i * count + k, 0)
+            ),
+        ),
         out_shape=jax.ShapeDtypeStruct((rows, MODEL_WIDTH), bf16),
         compiler_params=params(),
         cost_estimate=cost(
             2 * rows * MODEL_WIDTH * FF, 2 * MODEL_WIDTH * (rows + FF) + 2 * rows * FF
         ),
         name="expert_shares",
-    )(*scaled, weights)
+    )(orders, *scaled, weights)
 
 
 def expert_terms(pieces, scale, name):
@@ -1143,7 +1153,9 @@
         axis=0,
         tiled=True,
     )
-    clock.tick(*kv_flows)
+    grad_flows = [Flow(tokens_gather(flow.value)) for flow in far_grads]
+    clock.tick(kv_flows[0], kv_flows[-1], *grad_flows)
+    clock.tick(*kv_flows[1:-1], *grad_flows)
     key_values = [flow.value for flow in kv_flows[::-1]] + [own_kv]
     down_flow = expert_rows(after(expert_output, kv_flows[-1].value))
     Clock().tick(down_flow)
@@ -1155,18 +1167,21 @@
 
     input_flows = [Flow(tokens_gather(normed_two))]
     far_tokens = [Flow(one_move(normed_two, by_head(step))) for step in range(1, shared)]
-    clock.tick(input_flows[0], *far_tokens, ready=(down_flow.value,))
+    for flow in grad_flows:
+        clock.finish(flow)
+    grad_cores = [Flow(one_move(flow.value, by_seq(1))) for flow in grad_flows]
+    clock.tick(input_flows[0], *far_tokens, *grad_cores, ready=(down_flow.value,))
 
     def seq_gather(block):
         return lax.all_gather(block, "seq", axis=0, tiled=True)
 
     grads = [seq_gather(after(coded_grad, *key_values))] + [
-        seq_gather(after(flow.value, *key_values)) for flow in far_grads
+        jnp.concatenate([flow.value, core.value], axis=0)
+        for flow, core in zip(grad_flows, grad_cores)
     ]
     input_flows = input_flows + [Flow(tokens_gather(flow.value)) for flow in far_tokens]
     clock.tick(input_flows[0])
     core_flows = [Flow(one_move(clock.finish(input_flows[0]), by_seq(1)))]
-    clock.tick(core_flows[0], *input_flows[1:])
 
     back = []
     inputs = {}
@@ -1182,11 +1197,13 @@
         pending = clock.begin(*core_flows[step:], *input_flows[step + 1 :], *back)
         for core in range(2):
             if core == 1:
-                if step > 0:
-                    clock.end(pending, turn_of)
-                    pending = clock.begin(*back)
+                clock.end(pending, turn_of)
+                pending = clock.begin(*input_flows[step + 1 :], *back)
                 inputs[step, 1] = clock.finish(core_flows[step])
-            order = (blocks + core) ^ seq_index
+            if step == 0:
+                order = (blocks + core) ^ seq_index
+            else:
+                order = core * (groups // 2) + jnp.arange(groups // 2)
             scaled[step], hidden_grads[step, core], input_grad = experts(
                 order.astype(jnp.int32),
                 inputs[step, core],
@@ -1203,9 +1220,13 @@
         clock.end(pending, turn_of)
         back.append(Flow(tokens_scatter(*terms)))
 
+    everyone = jnp.arange(groups)
+    place_of = everyone ^ seq_index
+    place_of = (place_of % 2) * (groups // 2) + place_of // 2
+    orders = jnp.concatenate([everyone] + [place_of] * (shared - 1)).astype(jnp.int32)
     work = [
         lambda first: expert_shares(
-            [after(part, first) for part in scaled], w_down, tokens, groups
+            orders, [after(part, first) for part in scaled], w_down, tokens, groups
         ),
         lambda first: expert_terms(
             [(inputs[key], after(hidden_grads[key], first)) for key in inputs], 1.0, "up_terms"

time: 778 us -> 799 us (1.027)
  starting transfers between devices: 100 us -> 113 us
    ppermute x25 -> x30, waiting for transfers between devices: 115 us -> 135 us  [swap(): return lax.ppermute(block, 'seq', [(i, i ^ mask) for i in range(count)])]
    all_gather x1, waiting for transfers between devices: 14 us -> 0.02 us  [shards(): lax.all_gather(jnp.concatenate([query_weight, output_weight], axis=1), ('...]
    ppermute x8, waiting for transfers between devices: 97.8 us -> 85.7 us  [along_stream(): return lax.ppermute(block, ('head', 'seq'), route)]
    all_to_all x3, starting transfers between devices: 38.1 us -> 49.7 us  [spread(): return lax.all_to_all(block, axes, split_axis=0, concat_axis=0, tiled=True)]
    ppermute x25 -> x30, starting transfers between devices: 24.5 us -> 29.2 us  [swap(): return lax.ppermute(block, 'seq', [(i, i ^ mask) for i in range(count)])]
  transfers between devices with their start and end apart: 49 -> 53, of which waited for: 33 -> 35; matrix products, arithmetic and copies ran while one was open for 7% -> 7% of each run, Pallas kernels for 24% -> 23%
where the time goes in v3:
time: 799 us; the launch traced here: 792 us
  waiting for transfers between devices  388 us (49%)
  Pallas kernels  203 us (25%)
  starting transfers between devices  113 us (14%)
  other arithmetic  36.8 us (5%)
  local copies, waits for them, and re-layouts  36.6 us (5%)
  between operations  14.7 us (2%)
    ppermute x30, waiting for transfers between devices, swap(): return lax.ppermute(block, 'seq', [(i, i ^ mask) for i in range(count)])  135 us
    ppermute x8, waiting for transfers between devices, along_stream(): return lax.ppermute(block, ('head', 'seq'), route)  85.7 us
    all_gather x1, waiting for transfers between devices, shards(): w_small = lax.all_gather(small, ('head', 'seq'), axis=0, tiled=True)  68.6 us
    pallas_call x4, Pallas kernels, experts(): pl.pallas_call(kernel, grid_spec=pltpu.PrefetchScalarGridSpec(num_scalar_...  61.2 us
    all_to_all x3, waiting for transfers between devices, spread(): return lax.all_to_all(block, axes, split_axis=0, concat_axis=0, tiled=True)  57.7 us
    all_to_all x3, starting transfers between devices, spread(): return lax.all_to_all(block, axes, split_axis=0, concat_axis=0, tiled=True)  49.7 us
    pallas_call x2, Pallas kernels, expert_terms(): pl.pallas_call(kernel, grid=(MODEL_WIDTH // tile,), in_specs=in_specs, ou...  32.8 us
    ppermute x4, waiting for transfers between devices, swap_head(): return lax.ppermute(block, 'head', [(i, i ^ mask) for i in range(count)])  31.4 us
  transfers between devices with their start and end apart: 53, of which 35 were waited for; matrix products, arithmetic and copies ran while one was open for 7% of the time, Pallas kernels for 23%

profile of v3, /device:TPU:0, one launch (start us, length us, event | category | flops | bytes accessed | tf_op | source)
XLA Modules:
  0.0 792.2 jit_solution(3102764644081921094)
XLA Ops:
  20.0 7.4 all-to-all-start
  31.7 68.6 %all-gather.4.cloned.1.call-done.weight_ref.router_ref.small_ref = bf16[1536,1152]{1,0:T(8,128)(2,1)} async-done(((bf16[48,1152]{1,0:T(8,128)(2,1)}), bf16[1536,1152]{1,0:T(8,128)(2,1)}) %all-gather.4.cloned.1.call-update) | async-done | bytes 3538960 | tf_op jit(solution)/shard_map/all_gather | solution.py:1128
  104.5 11.5 %collective-permute-done = bf16[256,1664]{1,0:T(8,128)(2,1)S(1)} collective-permute-done((bf16[256,1664]{1,0:T(8,128)(2,1)S(1)}, bf16[256,1664]{1,0:T(8,128)(2,1)S(1)}, u32[]{:S(2)}, u32[]{:S(2)}) %collective-permute-start) | collective-permute-done | bytes 852000 | tf_op jit(solution)/shard_map/ppermute | solution.py:84
  124.2 7.7 collective-permute-done.2
  136.4 7.5 collective-permute-done.4.refs_3_
  143.9 7.9 collective-permute-start.5
  154.0 9.4 %collective-permute-done.5.refs_1_ = bf16[2,256,512]{2,1,0:T(8,128)(2,1)S(1)} collective-permute-done((bf16[2,256,512]{2,1,0:T(8,128)(2,1)S(1)}, bf16[2,256,512]{2,1,0:T(8,128)(2,1)S(1)}, u32[]{:S(2)}, u32[]{:S(2)}) %collective-permute-start.5) | collective-permute-done | bytes 524320 | tf_op jit(solution)/shard_map/ppermute | solution.py:61
  163.4 11.2 %collective-permute-done.6.refs_2_ = bf16[2,256,512]{2,1,0:T(8,128)(2,1)} collective-permute-done((bf16[2,256,512]{2,1,0:T(8,128)(2,1)S(1)}, bf16[2,256,512]{2,1,0:T(8,128)(2,1)}, u32[]{:S(2)}, u32[]{:S(2)}) %collective-permute-start.6) | collective-permute-done | bytes 524320 | tf_op jit(solution)/shard_map/ppermute | solution.py:61
  178.6 37.6 %all-to-all-start.1 = ((bf16[32,48,512]{2,1,0:T(8,128)(2,1)}), bf16[32,48,512]{2,1,0:T(8,128)(2,1)}, u32[]{:S(2)}, u32[]{:S(2)}) async-start(bf16[32,48,512]{2,1,0:T(8,128)(2,1)} %bitcast.19), calls=%async_computation.1 | async-start | bytes 3145728 | tf_op jit(solution)/shard_map/all_to_all | solution.py:1114
  219.7 44.5 %collective-permute-done.8 = bf16[2,128,1664]{2,1,0:T(8,128)(2,1)S(1)} collective-permute-done((bf16[2,128,1664]{2,1,0:T(8,128)(2,1)}, bf16[2,128,1664]{2,1,0:T(8,128)(2,1)S(1)}, u32[]{:S(2)}, u32[]{:S(2)}) %collective-permute-start.8) | collective-permute-done | bytes 852000 | tf_op jit(solution)/shard_map/ppermute | solution.py:45
  271.2 16.2 %attend.1 = (bf16[256,1536]{1,0:T(8,128)(2,1)}, f32[4,8,256]{2,1,0:T(8,128)}) custom-call(s32[1,256]{1,0:T(1,128)} %bitcast.205, bf16[256,1536]{1,0:T(8,128)(2,1)} %project_queries.1.query_ref, bf16[2,256,512]{2,1,0:T(8,128)(2,1)} %copy-done.21, bf16[2,256,512]{2,1,0:T(8,128)(2,1)} %copy-done.23, bf16[2,256,512]{2,1,0:T(8,128)(2,1)} %collective-permute-done.6.refs_2_, ...), custom_call_target="tpu_custom_call" | custom-call | flops 2013265920 | bytes 4194304 | tf_op jit(solution)/shard_map/attend/pallas_call | solution.py:808
  299.0 8.2 %collective-permute-done.9 = bf16[128,1536]{1,0:T(8,128)(2,1)S(1)} collective-permute-done((bf16[128,1536]{1,0:T(8,128)(2,1)}, bf16[128,1536]{1,0:T(8,128)(2,1)S(1)}, u32[]{:S(2)}, u32[]{:S(2)}) %collective-permute-start.9) | collective-permute-done | bytes 393248 | tf_op jit(solution)/shard_map/ppermute | solution.py:45
  310.1 6.2 collective-permute-done.11
  319.9 15.1 %collective-permute-done.14 = bf16[2,128,1536]{2,1,0:T(8,128)(2,1)S(1)} collective-permute-done((bf16[2,128,1536]{2,1,0:T(8,128)(2,1)S(1)}, bf16[2,128,1536]{2,1,0:T(8,128)(2,1)S(1)}, u32[]{:S(2)}, u32[]{:S(2)}) %collective-permute-start.14) | collective-permute-done | bytes 786464 | tf_op jit(solution)/shard_map/ppermute | solution.py:45
  340.5 15.3 %experts.4 = (bf16[2048,512]{1,0:T(8,128)(2,1)}, bf16[1024,1024]{1,0:T(8,128)(2,1)}, bf16[1024,1664]{1,0:T(8,128)(2,1)}) custom-call(s32[4]{0:T(128)} %get-tuple-element.368.order_ref, s32[1]{0:T(128)} %bitcast.10.expert_ref, bf16[1024,1536]{1,0:T(8,128)(2,1)} %bitcast.28.input_ref.refs_0_, bf16[2048,1664]{1,0:T(8,128)(2,1)} %all-gather.8.cloned.1.call-done.grad_ref.refs_0_, ...), custom_call_target="tpu_custom_call" | custom-call | flops 8053063680 | bytes 14155776 | tf_op jit(solution)/shard_map/experts/pallas_call | solution.py:979
  360.2 15.3 %experts.5 = (bf16[2048,512]{1,0:T(8,128)(2,1)}, bf16[1024,1024]{1,0:T(8,128)(2,1)}, bf16[1024,1664]{1,0:T(8,128)(2,1)}) custom-call(s32[4]{0:T(128)} %get-tuple-element.367.order_ref, s32[1]{0:T(128)} %bitcast.10.expert_ref, bf16[1024,1536]{1,0:T(8,128)(2,1)} %collective-permute-done.15.input_ref.refs_2_, ...), custom_call_target="tpu_custom_call", output_to_operand_aliasing={{0}: (8, {})} | custom-call | flops 8053063680 | bytes 14155776 | tf_op jit(solution)/shard_map/experts/pallas_call | solution.py:979
  385.4 15.5 %experts.6 = (bf16[2048,512]{1,0:T(8,128)(2,1)}, bf16[1024,1024]{1,0:T(8,128)(2,1)}, bf16[1024,1664]{1,0:T(8,128)(2,1)}) custom-call(s32[4]{0:T(128)} %iota.46.order_ref, s32[1]{0:T(128)} %bitcast.10.expert_ref, bf16[1024,1536]{1,0:T(8,128)(2,1)} %bitcast.40.input_ref.refs_4_, bf16[2048,1664]{1,0:T(8,128)(2,1)} %pad_maximum_fusion.grad_ref.refs_2_, ...), custom_call_target="tpu_custom_call" | custom-call | flops 8053063680 | bytes 14155776 | tf_op jit(solution)/shard_map/experts/pallas_call | solution.py:979
  407.0 15.2 %experts.7 = (bf16[2048,512]{1,0:T(8,128)(2,1)}, bf16[1024,1024]{1,0:T(8,128)(2,1)}, bf16[1024,1664]{1,0:T(8,128)(2,1)}) custom-call(s32[4]{0:T(128)} %iota_add_fusion.1.order_ref, s32[1]{0:T(128)} %bitcast.10.expert_ref, bf16[1024,1536]{1,0:T(8,128)(2,1)} %collective-permute-done.20.input_ref.refs_6_, ...), custom_call_target="tpu_custom_call", output_to_operand_aliasing={{0}: (8, {})} | custom-call | flops 8053063680 | bytes 14155776 | tf_op jit(solution)/shard_map/experts/pallas_call | solution.py:979
  425.6 18.1 %expert_shares.1 = bf16[4096,1536]{1,0:T(8,128)(2,1)} custom-call(s32[16]{0:T(128)} %pad_add_fusion.orders_ref, bf16[2048,512]{1,0:T(8,128)(2,1)} %get-tuple-element.217.refs_0_.refs_1_, bf16[2048,512]{1,0:T(8,128)(2,1)} %get-tuple-element.218.refs_1_.refs_3_, bf16[1536,512]{1,0:T(8,128)(2,1)} %bitcast.30.down_ref.refs_2_), custom_call_target="tpu_custom_call" | custom-call | flops 6442450944 | bytes 18350080 | tf_op jit(solution)/shard_map/expert_shares/pallas_call | solution.py:1024
  448.1 10.3 %collective-permute-done.24 = bf16[128,1664]{1,0:T(8,128)(2,1)S(1)} collective-permute-done((bf16[128,1664]{1,0:T(8,128)(2,1)S(1)}, bf16[128,1664]{1,0:T(8,128)(2,1)S(1)}, u32[]{:S(2)}, u32[]{:S(2)}) %collective-permute-start.24) | collective-permute-done | bytes 426016 | tf_op jit(solution)/shard_map/ppermute | solution.py:45
  462.1 20.9 %up_terms.1 = bf16[1536,1024]{1,0:T(8,128)(2,1)} custom-call(bf16[1024,1536]{1,0:T(8,128)(2,1)} %bitcast.28.input_ref.refs_0_, bf16[1024,1024]{1,0:T(8,128)(2,1)} %get-tuple-element.204.refs_1_, bf16[1024,1536]{1,0:T(8,128)(2,1)} %collective-permute-done.15.input_ref.refs_2_, bf16[1024,1024]{1,0:T(8,128)(2,1)} %get-tuple-element.206.refs_3_, ...), custom_call_target="tpu_custom_call" | custom-call | flops 12884901888 | bytes 24117248 | tf_op jit(solution)/shard_map/up_terms/pallas_call | solution.py:1059
  492.3 11.8 %down_terms.1 = bf16[1536,512]{1,0:T(8,128)(2,1)} custom-call(bf16[2048,1664]{1,0:T(8,128)(2,1)} %all-gather.8.cloned.1.call-done.grad_ref.refs_0_, bf16[2048,512]{1,0:T(8,128)(2,1)} %get-tuple-element.217.refs_0_.refs_1_, bf16[2048,1664]{1,0:T(8,128)(2,1)} %pad_maximum_fusion.grad_ref.refs_2_, bf16[2048,512]{1,0:T(8,128)(2,1)} %get-tuple-element.218.refs_1_.refs_3_), custom_call_target="tpu_custom_call" | custom-call | flops 6442450944 | bytes 18350080 | tf_op jit(solution)/shard_map/down_terms/pallas_call | solution.py:1059
  516.6 8.3 %collective-permute-done.31.refs_0_ = bf16[256,1664]{1,0:T(8,128)(2,1)S(1)} collective-permute-done((bf16[256,1664]{1,0:T(8,128)(2,1)S(1)}, bf16[256,1664]{1,0:T(8,128)(2,1)S(1)}, u32[]{:S(2)}, u32[]{:S(2)}) %collective-permute-start.31) | collective-permute-done | bytes 852000 | tf_op jit(solution)/shard_map/ppermute | solution.py:84
  532.7 7.9 return_to_attention.1
  540.6 27.9 %attend_backward.1 = (bf16[256,1536]{1,0:T(8,128)(2,1)}, bf16[2,256,512]{2,1,0:T(8,128)(2,1)}, bf16[2,256,512]{2,1,0:T(8,128)(2,1)}, bf16[2,256,512]{2,1,0:T(8,1...) custom-call(s32[1,256]{1,0:T(1,128)} %bitcast.206, bf16[256,1536]{1,0:T(8,128)(2,1)} %project_queries.1.query_ref, ...), custom_call_target="tpu_custom_call" | custom-call | flops 5033164800 | bytes 8388608 | tf_op jit(solution)/shard_map/attend_backward/pallas_call | solution.py:888
  568.4 9.7 %weight_terms.1 = bf16[1536,3072]{1,0:T(8,128)(2,1)} custom-call(bf16[256,1536]{1,0:T(8,128)(2,1)} %get-tuple-element.134.normed_ref.refs_0_, bf16[256,1536]{1,0:T(8,128)(2,1)} %get-tuple-element.231.refs_1_.refs_0_, bf16[256,1536]{1,0:T(8,128)(2,1)} %get-tuple-element.233.refs_2_, bf16[256,1536]{1,0:T(8,128)(2,1)} %get-tuple-element.146.mixture_ref.refs_3_), custom_call_target="tpu_custom_call" | custom-call | flops 2415919104 | bytes 11010048 | tf_op jit(solution)/shard_map/weight_terms/pallas_call | solution.py:577
  578.2 57.7 %all-to-all-done.2 = bf16[32,48,1536]{2,1,0:T(8,128)(2,1)} async-done(((bf16[32,48,1536]{2,1,0:T(8,128)(2,1)}), bf16[32,48,1536]{2,1,0:T(8,128)(2,1)}, u32[]{:S(2)}, u32[]{:S(2)}) %all-to-all-start.2) | async-done | bytes 4718624 | tf_op jit(solution)/shard_map/all_to_all | solution.py:1114
  645.5 13.5 %collective-permute-done.34.refs_3_ = bf16[2,256,512]{2,1,0:T(8,128)(2,1)S(1)} collective-permute-done((bf16[2,256,512]{2,1,0:T(8,128)(2,1)}, bf16[2,256,512]{2,1,0:T(8,128)(2,1)S(1)}, u32[]{:S(2)}, u32[]{:S(2)}) %collective-permute-start.34) | collective-permute-done | bytes 524320 | tf_op jit(solution)/shard_map/ppermute | solution.py:61
  659.1 44.0 %collective-permute-done.35.refs_4_ = bf16[2,256,512]{2,1,0:T(8,128)(2,1)} collective-permute-done((bf16[2,256,512]{2,1,0:T(8,128)(2,1)}, bf16[2,256,512]{2,1,0:T(8,128)(2,1)}, u32[]{:S(2)}, u32[]{:S(2)}) %collective-permute-start.35) | collective-permute-done | bytes 524320 | tf_op jit(solution)/shard_map/ppermute | solution.py:61
  703.1 13.0 %leave.1 = (f32[256,1536]{1,0:T(8,128)}, bf16[4,4,48,1152]{3,2,1,0:T(8,128)(2,1)}, bf16[4,4,48,1152]{3,2,1,0:T(8,128)(2,1)}) custom-call(s32[2]{0:T(128)} %pad_add_fusion.1.place_ref, f32[256,128]{1,0:T(8,128)} %get-tuple-element.369.cosine_ref, f32[256,128]{1,0:T(8,128)} %get-tuple-element.370.sine_ref, bf16[256,1536]{1,0:T(8,128)(2,1)} %hidden_ref.4, ...), custom_call_target="tpu_custom_call" | custom-call | flops 2818572288 | bytes 18087936 | tf_op jit(solution)/shard_map/leave/pallas_call | solution.py:683
  744.2 8.8 %collective-permute-done.39 = bf16[2,2,48,1152]{3,2,1,0:T(8,128)(2,1)S(1)} collective-permute-done((bf16[2,2,48,1152]{3,2,1,0:T(8,128)(2,1)S(1)}, bf16[2,2,48,1152]{3,2,1,0:T(8,128)(2,1)S(1)}, u32[]{:S(2)}, u32[]{:S(2)}) %collective-permute-start.39) | collective-permute-done | bytes 442400 | tf_op jit(solution)/shard_map/ppermute | solution.py:45
  775.5 6.0 collective-permute-done.43
  (239 shorter events, 199.3 us)
Async XLA Ops:
  7.2 93.1 %all-gather.4.cloned.1.call-start = ((), (), s32[]{:S(2)}) async-start(), calls=%async_computation.5 | async-start | bytes 3649536 | tf_op jit(solution)/shard_map/all_gather | solution.py:1128
  11.1 254.3 %all-gather.6.cloned.1.call-start = ((), (), s32[]{:S(2)}) async-start(), calls=%async_computation.6 | async-start | bytes 9732096 | tf_op jit(solution)/shard_map/all_gather | solution.py:1150
  20.0 96.1 %all-to-all-start = ((bf16[32,48,1024]{2,1,0:T(8,128)(2,1)}), bf16[32,48,1024]{2,1,0:T(8,128)(2,1)}, u32[]{:S(2)}, u32[]{:S(2)}) async-start(bf16[32,48,1024]{2,1,0:T(8,128)(2,1)} %bitcast.5), calls=%async_computation | async-start | bytes 6291456 | tf_op jit(solution)/shard_map/all_to_all | solution.py:1114
  27.4 313.1 %all-gather.8.cloned.1.call-start = ((), (), s32[]{:S(2)}) async-start(), calls=%async_computation.7 | async-start | bytes 7667712 | tf_op jit(solution)/shard_map/all_gather | solution.py:1176
  27.5 88.6 %collective-permute-start = (bf16[256,1664]{1,0:T(8,128)(2,1)S(1)}, bf16[256,1664]{1,0:T(8,128)(2,1)S(1)}, u32[]{:S(2)}, u32[]{:S(2)}) collective-permute-start(bf16[256,1664]{1,0:T(8,128)(2,1)S(1)} %concatenate.51), channel_id=1, source_target_pairs={{0,8},{8,0},{16,24},{24,16},{1,9},{9,1},{17,25},{25,17},{2,10},{10... | collective-permute-start | bytes 2555912 | tf_op jit(solution)/shard_map/ppermute | solution.py:84
  120.8 23.1 %collective-permute-start.4 = (bf16[2,256,512]{2,1,0:T(8,128)(2,1)}, bf16[2,256,512]{2,1,0:T(8,128)(2,1)S(1)}, u32[]{:S(2)}, u32[]{:S(2)}) collective-permute-start(bf16[2,256,512]{2,1,0:T(8,128)(2,1)} %get-tuple-element.145.refs_4_), channel_id=1, source_target_pairs={{0,8},{8,16},{16,24},{24,1},{1,9},{9,17},{17,25},{25,2},{2,10},{10... | collective-permute-start | bytes 1572872 | tf_op jit(solution)/shard_map/ppermute | solution.py:61
  143.9 19.5 %collective-permute-start.5 = (bf16[2,256,512]{2,1,0:T(8,128)(2,1)S(1)}, bf16[2,256,512]{2,1,0:T(8,128)(2,1)S(1)}, u32[]{:S(2)}, u32[]{:S(2)}) collective-permute-start(bf16[2,256,512]{2,1,0:T(8,128)(2,1)S(1)} %copy-done.20), channel_id=1, source_target_pairs={{0,24},{8,1},{16,9},{24,17},{1,25},{9,2},{17,10},{25,18},{2,26},{1... | collective-permute-start | bytes 1572872 | tf_op jit(solution)/shard_map/ppermute | solution.py:61
  151.8 22.8 %collective-permute-start.6 = (bf16[2,256,512]{2,1,0:T(8,128)(2,1)S(1)}, bf16[2,256,512]{2,1,0:T(8,128)(2,1)}, u32[]{:S(2)}, u32[]{:S(2)}) collective-permute-start(bf16[2,256,512]{2,1,0:T(8,128)(2,1)S(1)} %copy-done.20), channel_id=1, source_target_pairs={{0,16},{8,24},{16,1},{24,9},{1,17},{9,25},{17,2},{25,10},{2,18},{1... | collective-permute-start | bytes 1572872 | tf_op jit(solution)/shard_map/ppermute | solution.py:61
  178.6 116.8 %all-to-all-start.1 = ((bf16[32,48,512]{2,1,0:T(8,128)(2,1)}), bf16[32,48,512]{2,1,0:T(8,128)(2,1)}, u32[]{:S(2)}, u32[]{:S(2)}) async-start(bf16[32,48,512]{2,1,0:T(8,128)(2,1)} %bitcast.19), calls=%async_computation.1 | async-start | bytes 3145728 | tf_op jit(solution)/shard_map/all_to_all | solution.py:1114
  216.3 419.6 %reduce-scatter.3.cloned.1.call-start = ((), (), s32[]{:S(2)}) async-start(), calls=%async_computation.8 | async-start | bytes 14155776 | tf_op jit(solution)/shard_map/reduce_scatter | solution.py:1258
  216.5 47.7 %collective-permute-start.8 = (bf16[2,128,1664]{2,1,0:T(8,128)(2,1)}, bf16[2,128,1664]{2,1,0:T(8,128)(2,1)S(1)}, u32[]{:S(2)}, u32[]{:S(2)}) collective-permute-start(bf16[2,128,1664]{2,1,0:T(8,128)(2,1)} %get-tuple-element.151), channel_id=1, source_target_pairs={{0,2},{1,3},{2,0},{3,1},{4,6},{5,7},{6,4},{7,5},{8,10},{9,11},{10,... | collective-permute-start | bytes 2555912 | tf_op jit(solution)/shard_map/ppermute | solution.py:45
  218.2 45.9 %collective-permute-start.7 = (bf16[2,128,1664]{2,1,0:T(8,128)(2,1)S(1)}, bf16[2,128,1664]{2,1,0:T(8,128)(2,1)S(1)}, u32[]{:S(2)}, u32[]{:S(2)}) collective-permute-start(bf16[2,128,1664]{2,1,0:T(8,128)(2,1)S(1)} %get-tuple-element.150), channel_id=1, source_target_pairs={{0,4},{1,5},{2,6},{3,7},{4,0},{5,1},{6,2},{7,3},{8,12},{9,13},{10,... | collective-permute-start | bytes 2555912 | tf_op jit(solution)/shard_map/ppermute | solution.py:45
  295.5 20.8 %collective-permute-start.12 = (bf16[1024,1664]{1,0:T(8,128)(2,1)S(1)}, bf16[1024,1664]{1,0:T(8,128)(2,1)S(1)}, u32[]{:S(2)}, u32[]{:S(2)}) collective-permute-start(bf16[1024,1664]{1,0:T(8,128)(2,1)S(1)} %bitcast.185), channel_id=1, source_target_pairs={{0,1},{1,0},{2,3},{3,2},{4,5},{5,4},{6,7},{7,6},{8,9},{9,8},{10,11... | collective-permute-start | bytes 10223624 | tf_op jit(solution)/shard_map/ppermute | solution.py:45
  296.4 19.8 %collective-permute-start.11 = (bf16[256,1536]{1,0:T(8,128)(2,1)}, bf16[256,1536]{1,0:T(8,128)(2,1)S(1)}, u32[]{:S(2)}, u32[]{:S(2)}) collective-permute-start(bf16[256,1536]{1,0:T(8,128)(2,1)} %get-tuple-element.155.normed_ref.normed_two_ref), channel_id=1, source_target_pairs={{0,8},{8,0},{16,24},{24,16},{1,9},{9,1},{17,25},{25,17},{2,10},{10... | collective-permute-start | bytes 2359304 | tf_op jit(solution)/shard_map/ppermute | solution.py:84
  316.3 18.8 %collective-permute-start.14 = (bf16[2,128,1536]{2,1,0:T(8,128)(2,1)S(1)}, bf16[2,128,1536]{2,1,0:T(8,128)(2,1)S(1)}, u32[]{:S(2)}, u32[]{:S(2)}) collective-permute-start(bf16[2,128,1536]{2,1,0:T(8,128)(2,1)S(1)} %get-tuple-element.158), channel_id=1, source_target_pairs={{0,2},{1,3},{2,0},{3,1},{4,6},{5,7},{6,4},{7,5},{8,10},{9,11},{10,... | collective-permute-start | bytes 2359304 | tf_op jit(solution)/shard_map/ppermute | solution.py:45
  317.4 18.5 %collective-permute-start.13 = (bf16[2,128,1536]{2,1,0:T(8,128)(2,1)S(1)}, bf16[2,128,1536]{2,1,0:T(8,128)(2,1)S(1)}, u32[]{:S(2)}, u32[]{:S(2)}) collective-permute-start(bf16[2,128,1536]{2,1,0:T(8,128)(2,1)S(1)} %get-tuple-element.157), channel_id=1, source_target_pairs={{0,4},{1,5},{2,6},{3,7},{4,0},{5,1},{6,2},{7,3},{8,12},{9,13},{10,... | collective-permute-start | bytes 2359304 | tf_op jit(solution)/shard_map/ppermute | solution.py:45
  358.1 19.5 %collective-permute-start.18 = (bf16[2,128,1536]{2,1,0:T(8,128)(2,1)S(1)}, bf16[2,128,1536]{2,1,0:T(8,128)(2,1)S(1)}, u32[]{:S(2)}, u32[]{:S(2)}) collective-permute-start(bf16[2,128,1536]{2,1,0:T(8,128)(2,1)S(1)} %get-tuple-element.172), channel_id=1, source_target_pairs={{0,4},{1,5},{2,6},{3,7},{4,0},{5,1},{6,2},{7,3},{8,12},{9,13},{10,... | collective-permute-start | bytes 2359304 | tf_op jit(solution)/shard_map/ppermute | solution.py:45
  359.1 19.1 %collective-permute-start.19 = (bf16[2,128,1536]{2,1,0:T(8,128)(2,1)S(1)}, bf16[2,128,1536]{2,1,0:T(8,128)(2,1)S(1)}, u32[]{:S(2)}, u32[]{:S(2)}) collective-permute-start(bf16[2,128,1536]{2,1,0:T(8,128)(2,1)S(1)} %get-tuple-element.173), channel_id=1, source_target_pairs={{0,2},{1,3},{2,0},{3,1},{4,6},{5,7},{6,4},{7,5},{8,10},{9,11},{10,... | collective-permute-start | bytes 2359304 | tf_op jit(solution)/shard_map/ppermute | solution.py:45
  380.4 20.4 %collective-permute-start.21 = (bf16[1024,1664]{1,0:T(8,128)(2,1)}, bf16[1024,1664]{1,0:T(8,128)(2,1)}, u32[]{:S(2)}, u32[]{:S(2)}) collective-permute-start(bf16[1024,1664]{1,0:T(8,128)(2,1)} %get-tuple-element.179), channel_id=1, source_target_pairs={{0,1},{1,0},{2,3},{3,2},{4,5},{5,4},{6,7},{7,6},{8,9},{9,8},{10,11... | collective-permute-start | bytes 10223624 | tf_op jit(solution)/shard_map/ppermute | solution.py:45
  380.4 20.4 %collective-permute-start.20 = (bf16[1024,1536]{1,0:T(8,128)(2,1)}, bf16[1024,1536]{1,0:T(8,128)(2,1)}, u32[]{:S(2)}, u32[]{:S(2)}) collective-permute-start(bf16[1024,1536]{1,0:T(8,128)(2,1)} %bitcast.40.input_ref.refs_4_), channel_id=1, source_target_pairs={{0,1},{1,0},{2,3},{3,2},{4,5},{5,4},{6,7},{7,6},{8,9},{9,8},{10,11... | collective-permute-start | bytes 9437192 | tf_op jit(solution)/shard_map/ppermute | solution.py:45
  403.8 20.9 %collective-permute-start.22 = (bf16[2,128,1664]{2,1,0:T(8,128)(2,1)S(1)}, bf16[2,128,1664]{2,1,0:T(8,128)(2,1)}, u32[]{:S(2)}, u32[]{:S(2)}) collective-permute-start(bf16[2,128,1664]{2,1,0:T(8,128)(2,1)S(1)} %slice_bitcast_fusion.9), channel_id=1, source_target_pairs={{0,2},{1,3},{2,0},{3,1},{4,6},{5,7},{6,4},{7,5},{8,10},{9,11},{10,... | collective-permute-start | bytes 2555912 | tf_op jit(solution)/shard_map/ppermute | solution.py:45
  405.0 20.5 %collective-permute-start.23 = (bf16[2,128,1664]{2,1,0:T(8,128)(2,1)S(1)}, bf16[2,128,1664]{2,1,0:T(8,128)(2,1)}, u32[]{:S(2)}, u32[]{:S(2)}) collective-permute-start(bf16[2,128,1664]{2,1,0:T(8,128)(2,1)S(1)} %slice_bitcast_fusion.8), channel_id=1, source_target_pairs={{0,4},{1,5},{2,6},{3,7},{4,0},{5,1},{6,2},{7,3},{8,12},{9,13},{10,... | collective-permute-start | bytes 2555912 | tf_op jit(solution)/shard_map/ppermute | solution.py:45
  460.5 27.4 %collective-permute-start.27 = (bf16[2,128,1664]{2,1,0:T(8,128)(2,1)S(1)}, bf16[2,128,1664]{2,1,0:T(8,128)(2,1)S(1)}, u32[]{:S(2)}, u32[]{:S(2)}) collective-permute-start(bf16[2,128,1664]{2,1,0:T(8,128)(2,1)S(1)} %slice_bitcast_fusion.4), channel_id=1, source_target_pairs={{0,2},{1,3},{2,0},{3,1},{4,6},{5,7},{6,4},{7,5},{8,10},{9,11},{10,... | collective-permute-start | bytes 2555912 | tf_op jit(solution)/shard_map/ppermute | solution.py:45
  461.2 28.4 %collective-permute-start.28 = (bf16[2,128,1664]{2,1,0:T(8,128)(2,1)S(1)}, bf16[2,128,1664]{2,1,0:T(8,128)(2,1)S(1)}, u32[]{:S(2)}, u32[]{:S(2)}) collective-permute-start(bf16[2,128,1664]{2,1,0:T(8,128)(2,1)S(1)} %slice_bitcast_fusion.3), channel_id=1, source_target_pairs={{0,4},{1,5},{2,6},{3,7},{4,0},{5,1},{6,2},{7,3},{8,12},{9,13},{10,... | collective-permute-start | bytes 2555912 | tf_op jit(solution)/shard_map/ppermute | solution.py:45
  490.1 19.7 %collective-permute-start.29 = (bf16[128,1664]{1,0:T(8,128)(2,1)S(1)}, bf16[128,1664]{1,0:T(8,128)(2,1)S(1)}, u32[]{:S(2)}, u32[]{:S(2)}) collective-permute-start(bf16[128,1664]{1,0:T(8,128)(2,1)S(1)} %slice_bitcast_fusion.16), channel_id=1, source_target_pairs={{0,4},{1,5},{2,6},{3,7},{4,0},{5,1},{6,2},{7,3},{8,12},{9,13},{10,... | collective-permute-start | bytes 1277960 | tf_op jit(solution)/shard_map/ppermute | solution.py:45
  491.7 19.3 %collective-permute-start.30 = (bf16[128,1664]{1,0:T(8,128)(2,1)S(1)}, bf16[128,1664]{1,0:T(8,128)(2,1)S(1)}, u32[]{:S(2)}, u32[]{:S(2)}) collective-permute-start(bf16[128,1664]{1,0:T(8,128)(2,1)S(1)} %slice_bitcast_fusion.15), channel_id=1, source_target_pairs={{0,2},{1,3},{2,0},{3,1},{4,6},{5,7},{6,4},{7,5},{8,10},{9,11},{10,... | collective-permute-start | bytes 1277960 | tf_op jit(solution)/shard_map/ppermute | solution.py:45
  525.8 110.0 %all-to-all-start.2 = ((bf16[32,48,1536]{2,1,0:T(8,128)(2,1)}), bf16[32,48,1536]{2,1,0:T(8,128)(2,1)}, u32[]{:S(2)}, u32[]{:S(2)}) async-start(bf16[32,48,1536]{2,1,0:T(8,128)(2,1)} %bitcast.178), calls=%async_computation.3 | async-start | bytes 9437184 | tf_op jit(solution)/shard_map/all_to_all | solution.py:1114
  530.5 252.5 %reduce-scatter.5.cloned.1.call-start = ((), (), s32[]{:S(2)}) async-start(), calls=%async_computation.9 | async-start | bytes 9732096 | tf_op jit(solution)/shard_map/reduce_scatter | solution.py:1295
  638.3 20.7 %collective-permute-start.34 = (bf16[2,256,512]{2,1,0:T(8,128)(2,1)}, bf16[2,256,512]{2,1,0:T(8,128)(2,1)S(1)}, u32[]{:S(2)}, u32[]{:S(2)}) collective-permute-start(bf16[2,256,512]{2,1,0:T(8,128)(2,1)} %get-tuple-element.242), channel_id=1, source_target_pairs={{24,0},{1,8},{9,16},{17,24},{25,1},{2,9},{10,17},{18,25},{26,2},{3... | collective-permute-start | bytes 1572872 | tf_op jit(solution)/shard_map/ppermute | solution.py:61
  639.6 63.4 %collective-permute-start.35 = (bf16[2,256,512]{2,1,0:T(8,128)(2,1)}, bf16[2,256,512]{2,1,0:T(8,128)(2,1)}, u32[]{:S(2)}, u32[]{:S(2)}) collective-permute-start(bf16[2,256,512]{2,1,0:T(8,128)(2,1)} %get-tuple-element.243), channel_id=1, source_target_pairs={{16,0},{24,8},{1,16},{9,24},{17,1},{25,9},{2,17},{10,25},{18,2},{2... | collective-permute-start | bytes 1572872 | tf_op jit(solution)/shard_map/ppermute | solution.py:61
  640.9 62.1 %collective-permute-start.36 = (bf16[2,256,512]{2,1,0:T(8,128)(2,1)}, bf16[2,256,512]{2,1,0:T(8,128)(2,1)}, u32[]{:S(2)}, u32[]{:S(2)}) collective-permute-start(bf16[2,256,512]{2,1,0:T(8,128)(2,1)} %get-tuple-element.244), channel_id=1, source_target_pairs={{8,0},{16,8},{24,16},{1,24},{9,1},{17,9},{25,17},{2,25},{10,2},{18... | collective-permute-start | bytes 1572872 | tf_op jit(solution)/shard_map/ppermute | solution.py:61
  642.2 79.3 %collective-permute-start.32 = (bf16[256,1536]{1,0:T(8,128)(2,1)S(1)}, bf16[256,1536]{1,0:T(8,128)(2,1)S(1)}, u32[]{:S(2)}, u32[]{:S(2)}) collective-permute-start(bf16[256,1536]{1,0:T(8,128)(2,1)S(1)} %slice.225), channel_id=1, source_target_pairs={{0,8},{8,0},{16,24},{24,16},{1,9},{9,1},{17,25},{25,17},{2,10},{10... | collective-permute-start | bytes 2359304 | tf_op jit(solution)/shard_map/ppermute | solution.py:84
  (45 other events, 651.9 us)
Sparse Core Ops, SparseCore 0:
  11.5 88.7 all-gather.3
  103.8 109.4 all-gather.5
  215.8 67.6 all-gather.7
  443.8 152.1 reduce-scatter.2
  601.7 178.0 reduce-scatter.4

commit v4 on v3

--- a/solution.py
+++ b/solution.py
@@ -1157,7 +1157,7 @@
     clock.tick(kv_flows[0], kv_flows[-1], *grad_flows)
     clock.tick(*kv_flows[1:-1], *grad_flows)
     key_values = [flow.value for flow in kv_flows[::-1]] + [own_kv]
-    down_flow = expert_rows(after(expert_output, kv_flows[-1].value))
+    down_flow = expert_rows(after(expert_output, *clock.last))
     Clock().tick(down_flow)
     w_up = up_flow.value.reshape(MODEL_WIDTH, 2 * FF)
     w_down = down_flow.value.reshape(MODEL_WIDTH, FF)

time: 799 us -> 782 us (0.979)
  waiting for transfers between devices: 388 us -> 373 us
    all_to_all x3, starting transfers between devices: 49.7 us -> 24 us  [spread(): return lax.all_to_all(block, axes, split_axis=0, concat_axis=0, tiled=True)]
    ppermute x30, waiting for transfers between devices: 135 us -> 112 us  [swap(): return lax.ppermute(block, 'seq', [(i, i ^ mask) for i in range(count)])]
    ppermute x30, starting transfers between devices: 29.2 us -> 52.2 us  [swap(): return lax.ppermute(block, 'seq', [(i, i ^ mask) for i in range(count)])]
  transfers between devices with their start and end apart: 53 -> 53, of which waited for: 35 -> 36; matrix products, arithmetic and copies ran while one was open for 7% -> 8% of each run, Pallas kernels for 23% -> 24%
where the time goes in v4:
time: 782 us; the launch traced here: 775 us
  waiting for transfers between devices  373 us (48%)
  Pallas kernels  202 us (26%)
  starting transfers between devices  109 us (14%)
  local copies, waits for them, and re-layouts  38.4 us (5%)
  other arithmetic  37.6 us (5%)
  between operations  14.8 us (2%)
    ppermute x30, waiting for transfers between devices, swap(): return lax.ppermute(block, 'seq', [(i, i ^ mask) for i in range(count)])  112 us
    ppermute x8, waiting for transfers between devices, along_stream(): return lax.ppermute(block, ('head', 'seq'), route)  86 us
    all_gather x1, waiting for transfers between devices, shards(): w_small = lax.all_gather(small, ('head', 'seq'), axis=0, tiled=True)  68.6 us
    all_to_all x3, waiting for transfers between devices, spread(): return lax.all_to_all(block, axes, split_axis=0, concat_axis=0, tiled=True)  62.6 us
    pallas_call x4, Pallas kernels, experts(): pl.pallas_call(kernel, grid_spec=pltpu.PrefetchScalarGridSpec(num_scalar_...  61.2 us
    ppermute x30, starting transfers between devices, swap(): return lax.ppermute(block, 'seq', [(i, i ^ mask) for i in range(count)])  52.2 us
    ppermute x4, waiting for transfers between devices, swap_head(): return lax.ppermute(block, 'head', [(i, i ^ mask) for i in range(count)])  34 us
    pallas_call x2, Pallas kernels, expert_terms(): pl.pallas_call(kernel, grid=(MODEL_WIDTH // tile,), in_specs=in_specs, ou...  32.5 us
  transfers between devices with their start and end apart: 53, of which 36 were waited for; matrix products, arithmetic and copies ran while one was open for 8% of the time, Pallas kernels for 24%

profile of v4, /device:TPU:0, one launch (start us, length us, event | category | flops | bytes accessed | tf_op | source)
XLA Modules:
  0.0 775.0 jit_solution(879096661256572179)
XLA Ops:
  20.0 7.4 all-to-all-start
  31.7 68.6 %all-gather.4.cloned.1.call-done.weight_ref.router_ref.small_ref = bf16[1536,1152]{1,0:T(8,128)(2,1)} async-done(((bf16[48,1152]{1,0:T(8,128)(2,1)}), bf16[1536,1152]{1,0:T(8,128)(2,1)}) %all-gather.4.cloned.1.call-update) | async-done | bytes 3538960 | tf_op jit(solution)/shard_map/all_gather | solution.py:1128
  104.5 11.5 %collective-permute-done = bf16[256,1664]{1,0:T(8,128)(2,1)S(1)} collective-permute-done((bf16[256,1664]{1,0:T(8,128)(2,1)S(1)}, bf16[256,1664]{1,0:T(8,128)(2,1)S(1)}, u32[]{:S(2)}, u32[]{:S(2)}) %collective-permute-start) | collective-permute-done | bytes 852000 | tf_op jit(solution)/shard_map/ppermute | solution.py:84
  124.2 7.7 collective-permute-done.2
  135.5 8.4 %collective-permute-done.4.refs_3_ = bf16[2,256,512]{2,1,0:T(8,128)(2,1)S(1)} collective-permute-done((bf16[2,256,512]{2,1,0:T(8,128)(2,1)}, bf16[2,256,512]{2,1,0:T(8,128)(2,1)S(1)}, u32[]{:S(2)}, u32[]{:S(2)}) %collective-permute-start.4) | collective-permute-done | bytes 524320 | tf_op jit(solution)/shard_map/ppermute | solution.py:61
  143.9 7.9 %collective-permute-start.5 = (bf16[2,256,512]{2,1,0:T(8,128)(2,1)S(1)}, bf16[2,256,512]{2,1,0:T(8,128)(2,1)S(1)}, u32[]{:S(2)}, u32[]{:S(2)}) collective-permute-start(bf16[2,256,512]{2,1,0:T(8,128)(2,1)S(1)} %copy-done.22), channel_id=1, source_target_pairs={{0,24},{8,1},{16,9},{24,17},{1,25},{9,2},{17,10},{25,18},{2,26},{1... | collective-permute-start | bytes 1572872 | tf_op jit(solution)/shard_map/ppermute | solution.py:61
  154.0 9.4 %collective-permute-done.5.refs_1_ = bf16[2,256,512]{2,1,0:T(8,128)(2,1)S(1)} collective-permute-done((bf16[2,256,512]{2,1,0:T(8,128)(2,1)S(1)}, bf16[2,256,512]{2,1,0:T(8,128)(2,1)S(1)}, u32[]{:S(2)}, u32[]{:S(2)}) %collective-permute-start.5) | collective-permute-done | bytes 524320 | tf_op jit(solution)/shard_map/ppermute | solution.py:61
  164.3 10.4 %collective-permute-done.6.refs_2_ = bf16[2,256,512]{2,1,0:T(8,128)(2,1)} collective-permute-done((bf16[2,256,512]{2,1,0:T(8,128)(2,1)S(1)}, bf16[2,256,512]{2,1,0:T(8,128)(2,1)}, u32[]{:S(2)}, u32[]{:S(2)}) %collective-permute-start.6) | collective-permute-done | bytes 524320 | tf_op jit(solution)/shard_map/ppermute | solution.py:61
  174.7 24.6 %collective-permute-start.8 = (bf16[2,128,1664]{2,1,0:T(8,128)(2,1)S(1)}, bf16[2,128,1664]{2,1,0:T(8,128)(2,1)S(1)}, u32[]{:S(2)}, u32[]{:S(2)}) collective-permute-start(bf16[2,128,1664]{2,1,0:T(8,128)(2,1)S(1)} %get-tuple-element.151), channel_id=1, source_target_pairs={{0,2},{1,3},{2,0},{3,1},{4,6},{5,7},{6,4},{7,5},{8,10},{9,11},{10,... | collective-permute-start | bytes 2555912 | tf_op jit(solution)/shard_map/ppermute | solution.py:45
  202.6 16.9 %collective-permute-done.8 = bf16[2,128,1664]{2,1,0:T(8,128)(2,1)S(1)} collective-permute-done((bf16[2,128,1664]{2,1,0:T(8,128)(2,1)S(1)}, bf16[2,128,1664]{2,1,0:T(8,128)(2,1)S(1)}, u32[]{:S(2)}, u32[]{:S(2)}) %collective-permute-start.8) | collective-permute-done | bytes 852000 | tf_op jit(solution)/shard_map/ppermute | solution.py:45
  225.6 13.0 %all-to-all-start.1 = ((bf16[32,48,512]{2,1,0:T(8,128)(2,1)}), bf16[32,48,512]{2,1,0:T(8,128)(2,1)}, u32[]{:S(2)}, u32[]{:S(2)}) async-start(bf16[32,48,512]{2,1,0:T(8,128)(2,1)} %bitcast.19), calls=%async_computation.1 | async-start | bytes 3145728 | tf_op jit(solution)/shard_map/all_to_all | solution.py:1114
  247.4 16.2 %attend.1 = (bf16[256,1536]{1,0:T(8,128)(2,1)}, f32[4,8,256]{2,1,0:T(8,128)}) custom-call(s32[1,256]{1,0:T(1,128)} %bitcast.204, bf16[256,1536]{1,0:T(8,128)(2,1)} %project_queries.1.query_ref, bf16[2,256,512]{2,1,0:T(8,128)(2,1)} %copy-done.23, bf16[2,256,512]{2,1,0:T(8,128)(2,1)} %copy-done.25, bf16[2,256,512]{2,1,0:T(8,128)(2,1)} %collective-permute-done.6.refs_2_, ...), custom_call_target="tpu_custom_call" | custom-call | flops 2013265920 | bytes 4194304 | tf_op jit(solution)/shard_map/attend/pallas_call | solution.py:808
  279.3 8.9 %collective-permute-done.9 = bf16[128,1536]{1,0:T(8,128)(2,1)S(1)} collective-permute-done((bf16[128,1536]{1,0:T(8,128)(2,1)}, bf16[128,1536]{1,0:T(8,128)(2,1)S(1)}, u32[]{:S(2)}, u32[]{:S(2)}) %collective-permute-start.9) | collective-permute-done | bytes 393248 | tf_op jit(solution)/shard_map/ppermute | solution.py:45
  300.8 15.6 %collective-permute-done.14 = bf16[2,128,1536]{2,1,0:T(8,128)(2,1)S(1)} collective-permute-done((bf16[2,128,1536]{2,1,0:T(8,128)(2,1)S(1)}, bf16[2,128,1536]{2,1,0:T(8,128)(2,1)S(1)}, u32[]{:S(2)}, u32[]{:S(2)}) %collective-permute-start.14) | collective-permute-done | bytes 786464 | tf_op jit(solution)/shard_map/ppermute | solution.py:45
  322.5 15.3 %experts.4 = (bf16[2048,512]{1,0:T(8,128)(2,1)}, bf16[1024,1024]{1,0:T(8,128)(2,1)}, bf16[1024,1664]{1,0:T(8,128)(2,1)}) custom-call(s32[4]{0:T(128)} %get-tuple-element.368.order_ref, s32[1]{0:T(128)} %bitcast.10.expert_ref, bf16[1024,1536]{1,0:T(8,128)(2,1)} %bitcast.28.input_ref.refs_0_, bf16[2048,1664]{1,0:T(8,128)(2,1)} %all-gather.8.cloned.1.call-done.grad_ref.refs_0_, ...), custom_call_target="tpu_custom_call" | custom-call | flops 8053063680 | bytes 14155776 | tf_op jit(solution)/shard_map/experts/pallas_call | solution.py:979
  341.4 15.3 %experts.5 = (bf16[2048,512]{1,0:T(8,128)(2,1)}, bf16[1024,1024]{1,0:T(8,128)(2,1)}, bf16[1024,1664]{1,0:T(8,128)(2,1)}) custom-call(s32[4]{0:T(128)} %get-tuple-element.367.order_ref, s32[1]{0:T(128)} %bitcast.10.expert_ref, bf16[1024,1536]{1,0:T(8,128)(2,1)} %collective-permute-done.15.input_ref.refs_2_, ...), custom_call_target="tpu_custom_call", output_to_operand_aliasing={{0}: (8, {})} | custom-call | flops 8053063680 | bytes 14155776 | tf_op jit(solution)/shard_map/experts/pallas_call | solution.py:979
  366.8 15.5 %experts.6 = (bf16[2048,512]{1,0:T(8,128)(2,1)}, bf16[1024,1024]{1,0:T(8,128)(2,1)}, bf16[1024,1664]{1,0:T(8,128)(2,1)}) custom-call(s32[4]{0:T(128)} %iota.46.order_ref, s32[1]{0:T(128)} %bitcast.10.expert_ref, bf16[1024,1536]{1,0:T(8,128)(2,1)} %bitcast.40.input_ref.refs_4_, bf16[2048,1664]{1,0:T(8,128)(2,1)} %pad_maximum_fusion.grad_ref.refs_2_, ...), custom_call_target="tpu_custom_call" | custom-call | flops 8053063680 | bytes 14155776 | tf_op jit(solution)/shard_map/experts/pallas_call | solution.py:979
  387.9 15.2 %experts.7 = (bf16[2048,512]{1,0:T(8,128)(2,1)}, bf16[1024,1024]{1,0:T(8,128)(2,1)}, bf16[1024,1664]{1,0:T(8,128)(2,1)}) custom-call(s32[4]{0:T(128)} %iota_add_fusion.1.order_ref, s32[1]{0:T(128)} %bitcast.10.expert_ref, bf16[1024,1536]{1,0:T(8,128)(2,1)} %collective-permute-done.20.input_ref.refs_6_, ...), custom_call_target="tpu_custom_call", output_to_operand_aliasing={{0}: (8, {})} | custom-call | flops 8053063680 | bytes 14155776 | tf_op jit(solution)/shard_map/experts/pallas_call | solution.py:979
  406.8 18.1 %expert_shares.1 = bf16[4096,1536]{1,0:T(8,128)(2,1)} custom-call(s32[16]{0:T(128)} %pad_add_fusion.orders_ref, bf16[2048,512]{1,0:T(8,128)(2,1)} %get-tuple-element.217.refs_0_.refs_1_, bf16[2048,512]{1,0:T(8,128)(2,1)} %get-tuple-element.218.refs_1_.refs_3_, bf16[1536,512]{1,0:T(8,128)(2,1)} %bitcast.30.down_ref.refs_2_), custom_call_target="tpu_custom_call" | custom-call | flops 6442450944 | bytes 18350080 | tf_op jit(solution)/shard_map/expert_shares/pallas_call | solution.py:1024
  430.1 9.4 %collective-permute-done.24 = bf16[128,1664]{1,0:T(8,128)(2,1)S(1)} collective-permute-done((bf16[128,1664]{1,0:T(8,128)(2,1)S(1)}, bf16[128,1664]{1,0:T(8,128)(2,1)S(1)}, u32[]{:S(2)}, u32[]{:S(2)}) %collective-permute-start.24) | collective-permute-done | bytes 426016 | tf_op jit(solution)/shard_map/ppermute | solution.py:45
  443.5 20.8 %up_terms.1 = bf16[1536,1024]{1,0:T(8,128)(2,1)} custom-call(bf16[1024,1536]{1,0:T(8,128)(2,1)} %bitcast.28.input_ref.refs_0_, bf16[1024,1024]{1,0:T(8,128)(2,1)} %get-tuple-element.204.refs_1_, bf16[1024,1536]{1,0:T(8,128)(2,1)} %collective-permute-done.15.input_ref.refs_2_, bf16[1024,1024]{1,0:T(8,128)(2,1)} %get-tuple-element.206.refs_3_, ...), custom_call_target="tpu_custom_call" | custom-call | flops 12884901888 | bytes 24117248 | tf_op jit(solution)/shard_map/up_terms/pallas_call | solution.py:1059
  473.8 11.7 %down_terms.1 = bf16[1536,512]{1,0:T(8,128)(2,1)} custom-call(bf16[2048,1664]{1,0:T(8,128)(2,1)} %all-gather.8.cloned.1.call-done.grad_ref.refs_0_, bf16[2048,512]{1,0:T(8,128)(2,1)} %get-tuple-element.217.refs_0_.refs_1_, bf16[2048,1664]{1,0:T(8,128)(2,1)} %pad_maximum_fusion.grad_ref.refs_2_, bf16[2048,512]{1,0:T(8,128)(2,1)} %get-tuple-element.218.refs_1_.refs_3_), custom_call_target="tpu_custom_call" | custom-call | flops 6442450944 | bytes 18350080 | tf_op jit(solution)/shard_map/down_terms/pallas_call | solution.py:1059
  485.6 7.5 collective-permute-done.29
  497.9 10.5 %collective-permute-done.31.refs_0_ = bf16[256,1664]{1,0:T(8,128)(2,1)S(1)} collective-permute-done((bf16[256,1664]{1,0:T(8,128)(2,1)S(1)}, bf16[256,1664]{1,0:T(8,128)(2,1)S(1)}, u32[]{:S(2)}, u32[]{:S(2)}) %collective-permute-start.31) | collective-permute-done | bytes 852000 | tf_op jit(solution)/shard_map/ppermute | solution.py:84
  515.1 7.8 %return_to_attention.1 = (bf16[256,128]{1,0:T(8,128)(2,1)}, f32[256,1536]{1,0:T(8,128)}, bf16[256,1536]{1,0:T(8,128)(2,1)}, bf16[256,1536]{1,0:T(8,128)(2,1)}, f32[8,1536]{1,0:T(8,128)}) custom-call(f32[256,1664]{1,0:T(8,128)} %pad_maximum_fusion.2.back_ref, bf16[256,128]{1,0:T(8,128)(2,1)} %concatenate.58.code_ref, ...), custom_call_target="tpu_custom_call" | custom-call | flops 1207959552 | bytes 14155776 | tf_op jit(solution)/shard_map/return_to_attention/pallas_call | solution.py:489
  522.9 27.9 %attend_backward.1 = (bf16[256,1536]{1,0:T(8,128)(2,1)}, bf16[2,256,512]{2,1,0:T(8,128)(2,1)}, bf16[2,256,512]{2,1,0:T(8,128)(2,1)}, bf16[2,256,512]{2,1,0:T(8,1...) custom-call(s32[1,256]{1,0:T(1,128)} %bitcast.205, bf16[256,1536]{1,0:T(8,128)(2,1)} %project_queries.1.query_ref, ...), custom_call_target="tpu_custom_call" | custom-call | flops 5033164800 | bytes 8388608 | tf_op jit(solution)/shard_map/attend_backward/pallas_call | solution.py:888
  550.7 9.7 %weight_terms.1 = bf16[1536,3072]{1,0:T(8,128)(2,1)} custom-call(bf16[256,1536]{1,0:T(8,128)(2,1)} %get-tuple-element.134.normed_ref.refs_0_, bf16[256,1536]{1,0:T(8,128)(2,1)} %get-tuple-element.231.refs_1_.refs_0_, bf16[256,1536]{1,0:T(8,128)(2,1)} %get-tuple-element.233.refs_2_, bf16[256,1536]{1,0:T(8,128)(2,1)} %get-tuple-element.146.mixture_ref.refs_3_), custom_call_target="tpu_custom_call" | custom-call | flops 2415919104 | bytes 11010048 | tf_op jit(solution)/shard_map/weight_terms/pallas_call | solution.py:577
  560.5 57.7 %all-to-all-done.2 = bf16[32,48,1536]{2,1,0:T(8,128)(2,1)} async-done(((bf16[32,48,1536]{2,1,0:T(8,128)(2,1)}), bf16[32,48,1536]{2,1,0:T(8,128)(2,1)}, u32[]{:S(2)}, u32[]{:S(2)}) %all-to-all-start.2) | async-done | bytes 4718624 | tf_op jit(solution)/shard_map/all_to_all | solution.py:1114
  628.0 16.6 %collective-permute-done.34.refs_3_ = bf16[2,256,512]{2,1,0:T(8,128)(2,1)S(1)} collective-permute-done((bf16[2,256,512]{2,1,0:T(8,128)(2,1)}, bf16[2,256,512]{2,1,0:T(8,128)(2,1)S(1)}, u32[]{:S(2)}, u32[]{:S(2)}) %collective-permute-start.34) | collective-permute-done | bytes 524320 | tf_op jit(solution)/shard_map/ppermute | solution.py:61
  644.6 41.2 %collective-permute-done.35.refs_4_ = bf16[2,256,512]{2,1,0:T(8,128)(2,1)} collective-permute-done((bf16[2,256,512]{2,1,0:T(8,128)(2,1)}, bf16[2,256,512]{2,1,0:T(8,128)(2,1)}, u32[]{:S(2)}, u32[]{:S(2)}) %collective-permute-start.35) | collective-permute-done | bytes 524320 | tf_op jit(solution)/shard_map/ppermute | solution.py:61
  685.8 13.1 %leave.1 = (f32[256,1536]{1,0:T(8,128)}, bf16[4,4,48,1152]{3,2,1,0:T(8,128)(2,1)}, bf16[4,4,48,1152]{3,2,1,0:T(8,128)(2,1)}) custom-call(s32[2]{0:T(128)} %pad_add_fusion.1.place_ref, f32[256,128]{1,0:T(8,128)} %get-tuple-element.369.cosine_ref, f32[256,128]{1,0:T(8,128)} %get-tuple-element.370.sine_ref, bf16[256,1536]{1,0:T(8,128)(2,1)} %hidden_ref.4, ...), custom_call_target="tpu_custom_call" | custom-call | flops 2818572288 | bytes 18087936 | tf_op jit(solution)/shard_map/leave/pallas_call | solution.py:683
  726.7 8.8 %collective-permute-done.39 = bf16[2,2,48,1152]{3,2,1,0:T(8,128)(2,1)S(1)} collective-permute-done((bf16[2,2,48,1152]{3,2,1,0:T(8,128)(2,1)S(1)}, bf16[2,2,48,1152]{3,2,1,0:T(8,128)(2,1)S(1)}, u32[]{:S(2)}, u32[]{:S(2)}) %collective-permute-start.39) | collective-permute-done | bytes 442400 | tf_op jit(solution)/shard_map/ppermute | solution.py:45
  (243 shorter events, 211.6 us)
Async XLA Ops:
  7.2 93.1 %all-gather.4.cloned.1.call-start = ((), (), s32[]{:S(2)}) async-start(), calls=%async_computation.5 | async-start | bytes 3649536 | tf_op jit(solution)/shard_map/all_gather | solution.py:1128
  11.1 230.7 %all-gather.6.cloned.1.call-start = ((), (), s32[]{:S(2)}) async-start(), calls=%async_computation.6 | async-start | bytes 9732096 | tf_op jit(solution)/shard_map/all_gather | solution.py:1150
  20.0 96.1 %all-to-all-start = ((bf16[32,48,1024]{2,1,0:T(8,128)(2,1)}), bf16[32,48,1024]{2,1,0:T(8,128)(2,1)}, u32[]{:S(2)}, u32[]{:S(2)}) async-start(bf16[32,48,1024]{2,1,0:T(8,128)(2,1)} %bitcast.5), calls=%async_computation | async-start | bytes 6291456 | tf_op jit(solution)/shard_map/all_to_all | solution.py:1114
  27.4 295.1 %all-gather.8.cloned.1.call-start = ((), (), s32[]{:S(2)}) async-start(), calls=%async_computation.7 | async-start | bytes 7667712 | tf_op jit(solution)/shard_map/all_gather | solution.py:1176
  27.5 88.6 %collective-permute-start = (bf16[256,1664]{1,0:T(8,128)(2,1)S(1)}, bf16[256,1664]{1,0:T(8,128)(2,1)S(1)}, u32[]{:S(2)}, u32[]{:S(2)}) collective-permute-start(bf16[256,1664]{1,0:T(8,128)(2,1)S(1)} %concatenate.51), channel_id=1, source_target_pairs={{0,8},{8,0},{16,24},{24,16},{1,9},{9,1},{17,25},{25,17},{2,10},{10... | collective-permute-start | bytes 2555912 | tf_op jit(solution)/shard_map/ppermute | solution.py:84
  120.8 23.1 %collective-permute-start.4 = (bf16[2,256,512]{2,1,0:T(8,128)(2,1)}, bf16[2,256,512]{2,1,0:T(8,128)(2,1)S(1)}, u32[]{:S(2)}, u32[]{:S(2)}) collective-permute-start(bf16[2,256,512]{2,1,0:T(8,128)(2,1)} %get-tuple-element.145.refs_4_), channel_id=1, source_target_pairs={{0,8},{8,16},{16,24},{24,1},{1,9},{9,17},{17,25},{25,2},{2,10},{10... | collective-permute-start | bytes 1572872 | tf_op jit(solution)/shard_map/ppermute | solution.py:61
  143.9 19.5 %collective-permute-start.5 = (bf16[2,256,512]{2,1,0:T(8,128)(2,1)S(1)}, bf16[2,256,512]{2,1,0:T(8,128)(2,1)S(1)}, u32[]{:S(2)}, u32[]{:S(2)}) collective-permute-start(bf16[2,256,512]{2,1,0:T(8,128)(2,1)S(1)} %copy-done.22), channel_id=1, source_target_pairs={{0,24},{8,1},{16,9},{24,17},{1,25},{9,2},{17,10},{25,18},{2,26},{1... | collective-permute-start | bytes 1572872 | tf_op jit(solution)/shard_map/ppermute | solution.py:61
  151.8 22.8 %collective-permute-start.6 = (bf16[2,256,512]{2,1,0:T(8,128)(2,1)S(1)}, bf16[2,256,512]{2,1,0:T(8,128)(2,1)}, u32[]{:S(2)}, u32[]{:S(2)}) collective-permute-start(bf16[2,256,512]{2,1,0:T(8,128)(2,1)S(1)} %copy-done.22), channel_id=1, source_target_pairs={{0,16},{8,24},{16,1},{24,9},{1,17},{9,25},{17,2},{25,10},{2,18},{1... | collective-permute-start | bytes 1572872 | tf_op jit(solution)/shard_map/ppermute | solution.py:61
  174.7 44.8 %collective-permute-start.8 = (bf16[2,128,1664]{2,1,0:T(8,128)(2,1)S(1)}, bf16[2,128,1664]{2,1,0:T(8,128)(2,1)S(1)}, u32[]{:S(2)}, u32[]{:S(2)}) collective-permute-start(bf16[2,128,1664]{2,1,0:T(8,128)(2,1)S(1)} %get-tuple-element.151), channel_id=1, source_target_pairs={{0,2},{1,3},{2,0},{3,1},{4,6},{5,7},{6,4},{7,5},{8,10},{9,11},{10,... | collective-permute-start | bytes 2555912 | tf_op jit(solution)/shard_map/ppermute | solution.py:45
  199.3 22.4 %collective-permute-start.7 = (bf16[2,128,1664]{2,1,0:T(8,128)(2,1)S(1)}, bf16[2,128,1664]{2,1,0:T(8,128)(2,1)}, u32[]{:S(2)}, u32[]{:S(2)}) collective-permute-start(bf16[2,128,1664]{2,1,0:T(8,128)(2,1)S(1)} %get-tuple-element.150), channel_id=1, source_target_pairs={{0,4},{1,5},{2,6},{3,7},{4,0},{5,1},{6,2},{7,3},{8,12},{9,13},{10,... | collective-permute-start | bytes 2555912 | tf_op jit(solution)/shard_map/ppermute | solution.py:45
  225.6 50.9 %all-to-all-start.1 = ((bf16[32,48,512]{2,1,0:T(8,128)(2,1)}), bf16[32,48,512]{2,1,0:T(8,128)(2,1)}, u32[]{:S(2)}, u32[]{:S(2)}) async-start(bf16[32,48,512]{2,1,0:T(8,128)(2,1)} %bitcast.19), calls=%async_computation.1 | async-start | bytes 3145728 | tf_op jit(solution)/shard_map/all_to_all | solution.py:1114
  238.6 379.6 %reduce-scatter.3.cloned.1.call-start = ((), (), s32[]{:S(2)}) async-start(), calls=%async_computation.8 | async-start | bytes 14155776 | tf_op jit(solution)/shard_map/reduce_scatter | solution.py:1258
  276.6 20.9 %collective-permute-start.12 = (bf16[1024,1664]{1,0:T(8,128)(2,1)S(1)}, bf16[1024,1664]{1,0:T(8,128)(2,1)S(1)}, u32[]{:S(2)}, u32[]{:S(2)}) collective-permute-start(bf16[1024,1664]{1,0:T(8,128)(2,1)S(1)} %bitcast.185), channel_id=1, source_target_pairs={{0,1},{1,0},{2,3},{3,2},{4,5},{5,4},{6,7},{7,6},{8,9},{9,8},{10,11... | collective-permute-start | bytes 10223624 | tf_op jit(solution)/shard_map/ppermute | solution.py:45
  277.6 19.9 %collective-permute-start.11 = (bf16[256,1536]{1,0:T(8,128)(2,1)}, bf16[256,1536]{1,0:T(8,128)(2,1)S(1)}, u32[]{:S(2)}, u32[]{:S(2)}) collective-permute-start(bf16[256,1536]{1,0:T(8,128)(2,1)} %get-tuple-element.155.normed_ref.normed_two_ref), channel_id=1, source_target_pairs={{0,8},{8,0},{16,24},{24,16},{1,9},{9,1},{17,25},{25,17},{2,10},{10... | collective-permute-start | bytes 2359304 | tf_op jit(solution)/shard_map/ppermute | solution.py:84
  297.5 18.9 %collective-permute-start.14 = (bf16[2,128,1536]{2,1,0:T(8,128)(2,1)S(1)}, bf16[2,128,1536]{2,1,0:T(8,128)(2,1)S(1)}, u32[]{:S(2)}, u32[]{:S(2)}) collective-permute-start(bf16[2,128,1536]{2,1,0:T(8,128)(2,1)S(1)} %get-tuple-element.158), channel_id=1, source_target_pairs={{0,2},{1,3},{2,0},{3,1},{4,6},{5,7},{6,4},{7,5},{8,10},{9,11},{10,... | collective-permute-start | bytes 2359304 | tf_op jit(solution)/shard_map/ppermute | solution.py:45
  319.2 18.6 %collective-permute-start.15 = (bf16[1024,1536]{1,0:T(8,128)(2,1)}, bf16[1024,1536]{1,0:T(8,128)(2,1)}, u32[]{:S(2)}, u32[]{:S(2)}) collective-permute-start(bf16[1024,1536]{1,0:T(8,128)(2,1)} %bitcast.28.input_ref.refs_0_), channel_id=1, source_target_pairs={{0,1},{1,0},{2,3},{3,2},{4,5},{5,4},{6,7},{7,6},{8,9},{9,8},{10,11... | collective-permute-start | bytes 9437192 | tf_op jit(solution)/shard_map/ppermute | solution.py:45
  340.1 19.5 %collective-permute-start.18 = (bf16[2,128,1536]{2,1,0:T(8,128)(2,1)S(1)}, bf16[2,128,1536]{2,1,0:T(8,128)(2,1)S(1)}, u32[]{:S(2)}, u32[]{:S(2)}) collective-permute-start(bf16[2,128,1536]{2,1,0:T(8,128)(2,1)S(1)} %get-tuple-element.172), channel_id=1, source_target_pairs={{0,4},{1,5},{2,6},{3,7},{4,0},{5,1},{6,2},{7,3},{8,12},{9,13},{10,... | collective-permute-start | bytes 2359304 | tf_op jit(solution)/shard_map/ppermute | solution.py:45
  340.4 19.2 %collective-permute-start.19 = (bf16[2,128,1536]{2,1,0:T(8,128)(2,1)S(1)}, bf16[2,128,1536]{2,1,0:T(8,128)(2,1)S(1)}, u32[]{:S(2)}, u32[]{:S(2)}) collective-permute-start(bf16[2,128,1536]{2,1,0:T(8,128)(2,1)S(1)} %get-tuple-element.173), channel_id=1, source_target_pairs={{0,2},{1,3},{2,0},{3,1},{4,6},{5,7},{6,4},{7,5},{8,10},{9,11},{10,... | collective-permute-start | bytes 2359304 | tf_op jit(solution)/shard_map/ppermute | solution.py:45
  361.8 20.5 %collective-permute-start.21 = (bf16[1024,1664]{1,0:T(8,128)(2,1)}, bf16[1024,1664]{1,0:T(8,128)(2,1)}, u32[]{:S(2)}, u32[]{:S(2)}) collective-permute-start(bf16[1024,1664]{1,0:T(8,128)(2,1)} %get-tuple-element.179), channel_id=1, source_target_pairs={{0,1},{1,0},{2,3},{3,2},{4,5},{5,4},{6,7},{7,6},{8,9},{9,8},{10,11... | collective-permute-start | bytes 10223624 | tf_op jit(solution)/shard_map/ppermute | solution.py:45
  361.8 20.5 %collective-permute-start.20 = (bf16[1024,1536]{1,0:T(8,128)(2,1)}, bf16[1024,1536]{1,0:T(8,128)(2,1)}, u32[]{:S(2)}, u32[]{:S(2)}) collective-permute-start(bf16[1024,1536]{1,0:T(8,128)(2,1)} %bitcast.40.input_ref.refs_4_), channel_id=1, source_target_pairs={{0,1},{1,0},{2,3},{3,2},{4,5},{5,4},{6,7},{7,6},{8,9},{9,8},{10,11... | collective-permute-start | bytes 9437192 | tf_op jit(solution)/shard_map/ppermute | solution.py:45
  385.2 20.9 %collective-permute-start.22 = (bf16[2,128,1664]{2,1,0:T(8,128)(2,1)S(1)}, bf16[2,128,1664]{2,1,0:T(8,128)(2,1)}, u32[]{:S(2)}, u32[]{:S(2)}) collective-permute-start(bf16[2,128,1664]{2,1,0:T(8,128)(2,1)S(1)} %slice_bitcast_fusion.9), channel_id=1, source_target_pairs={{0,2},{1,3},{2,0},{3,1},{4,6},{5,7},{6,4},{7,5},{8,10},{9,11},{10,... | collective-permute-start | bytes 2555912 | tf_op jit(solution)/shard_map/ppermute | solution.py:45
  386.2 20.5 %collective-permute-start.23 = (bf16[2,128,1664]{2,1,0:T(8,128)(2,1)S(1)}, bf16[2,128,1664]{2,1,0:T(8,128)(2,1)}, u32[]{:S(2)}, u32[]{:S(2)}) collective-permute-start(bf16[2,128,1664]{2,1,0:T(8,128)(2,1)S(1)} %slice_bitcast_fusion.8), channel_id=1, source_target_pairs={{0,4},{1,5},{2,6},{3,7},{4,0},{5,1},{6,2},{7,3},{8,12},{9,13},{10,... | collective-permute-start | bytes 2555912 | tf_op jit(solution)/shard_map/ppermute | solution.py:45
  441.4 28.5 %collective-permute-start.27 = (bf16[2,128,1664]{2,1,0:T(8,128)(2,1)S(1)}, bf16[2,128,1664]{2,1,0:T(8,128)(2,1)S(1)}, u32[]{:S(2)}, u32[]{:S(2)}) collective-permute-start(bf16[2,128,1664]{2,1,0:T(8,128)(2,1)S(1)} %slice_bitcast_fusion.4), channel_id=1, source_target_pairs={{0,2},{1,3},{2,0},{3,1},{4,6},{5,7},{6,4},{7,5},{8,10},{9,11},{10,... | collective-permute-start | bytes 2555912 | tf_op jit(solution)/shard_map/ppermute | solution.py:45
  443.2 29.7 %collective-permute-start.28 = (bf16[2,128,1664]{2,1,0:T(8,128)(2,1)S(1)}, bf16[2,128,1664]{2,1,0:T(8,128)(2,1)S(1)}, u32[]{:S(2)}, u32[]{:S(2)}) collective-permute-start(bf16[2,128,1664]{2,1,0:T(8,128)(2,1)S(1)} %slice_bitcast_fusion.3), channel_id=1, source_target_pairs={{0,4},{1,5},{2,6},{3,7},{4,0},{5,1},{6,2},{7,3},{8,12},{9,13},{10,... | collective-permute-start | bytes 2555912 | tf_op jit(solution)/shard_map/ppermute | solution.py:45
  473.4 19.7 %collective-permute-start.29 = (bf16[128,1664]{1,0:T(8,128)(2,1)S(1)}, bf16[128,1664]{1,0:T(8,128)(2,1)S(1)}, u32[]{:S(2)}, u32[]{:S(2)}) collective-permute-start(bf16[128,1664]{1,0:T(8,128)(2,1)S(1)} %slice_bitcast_fusion.16), channel_id=1, source_target_pairs={{0,4},{1,5},{2,6},{3,7},{4,0},{5,1},{6,2},{7,3},{8,12},{9,13},{10,... | collective-permute-start | bytes 1277960 | tf_op jit(solution)/shard_map/ppermute | solution.py:45
  473.8 19.6 %collective-permute-start.30 = (bf16[128,1664]{1,0:T(8,128)(2,1)S(1)}, bf16[128,1664]{1,0:T(8,128)(2,1)S(1)}, u32[]{:S(2)}, u32[]{:S(2)}) collective-permute-start(bf16[128,1664]{1,0:T(8,128)(2,1)S(1)} %slice_bitcast_fusion.15), channel_id=1, source_target_pairs={{0,2},{1,3},{2,0},{3,1},{4,6},{5,7},{6,4},{7,5},{8,10},{9,11},{10,... | collective-permute-start | bytes 1277960 | tf_op jit(solution)/shard_map/ppermute | solution.py:45
  509.2 109.0 %all-to-all-start.2 = ((bf16[32,48,1536]{2,1,0:T(8,128)(2,1)}), bf16[32,48,1536]{2,1,0:T(8,128)(2,1)}, u32[]{:S(2)}, u32[]{:S(2)}) async-start(bf16[32,48,1536]{2,1,0:T(8,128)(2,1)} %bitcast.178), calls=%async_computation.3 | async-start | bytes 9437184 | tf_op jit(solution)/shard_map/all_to_all | solution.py:1114
  512.9 252.8 %reduce-scatter.5.cloned.1.call-start = ((), (), s32[]{:S(2)}) async-start(), calls=%async_computation.9 | async-start | bytes 9732096 | tf_op jit(solution)/shard_map/reduce_scatter | solution.py:1295
  620.8 23.8 %collective-permute-start.34 = (bf16[2,256,512]{2,1,0:T(8,128)(2,1)}, bf16[2,256,512]{2,1,0:T(8,128)(2,1)S(1)}, u32[]{:S(2)}, u32[]{:S(2)}) collective-permute-start(bf16[2,256,512]{2,1,0:T(8,128)(2,1)} %get-tuple-element.242), channel_id=1, source_target_pairs={{24,0},{1,8},{9,16},{17,24},{25,1},{2,9},{10,17},{18,25},{26,2},{3... | collective-permute-start | bytes 1572872 | tf_op jit(solution)/shard_map/ppermute | solution.py:61
  622.1 63.7 %collective-permute-start.35 = (bf16[2,256,512]{2,1,0:T(8,128)(2,1)}, bf16[2,256,512]{2,1,0:T(8,128)(2,1)}, u32[]{:S(2)}, u32[]{:S(2)}) collective-permute-start(bf16[2,256,512]{2,1,0:T(8,128)(2,1)} %get-tuple-element.243), channel_id=1, source_target_pairs={{16,0},{24,8},{1,16},{9,24},{17,1},{25,9},{2,17},{10,25},{18,2},{2... | collective-permute-start | bytes 1572872 | tf_op jit(solution)/shard_map/ppermute | solution.py:61
  623.4 62.4 %collective-permute-start.36 = (bf16[2,256,512]{2,1,0:T(8,128)(2,1)}, bf16[2,256,512]{2,1,0:T(8,128)(2,1)}, u32[]{:S(2)}, u32[]{:S(2)}) collective-permute-start(bf16[2,256,512]{2,1,0:T(8,128)(2,1)} %get-tuple-element.244), channel_id=1, source_target_pairs={{8,0},{16,8},{24,16},{1,24},{9,1},{17,9},{25,17},{2,25},{10,2},{18... | collective-permute-start | bytes 1572872 | tf_op jit(solution)/shard_map/ppermute | solution.py:61
  624.7 79.3 %collective-permute-start.32 = (bf16[256,1536]{1,0:T(8,128)(2,1)S(1)}, bf16[256,1536]{1,0:T(8,128)(2,1)S(1)}, u32[]{:S(2)}, u32[]{:S(2)}) collective-permute-start(bf16[256,1536]{1,0:T(8,128)(2,1)S(1)} %slice.225), channel_id=1, source_target_pairs={{0,8},{8,0},{16,24},{24,16},{1,9},{9,1},{17,25},{25,17},{2,10},{10... | collective-permute-start | bytes 2359304 | tf_op jit(solution)/shard_map/ppermute | solution.py:84
  (47 other events, 655.4 us)
Sparse Core Ops, SparseCore 0:
  11.5 88.7 all-gather.3
  103.8 109.4 all-gather.5
  215.8 66.2 all-gather.7
  425.0 147.8 reduce-scatter.2
  578.6 183.6 reduce-scatter.4
